TPU v7x, 32 devices: a whole 2x2x4 slice. The times are simulated.
32 devices in a mesh: row: 4 (over y, core), col: 4 (over z), dp: 2 (over x).
Axes of the slice: x: 2, y: 2, z: 4, core: 2. Of those that a mesh axis runs over, the one named last changes fastest.
Arguments:
- features: bfloat16 [1024, 512, 128], P(('dp', 'row'), 'col'), parts along dimension 0, may hold values from -6 to 6
- labels: int32 [1024, 512], P(('dp', 'row', 'col')), parts along dimension 0, may hold values from 0 to 63
- norm_gain: float32 [3, 128], replicated, may hold values from 0.5 to 1.5
- w_down: bfloat16 [2, 128, 64], replicated, may hold values from -0.5 to 0.5
- w_conv: bfloat16 [2, 3, 3, 64, 64], replicated, may hold values from -0.25 to 0.25
- w_up: bfloat16 [2, 64, 128], replicated, may hold values from -0.75 to 0.75
- w_head: bfloat16 [128, 64], replicated, may hold values from -0.5 to 0.5
- head_bias: float32 [64], replicated, may hold values from -4 to 4
Outputs:
- grad_input: float32 [1024, 512, 128], P(('dp', 'row'), 'col'), parts along dimension 0
There are 2 independent parts, one for each index of `dp`. A program takes and returns all parts, laid end to end along the dimension named above; an argument that names none is the same for every part. Nothing has to cross between parts.
All inputs are finite; a program needn't handle non-finite values.
Results may differ from a plain program's by a relative error of at most 0.0095.
Values may be sent and summed in bfloat16 or wider, within the bound.
No kernel may reach another device: no remote copies, remote signals or barrier semaphores. Data moves between devices by JAX's collectives and lax.ppermute only.
A program may use at most 192 MiB of HBM per device.

v0:
```python
import jax
import jax.numpy as jnp
from jax import lax
from jax.sharding import PartitionSpec as P

epsilon = 1e-05


def padded_2(cells, sides, width):
    for axis, dim in sides:
        count = lax.axis_size(axis)
        ends = count - 1
        head = lax.slice_in_dim(cells, 0, width, axis=dim)
        tail = lax.slice_in_dim(cells, cells.shape[dim] - width, cells.shape[dim], axis=dim)
        cells = jnp.concatenate(
            [
                lax.ppermute(tail, axis, [(i, (i + 1) % count) for i in range(ends)]),
                cells,
                lax.ppermute(head, axis, [((i + 1) % count, i) for i in range(ends)]),
            ],
            axis=dim,
        )
    return cells


def normalize(values, scales):
    average = jnp.mean(values, -1, keepdims=True)
    centred = values - average
    variance = jnp.mean(centred * centred, -1, keepdims=True)
    return centred * lax.rsqrt(variance + epsilon) * scales


def normalize_back(values, scales, upstream):
    unused, pullback = jax.vjp(lambda argument: normalize(argument, scales), values)
    return pullback(upstream)[0]


def elu_forward(values):
    return jnp.where(values > 0, values, jnp.expm1(jnp.minimum(values, 0.0)))


def elu_slope(values):
    return jnp.where(values > 0, 1.0, jnp.exp(jnp.minimum(values, 0.0)))


def bottleneck_in(stream, scales, down_weight):
    normed = normalize(stream, scales)
    lowered = jnp.dot(
        elu_forward(normed).astype(jnp.bfloat16), down_weight, preferred_element_type=jnp.float32
    )
    return (elu_forward(lowered).astype(jnp.bfloat16), normed, lowered)


def dilated(padded, kernel, spacing, row_count, col_count, mirrored):
    summed = jnp.zeros((row_count, col_count, kernel.shape[-1]), jnp.float32)
    for row_tap in range(3):
        for col_tap in range(3):
            if mirrored:
                start_row = (2 - row_tap) * spacing
                start_col = (2 - col_tap) * spacing
                weight = kernel[row_tap, col_tap].T
            else:
                start_row = row_tap * spacing
                start_col = col_tap * spacing
                weight = kernel[row_tap, col_tap]
            window = padded[start_row : start_row + row_count, start_col : start_col + col_count]
            summed = summed + jnp.dot(window, weight, preferred_element_type=jnp.float32)
    return summed


def bottleneck_out(convolved, up_weight):
    return jnp.dot(
        elu_forward(convolved).astype(jnp.bfloat16), up_weight, preferred_element_type=jnp.float32
    )


def block_back(upstream, saved_state, scales, down_weight, kernel, up_weight, spacing, widen):
    stream, normed, lowered, convolved = saved_state
    activated = jnp.dot(
        upstream.astype(jnp.bfloat16), up_weight.T, preferred_element_type=jnp.float32
    )
    conv_grad = (activated * elu_slope(convolved)).astype(jnp.bfloat16)
    padded = widen(conv_grad, spacing)
    lowered_grad = dilated(
        padded, kernel, spacing, conv_grad.shape[0], conv_grad.shape[1], True
    ) * elu_slope(lowered)
    normed_grad = jnp.dot(
        lowered_grad.astype(jnp.bfloat16), down_weight.T, preferred_element_type=jnp.float32
    ) * elu_slope(normed)
    return upstream + normalize_back(stream, scales, normed_grad)


def margins(values, spacing):
    return padded_2(values, (("row", 0), ("col", 1)), spacing)


def shards(features, labels, norm_gain, w_down, w_conv, w_up, w_head, head_bias):
    row_count = features.shape[0]
    col_count = features.shape[1]
    bin_count = w_head.shape[1]
    stream = features.astype(jnp.float32)
    stored = []
    for section_index, spacing in ((0, 4), (1, 8)):
        squeezed, normed, lowered = bottleneck_in(
            stream, norm_gain[section_index], w_down[section_index]
        )
        convolved = dilated(
            margins(squeezed, spacing), w_conv[section_index], spacing, row_count, col_count, False
        )
        stored.append((stream, normed, lowered, convolved))
        stream = stream + bottleneck_out(convolved, w_up[section_index])
    head_in = normalize(stream, norm_gain[2]).astype(jnp.bfloat16)
    logits = (jnp.dot(head_in, w_head, preferred_element_type=jnp.float32) + head_bias).astype(
        jnp.bfloat16
    )
    flat_logits = logits.reshape(row_count, col_count * bin_count)
    row_block = lax.all_to_all(flat_logits, "col", split_axis=0, concat_axis=1, tiled=True)
    block_rows = row_block.shape[0]
    map_size = row_block.shape[1] // bin_count
    facing = lax.all_to_all(row_block, ("row", "col"), split_axis=1, concat_axis=0, tiled=True)
    facing = jnp.swapaxes(facing.reshape(map_size, block_rows, bin_count), 0, 1)
    forward_logits = row_block.reshape(block_rows, map_size, bin_count)
    symmetric = 0.5 * (forward_logits.astype(jnp.float32) + facing.astype(jnp.float32))
    exponent = jnp.exp(symmetric)
    probability = exponent / jnp.sum(exponent, -1, keepdims=True)
    bin_numbers = jnp.arange(bin_count, dtype=jnp.int32)
    onehot = (labels[:, :, None] == bin_numbers).astype(jnp.float32)
    labels_facing = lax.all_to_all(
        labels, ("row", "col"), split_axis=1, concat_axis=0, tiled=True
    ).T
    onehot_facing = (labels_facing[:, :, None] == bin_numbers).astype(jnp.float32)
    logit_grad = (probability - 0.5 * (onehot + onehot_facing)).astype(jnp.bfloat16)
    tile_grad = lax.all_to_all(
        logit_grad.reshape(block_rows, map_size * bin_count),
        "col",
        split_axis=1,
        concat_axis=0,
        tiled=True,
    )
    tile_grad = tile_grad.reshape(row_count, col_count, bin_count)
    head_grad = jnp.dot(tile_grad, w_head.T, preferred_element_type=jnp.float32)
    stream_grad = normalize_back(stream, norm_gain[2], head_grad)
    for section_index, spacing in ((1, 8), (0, 4)):
        stream_grad = block_back(
            stream_grad,
            stored[section_index],
            norm_gain[section_index],
            w_down[section_index],
            w_conv[section_index],
            w_up[section_index],
            spacing,
            margins,
        )
    return stream_grad


def solution(mesh):
    return jax.shard_map(
        shards,
        mesh=mesh,
        in_specs=(
            P(("dp", "row"), "col", None),
            P(("dp", "row", "col"), None),
            P(),
            P(),
            P(),
            P(),
            P(),
            P(),
        ),
        out_specs=P(("dp", "row"), "col", None),
        check_vma=False,
    )
```

profile of v0, /device:TPU:1, one launch (start us, length us, event | category | flops | bytes accessed | tf_op | source)
XLA Modules:
  0.0 672.3 jit_solution(3244815515851694273)
XLA Ops:
  0.8 6.4 copy.35
  12.6 7.7 %fusion.19 = (bf16[128,128,64]{1,2,0:T(8,128)(2,1)S(1)}, f32[128,128,64]{1,2,0:T(8,128)}) fusion(bf16[128,128,128]{1,2,0:T(8,128)(2,1)S(1)} %copy-done.4, f32[128]{0:T(128)S(1)} %get-tuple-element.38, f32[128,128]{1,0:T(8,128)S(1)} %fusion.139, f32[128,128]{1,0:T(8,128)S(1)} %broadcast_multiply_fusion.2, bf16[2,128,64]{1,2,0:T(8,128)(2,1)S(1)} %copy-done.29), kind=kOutput, calls=%fused_computation.58 | convolution fusion | flops 289406976 | bytes 10633728 | tf_op jit(solution)/shard_map/dot_general | solution.py:48
  20.3 4.5 collective-permute-start
  33.9 5.2 copy.40
  39.1 5.2 copy.37
  58.4 4.4 copy.38
  62.8 6.5 pad_maximum_fusion.2
  84.5 13.3 %add_add_fusion.6 = f32[128,128,64]{1,2,0:T(8,128)S(1)} fusion(f32[128,128,64]{1,2,0:T(8,128)} %fusion.117, f32[128,128,64]{1,2,0:T(8,128)} %fusion.119, f32[128,128,64]{1,2,0:T(8,128)} %fusion.121, f32[128,128,64]{1,2,0:T(8,128)S(1)} %copy-done.15, f32[128,128,64]{1,2,0:T(8,128)} %fusion.123, f32[128,128,64]{1,2,0:T(8,128)} %fusion.125, ...), kind=kOutput, calls=%fused_computation.81 | convolution fusion | flops 142606336 | bytes 39862272 | tf_op jit(solution)/shard_map/dot_general | solution.py:67
  104.3 7.5 %fusion.25 = (bf16[128,128,64]{1,2,0:T(8,128)(2,1)S(1)}, f32[128,128,64]{1,2,0:T(8,128)}) fusion(f32[128,128,128]{1,2,0:T(8,128)S(1)} %get-tuple-element.43, f32[128]{0:T(128)S(1)} %get-tuple-element.39, f32[128,128]{1,0:T(8,128)S(1)} %fusion.140, f32[128,128]{1,0:T(8,128)S(1)} %broadcast_multiply_fusion.1, bf16[2,128,64]{1,2,0:T(8,128)(2,1)S(1)} %copy-done.29), kind=kOutput, calls=%fused_computation.64 | convolution fusion | flops 287309824 | bytes 14828032 | tf_op jit(solution)/shard_map/dot_general | solution.py:48
  125.7 6.1 copy.46
  131.7 5.4 copy.43
  149.1 5.8 copy.47
  154.9 4.6 copy.44
  159.5 6.5 pad_maximum_fusion
  180.3 14.5 %add_add_fusion.5 = f32[128,128,64]{1,2,0:T(8,128)S(1)} fusion(f32[128,128,64]{1,2,0:T(8,128)} %fusion.99, f32[128,128,64]{1,2,0:T(8,128)} %fusion.101, f32[128,128,64]{1,2,0:T(8,128)} %fusion.103, f32[128,128,64]{1,2,0:T(8,128)} %fusion.156, f32[128,128,64]{1,2,0:T(8,128)} %fusion.105, f32[128,128,64]{1,2,0:T(8,128)} %fusion.107, ...), kind=kOutput, calls=%fused_computation.80 | convolution fusion | flops 142606336 | bytes 39862272 | tf_op jit(solution)/shard_map/dot_general | solution.py:67
  206.1 6.6 all_to_all.48
  212.7 4.9 all-to-all-start
  218.6 45.8 %all-to-all-done = bf16[4,32,8192]{2,1,0:T(8,128)(2,1)S(1)} async-done(((bf16[4,32,8192]{2,1,0:T(8,128)(2,1)}), bf16[4,32,8192]{2,1,0:T(8,128)(2,1)S(1)}, u32[]{:S(2)}, u32[]{:S(2)}) %all-to-all-start) | async-done | bytes 2097184 | tf_op jit(solution)/shard_map/all_to_all | solution.py:117
  270.7 4.4 all_to_all.51
  279.2 5.9 all-to-all-start.1
  287.1 4.8 copy.50
  291.9 8.3 %reshape.109 = f32[32,512,64]{2,1,0:T(8,128)} reshape(f32[32,4,8192]{2,1,0:T(4,128)} %copy.50) | data formatting | bytes 8388608 | tf_op jit(solution)/shard_map/convert_element_type | solution.py:123
  300.2 33.6 %all-to-all-done.1 = bf16[32,16,2048]{2,0,1:T(8,128)(2,1)} async-done(((bf16[32,16,2048]{2,0,1:T(8,128)(2,1)}), bf16[32,16,2048]{2,0,1:T(8,128)(2,1)}, u32[]{:S(2)}, u32[]{:S(2)}) %all-to-all-start.1) | async-done | bytes 2097184 | tf_op jit(solution)/shard_map/all_to_all | solution.py:120
  337.9 7.8 %reshape.110 = f32[512,32,64]{2,1,0:T(8,128)} reshape(f32[16,32,2048]{2,1,0:T(8,128)} %convert_bitcast_fusion) | data formatting | bytes 8388608 | tf_op jit(solution)/shard_map/convert_element_type | solution.py:123
  345.8 33.8 %subtract_convert_fusion = bf16[32,512,64]{2,1,0:T(8,128)(2,1)} fusion(s32[32,512]{1,0:T(8,128)S(1)} %bitcast.256, s32[32,512]{1,0:T(8,128)S(1)} %copy-done.28, f32[32,512,64]{2,1,0:T(8,128)} %reshape.109, f32[512,32,64]{2,1,0:T(8,128)} %reshape.110), kind=kOutput, calls=%fused_computation.34 | output fusion | flops 11550783 | bytes 10616832 | tf_op jit(solution)/shard_map/div | solution.py:125
  379.6 6.5 all_to_all.57
  387.2 50.6 %all_to_all.64 = bf16[32,4,8192]{2,0,1:T(8,128)(2,1)S(1)} all-to-all(bf16[32,4,8192]{2,0,1:T(8,128)(2,1)S(1)} %copy.56), channel_id=1, replica_groups=mesh['row'=4,'col'=4,'dp'=2] {'col'}, dimensions={1} | all-to-all | bytes 4194304 | tf_op jit(solution)/shard_map/all_to_all | solution.py:133
  437.8 5.5 reshape.108
  443.4 6.3 multiply_reduce_fusion.1
  449.7 6.1 fusion.184
  471.6 6.0 copy.63
  477.6 5.4 copy.59
  484.3 4.7 collective-permute-start.11
  494.6 6.0 copy.64
  500.6 4.6 copy.60
  505.2 6.1 maximum_maximum_fusion.1
  525.8 21.7 %multiply_reduce_fusion = (f32[128,128]{1,0:T(8,128)S(1)}, f32[128,128,128]{1,2,0:T(8,128)}) fusion(f32[128,128,128]{1,2,0:T(8,128)} %copy-done.2, f32[128]{0:T(128)S(1)} %get-tuple-element.39, f32[128,128]{1,0:T(8,128)S(1)} %fusion.140, f32[128,128]{1,0:T(8,128)S(1)} %broadcast_multiply_fusion.1, bf16[2,128,64]{1,2,0:T(8,128)(2,1)S(1)} %copy-done.29, ...), kind=kOutput, calls=%fused_computation.32 | convolution fusion | flops 437239808 | bytes 56852992 | tf_op jit(solution)/shard_map/dot_general | solution.py:87
  547.5 8.8 %fusion.183 = (f32[128,128]{1,0:T(8,128)S(1)}, f32[128,128,128]{1,2,0:T(8,128)S(1)}) fusion(f32[128,128]{1,0:T(8,128)S(1)} %multiply_multiply_fusion.2, f32[128,128,128]{1,2,0:T(8,128)} %get-tuple-element.51, f32[128]{0:T(128)S(1)} %get-tuple-element.39, f32[128,128]{1,0:T(8,128)S(1)} %fusion.140, f32[128,128,128]{1,2,0:T(8,128)} %copy-done.2, ...), kind=kLoop, calls=%fused_computation.252 | loop fusion | flops 27246592 | bytes 25428480 | tf_op jit(solution)/shard_map/transpose(jvp())/reduce_sum | solution.py:28
  556.4 6.5 fusion.24
  575.1 5.2 copy.77
  580.3 5.2 copy.73
  596.5 4.7 copy.78
  601.2 4.4 copy.74
  605.6 5.9 maximum_maximum_fusion.3
  626.1 20.5 %fusion.16 = (f32[128,128]{1,0:T(8,128)S(1)}, f32[128,128,128]{1,2,0:T(8,128)}) fusion(bf16[128,128,128]{1,2,0:T(8,128)(2,1)} %copy.35, f32[128]{0:T(128)S(1)} %copy-done.31, f32[128,128]{1,0:T(8,128)S(1)} %copy-done.21, f32[128,128]{1,0:T(8,128)S(1)} %copy-done.19, bf16[2,128,64]{1,2,0:T(8,128)(2,1)S(1)} %copy-done.29, ...), kind=kOutput, calls=%fused_computation.26 | convolution fusion | flops 439336960 | bytes 52658688 | tf_op jit(solution)/shard_map/dot_general | solution.py:87
  646.7 8.2 %fusion.182 = (f32[128,128]{1,0:T(8,128)S(1)}, f32[128,128,128]{1,2,0:T(8,128)S(1)}) fusion(f32[128,128]{1,0:T(8,128)S(1)} %multiply_multiply_fusion.1, f32[128,128,128]{1,2,0:T(8,128)} %get-tuple-element.53, f32[128]{0:T(128)S(1)} %copy-done.31, f32[128,128]{1,0:T(8,128)S(1)} %copy-done.21, f32[128,128]{1,0:T(8,128)S(1)} %copy-done.19, ...), kind=kLoop, calls=%fused_computation.251 | loop fusion | flops 29343744 | bytes 21234176 | tf_op jit(solution)/shard_map/transpose(jvp())/reduce_sum | solution.py:28
  655.0 8.0 %add_add_fusion.3 = f32[128,128,128]{1,2,0:T(8,128)} fusion(f32[128,128,128]{1,2,0:T(8,128)S(1)} %get-tuple-element.6, f32[128,128]{1,0:T(8,128)S(1)} %negate_multiply_fusion, f32[128,128,128]{1,2,0:T(8,128)} %copy-done.7, f32[128,128]{1,0:T(8,128)S(1)} %negate_multiply_fusion.1, f32[128,128,128]{1,2,0:T(8,128)S(1)} %bitcast.216, ...), kind=kLoop, calls=%fused_computation.30 | loop fusion | flops 10485760 | bytes 33751040 | tf_op jit(solution)/shard_map/add | solution.py:90
  663.1 9.0 %copy.86 = f32[128,128,128]{2,1,0:T(8,128)} copy(f32[128,128,128]{1,2,0:T(8,128)} %add_add_fusion.3) | data formatting | bytes 16777216 | tf_op jit(solution)/shard_map/add | solution.py:90
  (196 shorter events, 195.8 us)
Async XLA Ops:
  0.0 201.0 %copy-start = (bf16[128,64]{0,1:T(8,128)(2,1)S(1)}, bf16[128,64]{0,1:T(8,128)(2,1)}, u32[]{:S(2)}) copy-start(bf16[128,64]{0,1:T(8,128)(2,1)} %param.14) | copy-start | bytes 49156
  0.8 11.8 %copy-start.30 = (f32[128]{0:T(128)}, f32[128]{0:T(128)S(1)}, u32[]{:S(2)}) copy-start(f32[128]{0:T(128)S(1)} %get-tuple-element.38) | copy-start | bytes 1540
  7.2 3.6 copy-start.4
  7.2 5.4 copy-start.29
  10.8 9.5 %copy-start.18 = (f32[128,128]{1,0:T(8,128)}, f32[128,128]{1,0:T(8,128)S(1)}, u32[]{:S(2)}) copy-start(f32[128,128]{1,0:T(8,128)S(1)} %broadcast_multiply_fusion.2) | copy-start | bytes 196612
  12.5 7.7 %copy-start.22 = (f32[128,128]{1,0:T(8,128)}, f32[128,128]{1,0:T(8,128)S(1)}, u32[]{:S(2)}) copy-start(f32[128,128]{1,0:T(8,128)S(1)} %fusion.11) | copy-start | bytes 196612
  12.6 7.7 %copy-start.20 = (f32[128,128]{1,0:T(8,128)}, f32[128,128]{1,0:T(8,128)S(1)}, u32[]{:S(2)}) copy-start(f32[128,128]{1,0:T(8,128)S(1)} %fusion.139) | copy-start | bytes 196612
  12.6 14.5 %copy-start.26 = (bf16[2,3,3,64,64]{4,3,2,1,0:T(8,128)(2,1)S(1)}, bf16[2,3,3,64,64]{4,3,2,1,0:T(8,128)(2,1)}, u32[]{:S(2)}) copy-start(bf16[2,3,3,64,64]{4,3,2,1,0:T(8,128)(2,1)} %param.12) | copy-start | bytes 442372
  20.3 9.9 %collective-permute-start = (bf16[4,128,64]{1,2,0:T(8,128)(2,1)S(1)}, bf16[4,128,64]{1,2,0:T(8,128)(2,1)S(1)}, u32[]{:S(2)}, u32[]{:S(2)}) collective-permute-start(bf16[4,128,64]{1,2,0:T(8,128)(2,1)S(1)} %get-tuple-element.33), channel_id=1, source_target_pairs={{0,8},{8,16},{16,24},{1,9},{9,17},{17,25},{2,10},{10,18},{18,26},{... | collective-permute-start | bytes 196616 | tf_op jit(solution)/shard_map/ppermute | solution.py:17
  24.8 5.6 collective-permute-start.1
  27.2 56.4 %copy-start.16 = (bf16[1,3,3,64,64]{3,4,2,1,0:T(8,128)(2,1)}, bf16[1,3,3,64,64]{3,4,2,1,0:T(8,128)(2,1)S(1)}, u32[]{:S(2)}) copy-start(bf16[1,3,3,64,64]{3,4,2,1,0:T(8,128)(2,1)S(1)} %copy.129) | copy-start | bytes 221188
  44.3 14.1 %collective-permute-start.2 = (bf16[136,4,64]{0,2,1:T(8,128)(2,1)S(1)}, bf16[136,4,64]{0,2,1:T(8,128)(2,1)S(1)}, u32[]{:S(2)}, u32[]{:S(2)}) collective-permute-start(bf16[136,4,64]{0,2,1:T(8,128)(2,1)S(1)} %copy.37), channel_id=1, source_target_pairs={{0,2},{2,4},{4,6},{1,3},{3,5},{5,7},{8,10},{10,12},{12,14},{9,11},... | collective-permute-start | bytes 208904 | tf_op jit(solution)/shard_map/ppermute | solution.py:17
  47.5 6.6 collective-permute-start.3
  69.3 6.3 copy-start.12
  84.5 13.3 %copy-start.5 = (bf16[128,128,128]{1,2,0:T(8,128)(2,1)S(1)}, bf16[128,128,128]{1,2,0:T(8,128)(2,1)}, u32[]{:S(2)}) copy-start(bf16[128,128,128]{1,2,0:T(8,128)(2,1)} %copy.35) | copy-start | bytes 12582916
  84.5 13.3 %copy-start.27 = (bf16[2,64,128]{2,1,0:T(8,128)(2,1)S(1)}, bf16[2,64,128]{2,1,0:T(8,128)(2,1)}, u32[]{:S(2)}) copy-start(bf16[2,64,128]{2,1,0:T(8,128)(2,1)} %param.13) | copy-start | bytes 98308
  103.1 8.7 %copy-start.24 = (f32[128,128]{1,0:T(8,128)}, f32[128,128]{1,0:T(8,128)S(1)}, u32[]{:S(2)}) copy-start(f32[128,128]{1,0:T(8,128)S(1)} %multiply_reduce_fusion.3) | copy-start | bytes 196612
  111.8 8.6 %collective-permute-start.4 = (bf16[8,128,64]{1,2,0:T(8,128)(2,1)S(1)}, bf16[8,128,64]{1,2,0:T(8,128)(2,1)S(1)}, u32[]{:S(2)}, u32[]{:S(2)}) collective-permute-start(bf16[8,128,64]{1,2,0:T(8,128)(2,1)S(1)} %get-tuple-element.31), channel_id=1, source_target_pairs={{0,8},{8,16},{16,24},{1,9},{9,17},{17,25},{2,10},{10,18},{18,26},{... | collective-permute-start | bytes 393224 | tf_op jit(solution)/shard_map/ppermute | solution.py:17
  115.8 6.3 collective-permute-start.5
  137.1 17.8 %collective-permute-start.6 = (bf16[144,8,64]{0,2,1:T(8,128)(2,1)S(1)}, bf16[144,8,64]{0,2,1:T(8,128)(2,1)S(1)}, u32[]{:S(2)}, u32[]{:S(2)}) collective-permute-start(bf16[144,8,64]{0,2,1:T(8,128)(2,1)S(1)} %copy.43), channel_id=1, source_target_pairs={{0,2},{2,4},{4,6},{1,3},{3,5},{5,7},{8,10},{10,12},{12,14},{9,11},... | collective-permute-start | bytes 442376 | tf_op jit(solution)/shard_map/ppermute | solution.py:17
  141.2 7.9 %collective-permute-start.7 = (bf16[144,8,64]{0,2,1:T(8,128)(2,1)}, bf16[144,8,64]{0,2,1:T(8,128)(2,1)}, u32[]{:S(2)}, u32[]{:S(2)}) collective-permute-start(bf16[144,8,64]{0,2,1:T(8,128)(2,1)} %copy.46), channel_id=1, source_target_pairs={{2,0},{4,2},{6,4},{3,1},{5,3},{7,5},{10,8},{12,10},{14,12},{11,9},... | collective-permute-start | bytes 442376 | tf_op jit(solution)/shard_map/ppermute | solution.py:19
  166.0 6.1 copy-start.14
  177.5 17.3 %slice-start = ((s8[8388608]{0:T(1024)(128)(4,1)}), s8[4194304]{0:T(1024)(128)(4,1)S(1)}, s32[]{:S(2)}) async-start(s8[8388608]{0:T(1024)(128)(4,1)} %bitcast.211), calls=%async_computation.4 | async-start | bytes 8388608
  180.3 14.5 %slice-start.1 = ((s8[8388608]{0:T(1024)(128)(4,1)}), s8[4194304]{0:T(1024)(128)(4,1)S(1)}, s32[]{:S(2)}) async-start(s8[8388608]{0:T(1024)(128)(4,1)} %bitcast.211), calls=%async_computation.5 | async-start | bytes 8388608
  206.1 11.5 %copy-start.28 = (s32[32,512]{1,0:T(8,128)S(1)}, s32[32,512]{1,0:T(8,128)}, u32[]{:S(2)}) copy-start(s32[32,512]{1,0:T(8,128)} %param.9) | copy-start | bytes 196612
  212.7 51.6 %all-to-all-start = ((bf16[4,32,8192]{2,1,0:T(8,128)(2,1)}), bf16[4,32,8192]{2,1,0:T(8,128)(2,1)S(1)}, u32[]{:S(2)}, u32[]{:S(2)}) async-start(bf16[4,32,8192]{2,1,0:T(8,128)(2,1)} %all_to_all.48), calls=%async_computation | async-start | bytes 4194304 | tf_op jit(solution)/shard_map/all_to_all | solution.py:117
  264.4 14.8 %all-to-all-start.2 = ((s32[16,1,1024]{2,1,0:T(1,128)}), s32[16,1,1024]{2,1,0:T(1,128)S(1)}, u32[]{:S(2)}, u32[]{:S(2)}) async-start(s32[16,1,1024]{2,1,0:T(1,128)} %reshape.152), calls=%async_computation.2 | async-start | bytes 131072 | tf_op jit(solution)/shard_map/all_to_all | solution.py:128
  279.2 54.7 %all-to-all-start.1 = ((bf16[32,16,2048]{2,0,1:T(8,128)(2,1)}), bf16[32,16,2048]{2,0,1:T(8,128)(2,1)}, u32[]{:S(2)}, u32[]{:S(2)}) async-start(bf16[32,16,2048]{2,0,1:T(8,128)(2,1)} %copy.52), calls=%async_computation.1 | async-start | bytes 4194304 | tf_op jit(solution)/shard_map/all_to_all | solution.py:120
  449.7 6.1 copy-start.10
  459.1 8.9 %collective-permute-start.9 = (bf16[8,128,64]{1,2,0:T(8,128)(2,1)S(1)}, bf16[8,128,64]{1,2,0:T(8,128)(2,1)S(1)}, u32[]{:S(2)}, u32[]{:S(2)}) collective-permute-start(bf16[8,128,64]{1,2,0:T(8,128)(2,1)S(1)} %get-tuple-element.29), channel_id=1, source_target_pairs={{8,0},{16,8},{24,16},{9,1},{17,9},{25,17},{10,2},{18,10},{26,18},{... | collective-permute-start | bytes 393224 | tf_op jit(solution)/shard_map/ppermute | solution.py:19
  462.4 5.6 collective-permute-start.8
  483.0 17.5 %collective-permute-start.10 = (bf16[144,8,64]{0,2,1:T(8,128)(2,1)S(1)}, bf16[144,8,64]{0,2,1:T(8,128)(2,1)S(1)}, u32[]{:S(2)}, u32[]{:S(2)}) collective-permute-start(bf16[144,8,64]{0,2,1:T(8,128)(2,1)S(1)} %copy.59), channel_id=1, source_target_pairs={{2,0},{4,2},{6,4},{3,1},{5,3},{7,5},{10,8},{12,10},{14,12},{11,9},... | collective-permute-start | bytes 442376 | tf_op jit(solution)/shard_map/ppermute | solution.py:19
  484.3 10.2 %collective-permute-start.11 = (bf16[144,8,64]{0,2,1:T(8,128)(2,1)}, bf16[144,8,64]{0,2,1:T(8,128)(2,1)}, u32[]{:S(2)}, u32[]{:S(2)}) collective-permute-start(bf16[144,8,64]{0,2,1:T(8,128)(2,1)} %copy.63), channel_id=1, source_target_pairs={{0,2},{2,4},{4,6},{1,3},{3,5},{5,7},{8,10},{10,12},{12,14},{9,11},... | collective-permute-start | bytes 442376 | tf_op jit(solution)/shard_map/ppermute | solution.py:17
  511.3 5.9 copy-start.13
  525.8 21.7 %copy-start.25 = (f32[128,128]{1,0:T(8,128)S(1)}, f32[128,128]{1,0:T(8,128)}, u32[]{:S(2)}) copy-start(f32[128,128]{1,0:T(8,128)} %copy-done.24) | copy-start | bytes 196612
  547.5 8.8 %slice-start.2 = ((s8[8388608]{0:T(1024)(128)(4,1)}), s8[4194304]{0:T(1024)(128)(4,1)S(1)}, s32[]{:S(2)}) async-start(s8[8388608]{0:T(1024)(128)(4,1)} %bitcast.213), calls=%async_computation.6 | async-start | bytes 8388608
  547.5 8.8 %slice-start.3 = ((s8[8388608]{0:T(1024)(128)(4,1)}), s8[4194304]{0:T(1024)(128)(4,1)S(1)}, s32[]{:S(2)}) async-start(s8[8388608]{0:T(1024)(128)(4,1)} %bitcast.213), calls=%async_computation.7 | async-start | bytes 8388608
  556.3 6.6 copy-start.7
  556.4 12.5 %copy-start.17 = (bf16[1,3,3,64,64]{3,4,2,1,0:T(8,128)(2,1)S(1)}, bf16[1,3,3,64,64]{3,4,2,1,0:T(8,128)(2,1)}, u32[]{:S(2)}) copy-start(bf16[1,3,3,64,64]{3,4,2,1,0:T(8,128)(2,1)} %copy-done.16) | copy-start | bytes 221188
  562.9 8.7 %collective-permute-start.13 = (bf16[4,128,64]{1,2,0:T(8,128)(2,1)S(1)}, bf16[4,128,64]{1,2,0:T(8,128)(2,1)S(1)}, u32[]{:S(2)}, u32[]{:S(2)}) collective-permute-start(bf16[4,128,64]{1,2,0:T(8,128)(2,1)S(1)} %get-tuple-element.27), channel_id=1, source_target_pairs={{8,0},{16,8},{24,16},{9,1},{17,9},{25,17},{10,2},{18,10},{26,18},{... | collective-permute-start | bytes 196616 | tf_op jit(solution)/shard_map/ppermute | solution.py:19
  565.4 6.2 collective-permute-start.12
  585.6 15.7 %collective-permute-start.14 = (bf16[136,4,64]{0,2,1:T(8,128)(2,1)S(1)}, bf16[136,4,64]{0,2,1:T(8,128)(2,1)S(1)}, u32[]{:S(2)}, u32[]{:S(2)}) collective-permute-start(bf16[136,4,64]{0,2,1:T(8,128)(2,1)S(1)} %copy.73), channel_id=1, source_target_pairs={{2,0},{4,2},{6,4},{3,1},{5,3},{7,5},{10,8},{12,10},{14,12},{11,9},... | collective-permute-start | bytes 208904 | tf_op jit(solution)/shard_map/ppermute | solution.py:19
  586.9 9.7 %collective-permute-start.15 = (bf16[136,4,64]{0,2,1:T(8,128)(2,1)S(1)}, bf16[136,4,64]{0,2,1:T(8,128)(2,1)S(1)}, u32[]{:S(2)}, u32[]{:S(2)}) collective-permute-start(bf16[136,4,64]{0,2,1:T(8,128)(2,1)S(1)} %copy.77), channel_id=1, source_target_pairs={{0,2},{2,4},{4,6},{1,3},{3,5},{5,7},{8,10},{10,12},{12,14},{9,11},... | collective-permute-start | bytes 208904 | tf_op jit(solution)/shard_map/ppermute | solution.py:17
  611.5 5.8 copy-start.11
  626.1 20.6 %copy-start.23 = (f32[128,128]{1,0:T(8,128)S(1)}, f32[128,128]{1,0:T(8,128)}, u32[]{:S(2)}) copy-start(f32[128,128]{1,0:T(8,128)} %copy-done.22) | copy-start | bytes 196612
  646.7 8.3 %slice-start.4 = ((s8[8388608]{0:T(1024)(128)(4,1)}), s8[4194304]{0:T(1024)(128)(4,1)S(1)}, s32[]{:S(2)}) async-start(s8[8388608]{0:T(1024)(128)(4,1)} %bitcast.215), calls=%async_computation.8 | async-start | bytes 8388608
  646.7 8.3 %slice-start.5 = ((s8[8388608]{0:T(1024)(128)(4,1)}), s8[4194304]{0:T(1024)(128)(4,1)S(1)}, s32[]{:S(2)}) async-start(s8[8388608]{0:T(1024)(128)(4,1)} %bitcast.215), calls=%async_computation.9 | async-start | bytes 8388608
  663.1 9.0 %copy-start.1 = (bf16[128,64]{0,1:T(8,128)(2,1)S(1)}, bf16[128,64]{0,1:T(8,128)(2,1)}, u32[]{:S(2)}) copy-start(bf16[128,64]{0,1:T(8,128)(2,1)} %param.14) | copy-start | bytes 49156
  (10 other events, 31.8 us)
where the time goes:
time: 680 us; the launch traced here: 672 us
  matrix products  198 us (29%)
  local copies, waits for them, and re-layouts  174 us (26%)
  other arithmetic  106 us (16%)
  waiting for transfers between devices  82.6 us (12%)
  starting transfers between devices  60 us (9%)
  blocking collectives  50.6 us (7%)
    dot_general x34, matrix products, dilated(): jnp.dot(window, weight, preferred_element_type=jnp.float32)  118 us
    all_to_all x1, blocking collectives, shards(): lax.all_to_all(logit_grad.reshape(block_rows, map_size * bin_count), 'col...  50.6 us
    all_to_all x1, waiting for transfers between devices, shards(): lax.all_to_all(flat_logits, 'col', split_axis=0, concat_axis=1, tiled=True)  45.8 us
    dot_general x2, matrix products, block_back(): jnp.dot(lowered_grad.astype(jnp.bfloat16), down_weight.T, preferred_eleme...  42.2 us
    div x1, other arithmetic, shards(): probability = exponent / jnp.sum(exponent, -1, keepdims=True)  33.8 us
    all_to_all x1, waiting for transfers between devices, shards(): lax.all_to_all(row_block, ('row', 'col'), split_axis=1, concat_axis=0, ti...  33.6 us
    ppermute x8, starting transfers between devices, padded_2(): lax.ppermute(tail, axis, [(i, (i + 1) % count) for i in range(ends)])  30.7 us
    slice x8, local copies, waits for them, and re-layouts, padded_2(): head = lax.slice_in_dim(cells, 0, width, axis=dim)  28.4 us
  transfers between devices with their start and end apart: 19, of which 5 were waited for; matrix products, arithmetic and copies ran while one was open for 11% of the time, Pallas kernels for 0%

commit v1 on v0

v1 whole, which is shorter than its diff:
```python
import functools

import jax
import jax.numpy as jnp
from jax import lax
from jax.experimental import pallas as pl
from jax.experimental.pallas import tpu as pltpu
from jax.sharding import PartitionSpec as P

epsilon = 1e-05
F32 = jnp.float32
BF16 = jnp.bfloat16
ROWS = 4
EDGE = 8
PAD = 16


def lane_low(shape):
    return lax.broadcasted_iota(jnp.int32, shape, len(shape) - 1) < shape[-1] // 2


def standardize(values):
    centred = values - jnp.mean(values, -1, keepdims=True)
    variance = jnp.mean(centred * centred, -1, keepdims=True)
    inverse = lax.rsqrt(variance + epsilon)
    return centred * inverse, inverse


def elu(values):
    return jnp.where(values > 0, values, jnp.exp(jnp.minimum(values, 0.0)) - 1.0)


def slope_of(values):
    return jnp.where(values > 0, 1.0, jnp.exp(jnp.minimum(values, 0.0)))


def slope_from_elu(activated):
    return 1.0 + jnp.minimum(activated, 0.0)


def standardize_back(standard, inverse, upstream):
    along = jnp.mean(upstream, -1, keepdims=True)
    across = jnp.mean(upstream * standard, -1, keepdims=True)
    return inverse * (upstream - along - standard * across)


def squeeze(stream, gain, down):
    standard, unused = standardize(stream)
    entered = elu(standard * gain).astype(BF16)
    return elu(jnp.dot(entered, down, preferred_element_type=F32))


def store_edges(values, refs, spacing, step, steps):
    top, bottom, left, right, corner_a, corner_b, corner_c, corner_d = refs
    columns = values.shape[2]
    low = lane_low((ROWS, EDGE, values.shape[3]))
    left[...] = jnp.where(low, values[0, :, :EDGE], values[1, :, :EDGE]).astype(BF16)
    right[...] = jnp.where(low, values[0, :, columns - EDGE :], values[1, :, columns - EDGE :]).astype(BF16)
    wide = lane_low((ROWS, columns // 2, values.shape[3]))
    taken = spacing // ROWS

    @pl.when(step < taken)
    def _():
        top[...] = jnp.where(wide, values[0, :, : columns // 2], values[0, :, columns // 2 :]).astype(BF16)
        corner_a[...] = values[0, :, :EDGE].astype(BF16)
        corner_b[...] = values[0, :, columns - EDGE :].astype(BF16)

    @pl.when(step >= steps - taken)
    def _():
        bottom[...] = jnp.where(wide, values[1, :, : columns // 2], values[1, :, columns // 2 :]).astype(BF16)
        corner_c[...] = values[1, :, :EDGE].astype(BF16)
        corner_d[...] = values[1, :, columns - EDGE :].astype(BF16)


def fill_padded(padded, centre, halos, spacing):
    above, below, before, after, corner_a, corner_b, corner_c, corner_d = halos
    rows, columns, lanes = centre.shape
    half = rows // 2

    def lay(row, carry):
        padded[spacing + row, PAD : PAD + columns] = centre[row]
        return carry

    lax.fori_loop(0, rows, lay, 0)

    def twice(packed):
        turned = pltpu.roll(packed, lanes // 2, packed.ndim - 1)
        low = lane_low(packed.shape)
        return jnp.where(low, packed, turned).astype(BF16), jnp.where(low, turned, packed).astype(BF16)

    def sides(row, carry):
        for halo, start in ((before, PAD - EDGE), (after, PAD + columns)):
            first, second = twice(halo[row].astype(F32))
            padded[spacing + row, start : start + EDGE] = first
            padded[spacing + half + row, start : start + EDGE] = second
        return carry

    lax.fori_loop(0, half, sides, 0)
    for halo, one, two, base in ((above, corner_a, corner_b, 0), (below, corner_c, corner_d, spacing + rows)):
        for row in range(spacing):
            first, second = twice(halo[row].astype(F32))
            padded[base + row, PAD : PAD + columns // 2] = first
            padded[base + row, PAD + columns // 2 : PAD + columns] = second
            padded[base + row, PAD - EDGE : PAD] = one[row]
            padded[base + row, PAD + columns : PAD + columns + EDGE] = two[row]


def convolve(padded, kernel, taps, spacing, step, half, columns):
    width = columns + 2 * PAD
    lanes = padded.shape[2]
    low = lane_low((ROWS, width, lanes))
    parts = []
    for side in range(2):
        start = side * half + step * ROWS
        first, second, third = (padded[pl.ds(start + tap * spacing, ROWS)] for tap in range(3))
        parts.append(jnp.concatenate([jnp.where(low, first, second), third], axis=2))
    joined = jnp.concatenate(parts, axis=0).reshape(2 * ROWS * width, 2 * lanes)
    taps[...] = jnp.dot(joined, kernel[...], preferred_element_type=F32).reshape(2 * ROWS, width, 3 * lanes)
    total = taps[:, PAD : PAD + columns, lanes : 2 * lanes]
    total = total + taps[:, PAD - spacing : PAD - spacing + columns, :lanes]
    total = total + taps[:, PAD + spacing : PAD + spacing + columns, 2 * lanes :]
    return total.reshape(2 * ROWS * columns, lanes)


def strip(reference):
    return reference[...].reshape(-1, reference.shape[-1])


def entry_kernel(spacing, steps, features, gain, down, squeezed, *edges):
    step = pl.program_id(0)
    values = squeeze(strip(features).astype(F32), gain[...], down[...]).reshape(squeezed.shape)
    squeezed[...] = values.astype(BF16)
    store_edges(values, edges, spacing, step, steps)


def middle_kernel(near, far, steps, centre, *rest):
    halos, rest = rest[:8], rest[8:]
    features, kernel, up, gain, down, stream_out, activated_out, squeezed, *rest = rest
    edges, (padded, taps) = rest[:8], rest[8:]
    step = pl.program_id(0)
    half, columns = centre.shape[0] // 2, centre.shape[1]

    @pl.when(step == 0)
    def _():
        fill_padded(padded, centre, halos, near)

    activated = elu(convolve(padded, kernel, taps, near, step, half, columns)).astype(BF16)
    activated_out[...] = activated.reshape(activated_out.shape)
    stream = strip(features).astype(F32) + jnp.dot(activated, up[...], preferred_element_type=F32)
    stream_out[...] = stream.reshape(stream_out.shape)
    values = squeeze(stream, gain[...], down[...]).reshape(squeezed.shape)
    squeezed[...] = values.astype(BF16)
    store_edges(values, edges, far, step, steps)


def head_kernel(near, steps, centre, *rest):
    halos, rest = rest[:8], rest[8:]
    stream_in, kernel, up, gain, head, bias, stream_out, activated_out, by_row, by_column, padded, taps = rest
    step = pl.program_id(0)
    half, columns = centre.shape[0] // 2, centre.shape[1]

    @pl.when(step == 0)
    def _():
        fill_padded(padded, centre, halos, near)

    activated = elu(convolve(padded, kernel, taps, near, step, half, columns)).astype(BF16)
    activated_out[...] = activated.reshape(activated_out.shape)
    stream = strip(stream_in) + jnp.dot(activated, up[...], preferred_element_type=F32)
    stream_out[...] = stream.reshape(stream_out.shape)
    standard, unused = standardize(stream)
    entered = (standard * gain[...]).astype(BF16).reshape(2, ROWS, columns, stream.shape[1])
    pairs = jnp.concatenate([entered[0], entered[1]], axis=2).reshape(ROWS * columns, -1)
    logits = jnp.dot(pairs, head[...], preferred_element_type=F32) + bias[...]
    by_row[...] = logits.astype(BF16).reshape(by_row.shape)
    pairs = jnp.concatenate([entered[:, :, : columns // 2], entered[:, :, columns // 2 :]], axis=3)
    logits = jnp.dot(pairs.reshape(ROWS * columns, -1), head[...], preferred_element_type=F32) + bias[...]
    by_column[...] = logits.astype(BF16).reshape(by_column.shape)


def loss_kernel(
    spacing, steps, by_row, facing, targets, stream, activated, gain, head, group, up, grad_out, conv_out, *rest
):
    edges, (turned,) = rest[:8], rest[8:]
    step = pl.program_id(0)
    inner = facing.shape[1] // ROWS

    @pl.when(step % inner == 0)
    def _():
        turned[...] = jnp.swapaxes(facing[...].astype(F32), 0, 1)

    start = (step % inner) * ROWS
    columns, lanes = by_row.shape[1:]
    symmetric = 0.5 * (by_row[...].astype(F32) + turned[pl.ds(start, ROWS)])
    exponent = jnp.exp(symmetric).reshape(ROWS * columns, lanes)
    upper = exponent.astype(BF16)
    lower = (exponent - upper.astype(F32)).astype(BF16)
    total = jnp.dot(upper, group[...], preferred_element_type=F32) + jnp.dot(
        lower, group[...], preferred_element_type=F32
    )
    logit_grad = (exponent / total - targets[...].astype(F32).reshape(exponent.shape)).astype(BF16)
    back = jnp.dot(logit_grad, head[...], preferred_element_type=F32)
    width = back.shape[1] // 2
    back = jnp.concatenate([back[:, :width], back[:, width:]], axis=0)
    standard, inverse = standardize(strip(stream))
    grad = standardize_back(standard, inverse, back * gain[...])
    grad_out[...] = grad.reshape(grad_out.shape)
    values = jnp.dot(grad.astype(BF16), up[...], preferred_element_type=F32)
    values = values * slope_from_elu(strip(activated).astype(F32))
    values = values.reshape(conv_out.shape)
    conv_out[...] = values.astype(BF16)
    store_edges(values, edges, spacing, step, steps)


def back_strip(spacing, step, centre, padded, taps, kernel, squeezed, down, stream, gain, upstream):
    half, columns = centre.shape[0] // 2, centre.shape[1]
    lowered = convolve(padded, kernel, taps, spacing, step, half, columns)
    lowered = lowered * slope_from_elu(strip(squeezed).astype(F32))
    entered = jnp.dot(lowered.astype(BF16), down[...], preferred_element_type=F32)
    standard, inverse = standardize(strip(stream).astype(F32))
    entered = entered * slope_of(standard * gain[...])
    return strip(upstream) + standardize_back(standard, inverse, entered * gain[...])


def back_kernel(near, far, steps, centre, *rest):
    halos, rest = rest[:8], rest[8:]
    kernel, squeezed, down, stream, gain, upstream, activated, up, grad_out, conv_out, *rest = rest
    edges, (padded, taps) = rest[:8], rest[8:]
    step = pl.program_id(0)

    @pl.when(step == 0)
    def _():
        fill_padded(padded, centre, halos, near)

    grad = back_strip(near, step, centre, padded, taps, kernel, squeezed, down, stream, gain, upstream)
    grad_out[...] = grad.reshape(grad_out.shape)
    values = jnp.dot(grad.astype(BF16), up[...], preferred_element_type=F32)
    values = values * slope_from_elu(strip(activated).astype(F32))
    values = values.reshape(conv_out.shape)
    conv_out[...] = values.astype(BF16)
    store_edges(values, edges, far, step, steps)


def final_kernel(near, centre, *rest):
    halos, rest = rest[:8], rest[8:]
    kernel, squeezed, down, stream, gain, upstream, grad_out, padded, taps = rest
    step = pl.program_id(0)

    @pl.when(step == 0)
    def _():
        fill_padded(padded, centre, halos, near)

    grad = back_strip(near, step, centre, padded, taps, kernel, squeezed, down, stream, gain, upstream)
    grad_out[...] = grad.reshape(grad_out.shape)


def shifted(values, row_move, col_move):
    rows, cols = lax.axis_size("row"), lax.axis_size("col")
    pairs = []
    for row in range(rows):
        for col in range(cols):
            if 0 <= row + row_move < rows and 0 <= col + col_move < cols:
                pairs.append((row * cols + col, (row + row_move) * cols + col + col_move))
    return lax.ppermute(values, ("row", "col"), pairs)


def exchange(edges):
    top, bottom, left, right, corner_a, corner_b, corner_c, corner_d = edges
    return (
        shifted(bottom, 1, 0),
        shifted(top, -1, 0),
        shifted(right, 0, 1),
        shifted(left, 0, -1),
        shifted(corner_d, 1, 1),
        shifted(corner_c, 1, -1),
        shifted(corner_b, -1, 1),
        shifted(corner_a, -1, -1),
    )


def facing_tile(tile):
    rows, cols = lax.axis_size("row"), lax.axis_size("col")
    if rows == cols:
        pairs = [(row * cols + col, col * cols + row) for row in range(rows) for col in range(cols)]
        return lax.ppermute(tile, ("row", "col"), pairs)
    if cols % rows:
        raise ValueError("unsupported mesh")
    times = cols // rows
    height = tile.shape[0] // times
    place = lax.axis_index("col") % times
    received = []
    for turn in range(times):
        piece = lax.dynamic_slice_in_dim(tile, ((place + turn) % times) * height, height, axis=0)
        pairs = [
            (row * cols + col, (col // times) * cols + times * row + (col % times + turn) % times)
            for row in range(rows)
            for col in range(cols)
        ]
        received.append(lax.ppermute(piece, ("row", "col"), pairs))
    stacked = jnp.stack(received)
    pieces = [
        lax.dynamic_index_in_dim(stacked, (place - source) % times, axis=0, keepdims=False)
        for source in range(times)
    ]
    return jnp.concatenate(pieces, axis=1)


def facing_logits(by_column):
    if lax.axis_size("row") == lax.axis_size("col"):
        return facing_tile(by_column)
    bins = by_column.shape[2] // 2
    tile = facing_tile(jnp.concatenate([by_column[..., :bins], by_column[..., bins:]], axis=1))
    half = tile.shape[1] // 2
    return jnp.concatenate([tile[:, :half], tile[:, half:]], axis=2)


def dilated_weights(kernel):
    twice = jnp.concatenate([kernel, kernel], axis=3)
    flat = jnp.transpose(twice, (0, 2, 1, 3)).reshape(3 * kernel.shape[2], -1)
    return jnp.pad(flat, ((0, kernel.shape[2]), (0, 0)))


def mirrored(kernel):
    return jnp.swapaxes(kernel[::-1, ::-1], 2, 3)


def doubled_columns(weight):
    return jnp.concatenate([weight, weight], axis=1)


def padded_rows(weight):
    return jnp.pad(weight, ((0, weight.shape[0]), (0, 0)))


def diagonal(weight):
    zeros = jnp.zeros_like(weight)
    return jnp.concatenate(
        [jnp.concatenate([weight, zeros], axis=1), jnp.concatenate([zeros, weight], axis=1)], axis=0
    )


def shards(features, labels, norm_gain, w_down, w_conv, w_up, w_head, head_bias):
    rows, columns, channels = features.shape
    narrow = w_down.shape[2]
    bins = w_head.shape[1]
    half = rows // 2
    steps = half // ROWS
    lanes = 2 * narrow
    near, far = 4, 8

    gains = [norm_gain[index : index + 1] for index in range(3)]
    downs = [doubled_columns(w_down[index]) for index in range(2)]
    downs_back = [padded_rows(w_down[index].T) for index in range(2)]
    ups = [padded_rows(w_up[index]) for index in range(2)]
    ups_back = [doubled_columns(w_up[index].T) for index in range(2)]
    convs = [dilated_weights(w_conv[index]) for index in range(2)]
    convs_back = [dilated_weights(mirrored(w_conv[index])) for index in range(2)]
    head = diagonal(w_head)
    head_back = diagonal(w_head.T)
    bias = jnp.concatenate([head_bias, head_bias])[None]
    group = diagonal(jnp.ones((bins, bins), BF16))

    def whole(array):
        zeros = (0,) * array.ndim
        return pl.BlockSpec(array.shape, lambda step: zeros)

    def strip_spec(width):
        return pl.BlockSpec((2, ROWS, columns, width), lambda step: (0, step, 0, 0))

    def halves(dtype, width):
        return jax.ShapeDtypeStruct((2, half, columns, width), dtype)

    def edges(spacing):
        taken = spacing // ROWS
        first = lambda step: (jnp.minimum(step, taken - 1), 0, 0)
        last = lambda step: (jnp.maximum(step - (steps - taken), 0), 0, 0)
        each = lambda step: (step, 0, 0)
        entries = [
            ((spacing, columns // 2, lanes), first),
            ((spacing, columns // 2, lanes), last),
            ((half, EDGE, lanes), each),
            ((half, EDGE, lanes), each),
            ((spacing, EDGE, lanes), first),
            ((spacing, EDGE, lanes), first),
            ((spacing, EDGE, lanes), last),
            ((spacing, EDGE, lanes), last),
        ]
        shapes = [jax.ShapeDtypeStruct(shape, BF16) for shape, index in entries]
        specs = [pl.BlockSpec((ROWS,) + shape[1:], index) for shape, index in entries]
        return shapes, specs

    def scratch(spacing):
        width = columns + 2 * PAD
        return [
            pltpu.VMEM((rows + 2 * spacing, width, lanes), BF16),
            pltpu.VMEM((2 * ROWS, width, 3 * lanes), F32),
        ]

    def cost(convolutions, passes):
        pixels = rows * columns
        return pl.CostEstimate(
            flops=pixels * (convolutions * 18 * narrow * narrow + 4 * narrow * channels),
            bytes_accessed=pixels * channels * passes,
            transcendentals=pixels * channels,
        )

    def call(body, inputs, specs, shapes, out_specs, scratch_shapes, estimate, name):
        return pl.pallas_call(
            body,
            grid=(steps,),
            in_specs=specs,
            out_specs=out_specs,
            out_shape=shapes,
            scratch_shapes=scratch_shapes,
            compiler_params=pltpu.CompilerParams(vmem_limit_bytes=56 * 1024 * 1024),
            cost_estimate=estimate,
            name=name,
        )(*inputs)

    split = features.reshape(2, half, columns, channels)
    bf_spec = strip_spec(channels)
    near_shapes, near_specs = edges(near)
    far_shapes, far_specs = edges(far)

    squeezed_1, *sent = call(
        functools.partial(entry_kernel, near, steps),
        (split, gains[0], downs[0]),
        [bf_spec, whole(gains[0]), whole(downs[0])],
        [halves(BF16, lanes)] + near_shapes,
        [strip_spec(lanes)] + near_specs,
        [],
        cost(0, 4),
        "entry",
    )
    halos = exchange(sent)

    def tile(array):
        return array.reshape(rows, columns, array.shape[-1])

    centre = tile(squeezed_1)
    stream_1, activated_1, squeezed_2, *sent = call(
        functools.partial(middle_kernel, near, far, steps),
        (centre, *halos, split, convs[0], ups[0], gains[1], downs[1]),
        [whole(centre)] + [whole(halo) for halo in halos] + [bf_spec]
        + [whole(array) for array in (convs[0], ups[0], gains[1], downs[1])],
        [halves(F32, channels), halves(BF16, lanes), halves(BF16, lanes)] + far_shapes,
        [strip_spec(channels), strip_spec(lanes), strip_spec(lanes)] + far_specs,
        scratch(near),
        cost(1, 12),
        "middle",
    )
    halos = exchange(sent)

    centre = tile(squeezed_2)
    by_row_spec = pl.BlockSpec((ROWS, columns, 2 * bins), lambda step: (step, 0, 0))
    stream_2, activated_2, by_row, by_column = call(
        functools.partial(head_kernel, far, steps),
        (centre, *halos, stream_1, convs[1], ups[1], gains[2], head, bias),
        [whole(centre)] + [whole(halo) for halo in halos] + [bf_spec]
        + [whole(array) for array in (convs[1], ups[1], gains[2], head, bias)],
        [
            halves(F32, channels),
            halves(BF16, lanes),
            jax.ShapeDtypeStruct((half, columns, 2 * bins), BF16),
            jax.ShapeDtypeStruct((2, half, columns // 2, 2 * bins), BF16),
        ],
        [
            strip_spec(channels),
            strip_spec(lanes),
            by_row_spec,
            pl.BlockSpec((2, ROWS, columns // 2, 2 * bins), lambda step: (0, step, 0, 0)),
        ],
        scratch(far),
        cost(1, 14),
        "head",
    )
    facing = facing_logits(by_column.reshape(rows, columns // 2, 2 * bins))

    own_labels = lax.all_to_all(labels, "col", split_axis=1, concat_axis=0, tiled=True)
    facing_labels = facing_tile(own_labels).T
    numbers = jnp.arange(bins, dtype=jnp.int32)

    def onehot(values):
        return (values[:, :, None] == numbers).astype(F32)

    targets = jnp.concatenate(
        [
            0.5 * (onehot(own_labels[part]) + onehot(facing_labels[part]))
            for part in (slice(0, half), slice(half, rows))
        ],
        axis=2,
    ).astype(BF16)

    inner = 16 // ROWS
    grad_2, conv_grad_2, *sent = call(
        functools.partial(loss_kernel, far, steps),
        (by_row, facing, targets, stream_2, activated_2, gains[2], head_back, group, ups_back[1]),
        [
            by_row_spec,
            pl.BlockSpec((columns, ROWS * inner, 2 * bins), lambda step: (0, step // inner, 0)),
            by_row_spec,
            bf_spec,
            strip_spec(lanes),
        ]
        + [whole(array) for array in (gains[2], head_back, group, ups_back[1])],
        [halves(F32, channels), halves(BF16, lanes)] + far_shapes,
        [strip_spec(channels), strip_spec(lanes)] + far_specs,
        [pltpu.VMEM((ROWS * inner, columns, 2 * bins), F32)],
        cost(0, 18),
        "loss",
    )
    halos = exchange(sent)

    centre = tile(conv_grad_2)
    grad_1, conv_grad_1, *sent = call(
        functools.partial(back_kernel, far, near, steps),
        (centre, *halos, convs_back[1], squeezed_2, downs_back[1], stream_1, gains[1], grad_2, activated_1, ups_back[0]),
        [whole(centre)] + [whole(halo) for halo in halos]
        + [
            whole(convs_back[1]),
            strip_spec(lanes),
            whole(downs_back[1]),
            bf_spec,
            whole(gains[1]),
            bf_spec,
            strip_spec(lanes),
            whole(ups_back[0]),
        ],
        [halves(F32, channels), halves(BF16, lanes)] + near_shapes,
        [strip_spec(channels), strip_spec(lanes)] + near_specs,
        scratch(far),
        cost(1, 20),
        "back",
    )
    halos = exchange(sent)

    centre = tile(conv_grad_1)
    (grad_0,) = call(
        functools.partial(final_kernel, near),
        (centre, *halos, convs_back[0], squeezed_1, downs_back[0], split, gains[0], grad_1),
        [whole(centre)] + [whole(halo) for halo in halos]
        + [
            whole(convs_back[0]),
            strip_spec(lanes),
            whole(downs_back[0]),
            bf_spec,
            whole(gains[0]),
            bf_spec,
        ],
        [halves(F32, channels)],
        [strip_spec(channels)],
        scratch(near),
        cost(1, 16),
        "final",
    )
    return grad_0.reshape(features.shape)


def solution(mesh):
    return jax.shard_map(
        shards,
        mesh=mesh,
        in_specs=(
            P(("dp", "row"), "col", None),
            P(("dp", "row", "col"), None),
            P(),
            P(),
            P(),
            P(),
            P(),
            P(),
        ),
        out_specs=P(("dp", "row"), "col", None),
        check_vma=False,
    )
```

time: 680 us -> 383 us (0.56)
  matrix products: 198 us -> 0 us
  local copies, waits for them, and re-layouts: 174 us -> 15 us
  Pallas kernels: 0 us -> 155 us
  other arithmetic: 106 us -> 11.8 us
  blocking collectives: 50.6 us -> 0 us
  starting transfers between devices: 60 us -> 89.4 us
  waiting for transfers between devices: 82.6 us -> 107 us
    dot_general x44 -> x0, matrix products: 198 us -> none  [the longest x34 118 us: dilated(): jnp.dot(window, weight, preferred_element_type=jnp.float32)]
    pallas_call x0 -> x6, Pallas kernels: none -> 155 us  [call(): pl.pallas_call(body, grid=(steps,), in_specs=specs, out_specs=out_specs,...]
    slice x17 -> x6, local copies, waits for them, and re-layouts: 56.8 us -> 1.63 us  [the longest x1 1.39 us: shards(): gains = [norm_gain[index:index + 1] for index in range(3)]]
    all_to_all x1 -> x0, blocking collectives: 50.6 us -> none  [shards(): lax.all_to_all(logit_grad.reshape(block_rows, map_size * bin_count), 'col...]
    ppermute x16 -> x34, starting transfers between devices: 45.8 us -> 86.1 us  [the longest x32 81.2 us: shifted(): return lax.ppermute(values, ('row', 'col'), pairs)]
    ppermute x8 -> x0, local copies, waits for them, and re-layouts: 38.7 us -> none  [the longest x4 19.6 us: padded_2(): lax.ppermute(tail, axis, [(i, (i + 1) % count) for i in range(ends)])]
    div x10 -> x0, other arithmetic: 33.9 us -> none  [the longest x1 33.8 us: shards(): probability = exponent / jnp.sum(exponent, -1, keepdims=True)]
    reduce_sum x7 -> x0, other arithmetic: 32.8 us -> none  [the longest x3 23.1 us: normalize(): centred = values - average]
  transfers between devices with their start and end apart: 19 -> 35, of which waited for: 5 -> 8; matrix products, arithmetic and copies ran while one was open for 11% -> 5% of each run, Pallas kernels for 0% -> 0%
where the time goes in v1:
time: 383 us; the launch traced here: 379 us
  Pallas kernels  155 us (40%)
  waiting for transfers between devices  107 us (28%)
  starting transfers between devices  89.4 us (23%)
  local copies, waits for them, and re-layouts  15 us (4%)
  other arithmetic  11.8 us (3%)
    pallas_call x6, Pallas kernels, call(): pl.pallas_call(body, grid=(steps,), in_specs=specs, out_specs=out_specs,...  155 us
    all_to_all x1, waiting for transfers between devices, shards(): lax.all_to_all(labels, 'col', split_axis=1, concat_axis=0, tiled=True)  87.9 us
    ppermute x32, starting transfers between devices, shifted(): return lax.ppermute(values, ('row', 'col'), pairs)  81.2 us
    ppermute x32, waiting for transfers between devices, shifted(): return lax.ppermute(values, ('row', 'col'), pairs)  15.7 us
  transfers between devices with their start and end apart: 35, of which 8 were waited for; matrix products, arithmetic and copies ran while one was open for 5% of the time, Pallas kernels for 0%

profile of v1, /device:TPU:1, one launch (start us, length us, event | category | flops | bytes accessed | tf_op | source)
XLA Modules:
  0.0 379.3 jit_solution(4793482682521678084)
XLA Ops:
  1.5 1.4 fusion.9
  2.9 14.6 %entry.1 = (bf16[2,64,128,128]{3,2,1,0:T(8,128)(2,1)}, bf16[4,64,128]{2,1,0:T(8,128)(2,1)}, bf16[4,64,128]{2,1,0:T(8,128)(2,1)}, bf16[64,8,128]{2,1,0:T(8,128)(2...) custom-call(bf16[2,64,128,128]{3,2,1,0:T(8,128)(2,1)} %bitcast.77, ...), custom_call_target="tpu_custom_call" | custom-call | flops 536870912 | bytes 8388608 | tf_op jit(solution)/shard_map/entry/pallas_call | solution.py:407
  17.5 4.0 %collective-permute-start.2 = (bf16[64,8,128]{2,1,0:T(8,128)(2,1)}, bf16[64,8,128]{2,1,0:T(8,128)(2,1)S(1)}, u32[]{:S(2)}, u32[]{:S(2)}) collective-permute-start(bf16[64,8,128]{2,1,0:T(8,128)(2,1)} %get-tuple-element.52), channel_id=1, source_target_pairs={{0,2},{2,4},{4,6},{8,10},{10,12},{12,14},{16,18},{18,20},{20,22},{... | collective-permute-start | bytes 393224 | tf_op jit(solution)/shard_map/ppermute | solution.py:263
  21.5 1.3 collective-permute-start.3
  22.8 6.1 %collective-permute-start.4 = (bf16[4,8,128]{2,1,0:T(8,128)(2,1)}, bf16[4,8,128]{2,1,0:T(8,128)(2,1)S(1)}, u32[]{:S(2)}, u32[]{:S(2)}) collective-permute-start(bf16[4,8,128]{2,1,0:T(8,128)(2,1)} %get-tuple-element.54), channel_id=1, source_target_pairs={{0,10},{2,12},{4,14},{8,18},{10,20},{12,22},{16,26},{18,28},{20,30... | collective-permute-start | bytes 24584 | tf_op jit(solution)/shard_map/ppermute | solution.py:263
  28.9 1.3 collective-permute-start.5
  30.2 4.3 %collective-permute-start.6 = (bf16[4,8,128]{2,1,0:T(8,128)(2,1)}, bf16[4,8,128]{2,1,0:T(8,128)(2,1)S(1)}, u32[]{:S(2)}, u32[]{:S(2)}) collective-permute-start(bf16[4,8,128]{2,1,0:T(8,128)(2,1)} %get-tuple-element.56), channel_id=1, source_target_pairs={{8,2},{10,4},{12,6},{16,10},{18,12},{20,14},{24,18},{26,20},{28,22... | collective-permute-start | bytes 24584 | tf_op jit(solution)/shard_map/ppermute | solution.py:263
  34.8 2.9 collective-permute-start
  37.7 1.9 collective-permute-start.1
  39.7 1.3 collective-permute-start.7
  43.2 2.7 collective-permute-done.7.rest_7_
  46.6 30.7 %middle.1 = (f32[2,64,128,128]{3,2,1,0:T(8,128)}, bf16[2,64,128,128]{3,2,1,0:T(8,128)(2,1)}, bf16[2,64,128,128]{3,2,1,0:T(8,128)(2,1)}, bf16[8,64,128]{2,1,0:T(8...) custom-call(bf16[128,128,128]{2,1,0:T(8,128)(2,1)} %bitcast.80, ...), custom_call_target="tpu_custom_call" | custom-call | flops 1744830464 | bytes 25165824 | tf_op jit(solution)/shard_map/middle/pallas_call | solution.py:407
  77.3 3.8 collective-permute-start.12
  81.1 1.3 collective-permute-start.13
  82.5 3.3 collective-permute-start.10
  85.8 1.3 collective-permute-start.11
  87.1 2.4 collective-permute-start.8
  89.5 2.2 collective-permute-start.9
  91.7 3.5 collective-permute-start.14
  99.7 4.4 %collective-permute-done.15.rest_7_ = bf16[8,8,128]{2,1,0:T(8,128)(2,1)S(1)} collective-permute-done((bf16[8,8,128]{2,1,0:T(8,128)(2,1)}, bf16[8,8,128]{2,1,0:T(8,128)(2,1)S(1)}, u32[]{:S(2)}, u32[]{:S(2)}) %collective-permute-start.15) | collective-permute-done | bytes 16416 | tf_op jit(solution)/shard_map/ppermute | solution.py:263
  104.9 29.2 %head.1 = (f32[2,64,128,128]{3,2,1,0:T(8,128)}, bf16[2,64,128,128]{3,2,1,0:T(8,128)(2,1)}, bf16[64,128,128]{2,1,0:T(8,128)(2,1)}, bf16[2,64,64,128]{3,2,1,0:T(8,128)(2,1)}) custom-call(bf16[128,128,128]{2,1,0:T(8,128)(2,1)} %bitcast.81, bf16[8,64,128]{2,1,0:T(8,128)(2,1)} %copy-done.14, bf16[8,64,128]{2,1,0:T(8,128)(2,1)} %copy-done.15, ...), custom_call_target="tpu_custom_call" | custom-call | flops 1744830464 | bytes 29360128 | tf_op jit(solution)/shard_map/head/pallas_call | solution.py:407
  134.0 2.7 collective-permute-start.16
  137.4 3.4 all-to-all-start
  142.2 87.9 %all-to-all-done = s32[32,4,128]{2,0,1:T(8,128)S(1)} async-done(((s32[32,4,128]{2,0,1:T(8,128)}), s32[32,4,128]{2,0,1:T(8,128)S(1)}, u32[]{:S(2)}, u32[]{:S(2)}) %all-to-all-start) | async-done | bytes 65568 | tf_op jit(solution)/shard_map/all_to_all | solution.py:478
  230.1 2.1 collective-permute-start.17
  232.2 3.4 collective-permute-done.17
  235.9 5.7 %multiply_convert_fusion = (bf16[64,128,64]{2,1,0:T(8,128)(2,1)S(1)}, bf16[64,128,64]{2,1,0:T(8,128)(2,1)S(1)}) fusion(s32[64,128]{1,0:T(8,128)S(1)} %copy.82, s32[64,128]{1,0:T(8,128)S(1)} %bitcast.96, s32[64,128]{1,0:T(8,128)S(1)} %copy.81, s32[64,128]{1,0:T(8,128)S(1)} %bitcast.95), kind=kLoop, calls=%fused_computation | loop fusion | flops 7340032 | bytes 2228224 | tf_op jit(solution)/shard_map/convert.1
  241.6 2.5 pad_maximum_fusion.targets
  244.1 1.3 copy-done.2
  245.4 22.0 %loss.1 = (f32[2,64,128,128]{3,2,1,0:T(8,128)}, bf16[2,64,128,128]{3,2,1,0:T(8,128)(2,1)}, bf16[8,64,128]{2,1,0:T(8,128)(2,1)}, bf16[8,64,128]{2,1,0:T(8,128)(2,...) custom-call(bf16[64,128,128]{2,1,0:T(8,128)(2,1)} %get-tuple-element, ...), custom_call_target="tpu_custom_call" | custom-call | flops 536870912 | bytes 37748736 | tf_op jit(solution)/shard_map/loss/pallas_call | solution.py:407
  267.4 2.9 collective-permute-start.22
  270.3 1.3 collective-permute-start.23
  271.6 1.9 collective-permute-start.18
  273.6 2.4 collective-permute-start.19
  276.0 3.4 collective-permute-start.20
  279.5 1.3 collective-permute-start.21
  280.8 3.8 %collective-permute-start.24 = (bf16[8,8,128]{2,1,0:T(8,128)(2,1)}, bf16[8,8,128]{2,1,0:T(8,128)(2,1)S(1)}, u32[]{:S(2)}, u32[]{:S(2)}) collective-permute-start(bf16[8,8,128]{2,1,0:T(8,128)(2,1)} %get-tuple-element.79), channel_id=1, source_target_pairs={{8,2},{10,4},{12,6},{16,10},{18,12},{20,14},{24,18},{26,20},{28,22... | collective-permute-start | bytes 49160 | tf_op jit(solution)/shard_map/ppermute | solution.py:263
  289.2 4.1 %collective-permute-done.25.rest_7_ = bf16[8,8,128]{2,1,0:T(8,128)(2,1)S(1)} collective-permute-done((bf16[8,8,128]{2,1,0:T(8,128)(2,1)}, bf16[8,8,128]{2,1,0:T(8,128)(2,1)S(1)}, u32[]{:S(2)}, u32[]{:S(2)}) %collective-permute-start.25) | collective-permute-done | bytes 16416 | tf_op jit(solution)/shard_map/ppermute | solution.py:263
  294.1 31.0 %back.1 = (f32[2,64,128,128]{3,2,1,0:T(8,128)}, bf16[2,64,128,128]{3,2,1,0:T(8,128)(2,1)}, bf16[4,64,128]{2,1,0:T(8,128)(2,1)}, bf16[4,64,128]{2,1,0:T(8,128)(2,...) custom-call(bf16[128,128,128]{2,1,0:T(8,128)(2,1)} %bitcast.82, ...), custom_call_target="tpu_custom_call" | custom-call | flops 1744830464 | bytes 41943040 | tf_op jit(solution)/shard_map/back/pallas_call | solution.py:407
  325.1 3.9 %collective-permute-start.28 = (bf16[64,8,128]{2,1,0:T(8,128)(2,1)}, bf16[64,8,128]{2,1,0:T(8,128)(2,1)S(1)}, u32[]{:S(2)}, u32[]{:S(2)}) collective-permute-start(bf16[64,8,128]{2,1,0:T(8,128)(2,1)} %get-tuple-element.86), channel_id=1, source_target_pairs={{0,2},{2,4},{4,6},{8,10},{10,12},{12,14},{16,18},{18,20},{20,22},{... | collective-permute-start | bytes 393224 | tf_op jit(solution)/shard_map/ppermute | solution.py:263
  329.1 1.3 collective-permute-start.29
  330.4 4.3 %collective-permute-start.30 = (bf16[4,8,128]{2,1,0:T(8,128)(2,1)}, bf16[4,8,128]{2,1,0:T(8,128)(2,1)S(1)}, u32[]{:S(2)}, u32[]{:S(2)}) collective-permute-start(bf16[4,8,128]{2,1,0:T(8,128)(2,1)} %get-tuple-element.88), channel_id=1, source_target_pairs={{0,10},{2,12},{4,14},{8,18},{10,20},{12,22},{16,26},{18,28},{20,30... | collective-permute-start | bytes 24584 | tf_op jit(solution)/shard_map/ppermute | solution.py:263
  335.9 4.3 %collective-permute-start.32 = (bf16[4,8,128]{2,1,0:T(8,128)(2,1)}, bf16[4,8,128]{2,1,0:T(8,128)(2,1)S(1)}, u32[]{:S(2)}, u32[]{:S(2)}) collective-permute-start(bf16[4,8,128]{2,1,0:T(8,128)(2,1)} %get-tuple-element.90), channel_id=1, source_target_pairs={{8,2},{10,4},{12,6},{16,10},{18,12},{20,14},{24,18},{26,20},{28,22... | collective-permute-start | bytes 24584 | tf_op jit(solution)/shard_map/ppermute | solution.py:263
  340.2 2.6 collective-permute-start.26
  342.8 1.9 collective-permute-start.27
  344.8 1.3 collective-permute-start.33
  347.7 3.2 collective-permute-done.33.rest_7_
  351.7 27.6 %final.1 = f32[2,64,128,128]{3,2,1,0:T(8,128)} custom-call(bf16[128,128,128]{2,1,0:T(8,128)(2,1)} %bitcast.83, bf16[4,64,128]{2,1,0:T(8,128)(2,1)} %copy-done.17, bf16[4,64,128]{2,1,0:T(8,128)(2,1)} %copy-done.19, bf16[64,8,128]{2,1,0:T(8,128)(2,1)} %copy-done.9, bf16[64,8,128]{2,1,0:T(8,128)(2,1)} %copy-done.10, bf16[4,8,128]{2,1,0:T(8,128)(2,1)} %copy-done.34, ...), custom_call_target="tpu_custom_call" | custom-call | flops 1744830464 | bytes 33554432 | tf_op jit(solution)/shard_map/final/pallas_call | solution.py:407
  (149 shorter events, 21.1 us)
Async XLA Ops:
  0.0 136.8 %copy-start = (s32[32,512]{1,0:T(8,128)S(1)}, s32[32,512]{1,0:T(8,128)}, u32[]{:S(2)}) copy-start(s32[32,512]{1,0:T(8,128)} %param.9) | copy-start | bytes 196612
  0.0 34.5 %copy-start.3 = (bf16[2,3,3,64,64]{4,3,2,1,0:T(8,128)(2,1)S(1)}, bf16[2,3,3,64,64]{4,3,2,1,0:T(8,128)(2,1)}, u32[]{:S(2)}) copy-start(bf16[2,3,3,64,64]{4,3,2,1,0:T(8,128)(2,1)} %param.12) | copy-start | bytes 442372
  0.0 34.5 %copy-start.21 = (bf16[2,64,128]{2,1,0:T(8,128)(2,1)S(1)}, bf16[2,64,128]{2,1,0:T(8,128)(2,1)}, u32[]{:S(2)}) copy-start(bf16[2,64,128]{2,1,0:T(8,128)(2,1)} %param.13) | copy-start | bytes 98308
  17.5 28.4 %collective-permute-start.2 = (bf16[64,8,128]{2,1,0:T(8,128)(2,1)}, bf16[64,8,128]{2,1,0:T(8,128)(2,1)S(1)}, u32[]{:S(2)}, u32[]{:S(2)}) collective-permute-start(bf16[64,8,128]{2,1,0:T(8,128)(2,1)} %get-tuple-element.52), channel_id=1, source_target_pairs={{0,2},{2,4},{4,6},{8,10},{10,12},{12,14},{16,18},{18,20},{20,22},{... | collective-permute-start | bytes 393224 | tf_op jit(solution)/shard_map/ppermute | solution.py:263
  21.5 24.4 %collective-permute-start.3 = (bf16[64,8,128]{2,1,0:T(8,128)(2,1)}, bf16[64,8,128]{2,1,0:T(8,128)(2,1)S(1)}, u32[]{:S(2)}, u32[]{:S(2)}) collective-permute-start(bf16[64,8,128]{2,1,0:T(8,128)(2,1)} %get-tuple-element.53), channel_id=1, source_target_pairs={{2,0},{4,2},{6,4},{10,8},{12,10},{14,12},{18,16},{20,18},{22,20},{... | collective-permute-start | bytes 393224 | tf_op jit(solution)/shard_map/ppermute | solution.py:263
  22.8 11.9 %collective-permute-start.4 = (bf16[4,8,128]{2,1,0:T(8,128)(2,1)}, bf16[4,8,128]{2,1,0:T(8,128)(2,1)S(1)}, u32[]{:S(2)}, u32[]{:S(2)}) collective-permute-start(bf16[4,8,128]{2,1,0:T(8,128)(2,1)} %get-tuple-element.54), channel_id=1, source_target_pairs={{0,10},{2,12},{4,14},{8,18},{10,20},{12,22},{16,26},{18,28},{20,30... | collective-permute-start | bytes 24584 | tf_op jit(solution)/shard_map/ppermute | solution.py:263
  28.9 8.8 %collective-permute-start.5 = (bf16[4,8,128]{2,1,0:T(8,128)(2,1)}, bf16[4,8,128]{2,1,0:T(8,128)(2,1)S(1)}, u32[]{:S(2)}, u32[]{:S(2)}) collective-permute-start(bf16[4,8,128]{2,1,0:T(8,128)(2,1)} %get-tuple-element.55), channel_id=1, source_target_pairs={{2,8},{4,10},{6,12},{10,16},{12,18},{14,20},{18,24},{20,26},{22,28... | collective-permute-start | bytes 24584 | tf_op jit(solution)/shard_map/ppermute | solution.py:263
  30.2 9.4 %collective-permute-start.6 = (bf16[4,8,128]{2,1,0:T(8,128)(2,1)}, bf16[4,8,128]{2,1,0:T(8,128)(2,1)S(1)}, u32[]{:S(2)}, u32[]{:S(2)}) collective-permute-start(bf16[4,8,128]{2,1,0:T(8,128)(2,1)} %get-tuple-element.56), channel_id=1, source_target_pairs={{8,2},{10,4},{12,6},{16,10},{18,12},{20,14},{24,18},{26,20},{28,22... | collective-permute-start | bytes 24584 | tf_op jit(solution)/shard_map/ppermute | solution.py:263
  34.7 11.2 %copy-start.30 = (bf16[4,8,128]{2,1,0:T(8,128)(2,1)}, bf16[4,8,128]{2,1,0:T(8,128)(2,1)S(1)}, u32[]{:S(2)}) copy-start(bf16[4,8,128]{2,1,0:T(8,128)(2,1)S(1)} %collective-permute-done.4.rest_4_) | copy-start | bytes 24580
  34.8 11.1 %collective-permute-start = (bf16[4,64,128]{2,1,0:T(8,128)(2,1)}, bf16[4,64,128]{2,1,0:T(8,128)(2,1)S(1)}, u32[]{:S(2)}, u32[]{:S(2)}) collective-permute-start(bf16[4,64,128]{2,1,0:T(8,128)(2,1)} %get-tuple-element.50), channel_id=1, source_target_pairs={{0,8},{2,10},{4,12},{6,14},{8,16},{10,18},{12,20},{14,22},{16,24},... | collective-permute-start | bytes 196616 | tf_op jit(solution)/shard_map/ppermute | solution.py:263
  37.7 8.2 %copy-start.31 = (bf16[4,8,128]{2,1,0:T(8,128)(2,1)}, bf16[4,8,128]{2,1,0:T(8,128)(2,1)S(1)}, u32[]{:S(2)}) copy-start(bf16[4,8,128]{2,1,0:T(8,128)(2,1)S(1)} %collective-permute-done.5.rest_5_) | copy-start | bytes 24580
  37.7 8.2 %collective-permute-start.1 = (bf16[4,64,128]{2,1,0:T(8,128)(2,1)}, bf16[4,64,128]{2,1,0:T(8,128)(2,1)S(1)}, u32[]{:S(2)}, u32[]{:S(2)}) collective-permute-start(bf16[4,64,128]{2,1,0:T(8,128)(2,1)} %get-tuple-element.51), channel_id=1, source_target_pairs={{8,0},{10,2},{12,4},{14,6},{16,8},{18,10},{20,12},{22,14},{24,16},... | collective-permute-start | bytes 196616 | tf_op jit(solution)/shard_map/ppermute | solution.py:263
  39.7 6.2 %collective-permute-start.7 = (bf16[4,8,128]{2,1,0:T(8,128)(2,1)}, bf16[4,8,128]{2,1,0:T(8,128)(2,1)S(1)}, u32[]{:S(2)}, u32[]{:S(2)}) collective-permute-start(bf16[4,8,128]{2,1,0:T(8,128)(2,1)} %get-tuple-element.57), channel_id=1, source_target_pairs={{10,0},{12,2},{14,4},{18,8},{20,10},{22,12},{26,16},{28,18},{30,20... | collective-permute-start | bytes 24584 | tf_op jit(solution)/shard_map/ppermute | solution.py:263
  46.6 35.8 %copy-start.20 = (bf16[128,64]{0,1:T(8,128)(2,1)S(1)}, bf16[128,64]{0,1:T(8,128)(2,1)}, u32[]{:S(2)}) copy-start(bf16[128,64]{0,1:T(8,128)(2,1)} %param.14) | copy-start | bytes 49156
  46.6 51.0 %copy-start.38 = (f32[64]{0:T(128)S(1)}, f32[64]{0:T(128)}, u32[]{:S(2)}) copy-start(f32[64]{0:T(128)} %param.15) | copy-start | bytes 772
  77.3 12.2 %collective-permute-start.12 = (bf16[8,8,128]{2,1,0:T(8,128)(2,1)}, bf16[8,8,128]{2,1,0:T(8,128)(2,1)S(1)}, u32[]{:S(2)}, u32[]{:S(2)}) collective-permute-start(bf16[8,8,128]{2,1,0:T(8,128)(2,1)} %get-tuple-element.63), channel_id=1, source_target_pairs={{0,10},{2,12},{4,14},{8,18},{10,20},{12,22},{16,26},{18,28},{20,30... | collective-permute-start | bytes 49160 | tf_op jit(solution)/shard_map/ppermute | solution.py:263
  81.1 10.6 %collective-permute-start.13 = (bf16[8,8,128]{2,1,0:T(8,128)(2,1)}, bf16[8,8,128]{2,1,0:T(8,128)(2,1)S(1)}, u32[]{:S(2)}, u32[]{:S(2)}) collective-permute-start(bf16[8,8,128]{2,1,0:T(8,128)(2,1)} %get-tuple-element.64), channel_id=1, source_target_pairs={{2,8},{4,10},{6,12},{10,16},{12,18},{14,20},{18,24},{20,26},{22,28... | collective-permute-start | bytes 49160 | tf_op jit(solution)/shard_map/ppermute | solution.py:263
  82.5 21.6 %collective-permute-start.10 = (bf16[64,8,128]{2,1,0:T(8,128)(2,1)}, bf16[64,8,128]{2,1,0:T(8,128)(2,1)S(1)}, u32[]{:S(2)}, u32[]{:S(2)}) collective-permute-start(bf16[64,8,128]{2,1,0:T(8,128)(2,1)} %get-tuple-element.61), channel_id=1, source_target_pairs={{0,2},{2,4},{4,6},{8,10},{10,12},{12,14},{16,18},{18,20},{20,22},{... | collective-permute-start | bytes 393224 | tf_op jit(solution)/shard_map/ppermute | solution.py:263
  85.8 18.3 %collective-permute-start.11 = (bf16[64,8,128]{2,1,0:T(8,128)(2,1)}, bf16[64,8,128]{2,1,0:T(8,128)(2,1)S(1)}, u32[]{:S(2)}, u32[]{:S(2)}) collective-permute-start(bf16[64,8,128]{2,1,0:T(8,128)(2,1)} %get-tuple-element.62), channel_id=1, source_target_pairs={{2,0},{4,2},{6,4},{10,8},{12,10},{14,12},{18,16},{20,18},{22,20},{... | collective-permute-start | bytes 393224 | tf_op jit(solution)/shard_map/ppermute | solution.py:263
  87.1 17.0 %collective-permute-start.8 = (bf16[8,64,128]{2,1,0:T(8,128)(2,1)}, bf16[8,64,128]{2,1,0:T(8,128)(2,1)S(1)}, u32[]{:S(2)}, u32[]{:S(2)}) collective-permute-start(bf16[8,64,128]{2,1,0:T(8,128)(2,1)} %get-tuple-element.59), channel_id=1, source_target_pairs={{0,8},{2,10},{4,12},{6,14},{8,16},{10,18},{12,20},{14,22},{16,24},... | collective-permute-start | bytes 393224 | tf_op jit(solution)/shard_map/ppermute | solution.py:263
  89.5 14.6 %copy-start.24 = (bf16[8,8,128]{2,1,0:T(8,128)(2,1)}, bf16[8,8,128]{2,1,0:T(8,128)(2,1)S(1)}, u32[]{:S(2)}) copy-start(bf16[8,8,128]{2,1,0:T(8,128)(2,1)S(1)} %collective-permute-done.12.rest_4_) | copy-start | bytes 49156
  89.5 14.6 %collective-permute-start.9 = (bf16[8,64,128]{2,1,0:T(8,128)(2,1)}, bf16[8,64,128]{2,1,0:T(8,128)(2,1)S(1)}, u32[]{:S(2)}, u32[]{:S(2)}) collective-permute-start(bf16[8,64,128]{2,1,0:T(8,128)(2,1)} %get-tuple-element.60), channel_id=1, source_target_pairs={{8,0},{10,2},{12,4},{14,6},{16,8},{18,10},{20,12},{22,14},{24,16},... | collective-permute-start | bytes 393224 | tf_op jit(solution)/shard_map/ppermute | solution.py:263
  91.7 12.4 %copy-start.25 = (bf16[8,8,128]{2,1,0:T(8,128)(2,1)}, bf16[8,8,128]{2,1,0:T(8,128)(2,1)S(1)}, u32[]{:S(2)}) copy-start(bf16[8,8,128]{2,1,0:T(8,128)(2,1)S(1)} %collective-permute-done.13.rest_5_) | copy-start | bytes 49156
  91.7 4.6 %collective-permute-start.14 = (bf16[8,8,128]{2,1,0:T(8,128)(2,1)}, bf16[8,8,128]{2,1,0:T(8,128)(2,1)S(1)}, u32[]{:S(2)}, u32[]{:S(2)}) collective-permute-start(bf16[8,8,128]{2,1,0:T(8,128)(2,1)} %get-tuple-element.65), channel_id=1, source_target_pairs={{8,2},{10,4},{12,6},{16,10},{18,12},{20,14},{24,18},{26,20},{28,22... | collective-permute-start | bytes 49160 | tf_op jit(solution)/shard_map/ppermute | solution.py:263
  96.3 7.7 %collective-permute-start.15 = (bf16[8,8,128]{2,1,0:T(8,128)(2,1)}, bf16[8,8,128]{2,1,0:T(8,128)(2,1)S(1)}, u32[]{:S(2)}, u32[]{:S(2)}) collective-permute-start(bf16[8,8,128]{2,1,0:T(8,128)(2,1)} %get-tuple-element.66), channel_id=1, source_target_pairs={{10,0},{12,2},{14,4},{18,8},{20,10},{22,12},{26,16},{28,18},{30,20... | collective-permute-start | bytes 49160 | tf_op jit(solution)/shard_map/ppermute | solution.py:263
  134.0 110.1 %collective-permute-start.16 = (bf16[128,64,128]{2,1,0:T(8,128)(2,1)}, bf16[128,64,128]{2,1,0:T(8,128)(2,1)S(1)}, u32[]{:S(2)}, u32[]{:S(2)}) collective-permute-start(bf16[128,64,128]{2,1,0:T(8,128)(2,1)} %bitcast.100), channel_id=1, source_target_pairs={{0,0},{2,8},{4,16},{6,24},{8,2},{10,10},{12,18},{14,26},{16,4},{18... | collective-permute-start | bytes 6291464 | tf_op jit(solution)/shard_map/ppermute | solution.py:284
  137.4 92.7 %all-to-all-start = ((s32[32,4,128]{2,0,1:T(8,128)}), s32[32,4,128]{2,0,1:T(8,128)S(1)}, u32[]{:S(2)}, u32[]{:S(2)}) async-start(s32[32,4,128]{2,0,1:T(8,128)} %copy_bitcast_fusion.4), calls=%async_computation | async-start | bytes 131072 | tf_op jit(solution)/shard_map/all_to_all | solution.py:478
  230.1 5.6 %collective-permute-start.17 = (s32[128,128]{1,0:T(8,128)S(1)}, s32[128,128]{1,0:T(8,128)S(1)}, u32[]{:S(2)}, u32[]{:S(2)}) collective-permute-start(s32[128,128]{1,0:T(8,128)S(1)} %bitcast.92), channel_id=1, source_target_pairs={{0,0},{2,8},{4,16},{6,24},{8,2},{10,10},{12,18},{14,26},{16,4},{18... | collective-permute-start | bytes 196616 | tf_op jit(solution)/shard_map/ppermute | solution.py:284
  267.4 12.0 %collective-permute-start.22 = (bf16[8,8,128]{2,1,0:T(8,128)(2,1)}, bf16[8,8,128]{2,1,0:T(8,128)(2,1)S(1)}, u32[]{:S(2)}, u32[]{:S(2)}) collective-permute-start(bf16[8,8,128]{2,1,0:T(8,128)(2,1)} %get-tuple-element.77), channel_id=1, source_target_pairs={{0,10},{2,12},{4,14},{8,18},{10,20},{12,22},{16,26},{18,28},{20,30... | collective-permute-start | bytes 49160 | tf_op jit(solution)/shard_map/ppermute | solution.py:263
  270.3 10.4 %collective-permute-start.23 = (bf16[8,8,128]{2,1,0:T(8,128)(2,1)}, bf16[8,8,128]{2,1,0:T(8,128)(2,1)S(1)}, u32[]{:S(2)}, u32[]{:S(2)}) collective-permute-start(bf16[8,8,128]{2,1,0:T(8,128)(2,1)} %get-tuple-element.78), channel_id=1, source_target_pairs={{2,8},{4,10},{6,12},{10,16},{12,18},{14,20},{18,24},{20,26},{22,28... | collective-permute-start | bytes 49160 | tf_op jit(solution)/shard_map/ppermute | solution.py:263
  271.6 21.7 %collective-permute-start.18 = (bf16[8,64,128]{2,1,0:T(8,128)(2,1)}, bf16[8,64,128]{2,1,0:T(8,128)(2,1)S(1)}, u32[]{:S(2)}, u32[]{:S(2)}) collective-permute-start(bf16[8,64,128]{2,1,0:T(8,128)(2,1)} %get-tuple-element.73), channel_id=1, source_target_pairs={{0,8},{2,10},{4,12},{6,14},{8,16},{10,18},{12,20},{14,22},{16,24},... | collective-permute-start | bytes 393224 | tf_op jit(solution)/shard_map/ppermute | solution.py:263
  273.6 19.7 %collective-permute-start.19 = (bf16[8,64,128]{2,1,0:T(8,128)(2,1)}, bf16[8,64,128]{2,1,0:T(8,128)(2,1)S(1)}, u32[]{:S(2)}, u32[]{:S(2)}) collective-permute-start(bf16[8,64,128]{2,1,0:T(8,128)(2,1)} %get-tuple-element.74), channel_id=1, source_target_pairs={{8,0},{10,2},{12,4},{14,6},{16,8},{18,10},{20,12},{22,14},{24,16},... | collective-permute-start | bytes 393224 | tf_op jit(solution)/shard_map/ppermute | solution.py:263
  276.0 17.3 %collective-permute-start.20 = (bf16[64,8,128]{2,1,0:T(8,128)(2,1)}, bf16[64,8,128]{2,1,0:T(8,128)(2,1)S(1)}, u32[]{:S(2)}, u32[]{:S(2)}) collective-permute-start(bf16[64,8,128]{2,1,0:T(8,128)(2,1)} %get-tuple-element.75), channel_id=1, source_target_pairs={{0,2},{2,4},{4,6},{8,10},{10,12},{12,14},{16,18},{18,20},{20,22},{... | collective-permute-start | bytes 393224 | tf_op jit(solution)/shard_map/ppermute | solution.py:263
  279.4 13.9 %copy-start.22 = (bf16[8,8,128]{2,1,0:T(8,128)(2,1)}, bf16[8,8,128]{2,1,0:T(8,128)(2,1)S(1)}, u32[]{:S(2)}) copy-start(bf16[8,8,128]{2,1,0:T(8,128)(2,1)S(1)} %collective-permute-done.22.rest_4_) | copy-start | bytes 49156
  279.5 13.9 %collective-permute-start.21 = (bf16[64,8,128]{2,1,0:T(8,128)(2,1)}, bf16[64,8,128]{2,1,0:T(8,128)(2,1)S(1)}, u32[]{:S(2)}, u32[]{:S(2)}) collective-permute-start(bf16[64,8,128]{2,1,0:T(8,128)(2,1)} %get-tuple-element.76), channel_id=1, source_target_pairs={{2,0},{4,2},{6,4},{10,8},{12,10},{14,12},{18,16},{20,18},{22,20},{... | collective-permute-start | bytes 393224 | tf_op jit(solution)/shard_map/ppermute | solution.py:263
  280.8 12.6 %copy-start.23 = (bf16[8,8,128]{2,1,0:T(8,128)(2,1)}, bf16[8,8,128]{2,1,0:T(8,128)(2,1)S(1)}, u32[]{:S(2)}) copy-start(bf16[8,8,128]{2,1,0:T(8,128)(2,1)S(1)} %collective-permute-done.23.rest_5_) | copy-start | bytes 49156
  280.8 4.9 %collective-permute-start.24 = (bf16[8,8,128]{2,1,0:T(8,128)(2,1)}, bf16[8,8,128]{2,1,0:T(8,128)(2,1)S(1)}, u32[]{:S(2)}, u32[]{:S(2)}) collective-permute-start(bf16[8,8,128]{2,1,0:T(8,128)(2,1)} %get-tuple-element.79), channel_id=1, source_target_pairs={{8,2},{10,4},{12,6},{16,10},{18,12},{20,14},{24,18},{26,20},{28,22... | collective-permute-start | bytes 49160 | tf_op jit(solution)/shard_map/ppermute | solution.py:263
  285.7 7.6 %collective-permute-start.25 = (bf16[8,8,128]{2,1,0:T(8,128)(2,1)}, bf16[8,8,128]{2,1,0:T(8,128)(2,1)S(1)}, u32[]{:S(2)}, u32[]{:S(2)}) collective-permute-start(bf16[8,8,128]{2,1,0:T(8,128)(2,1)} %get-tuple-element.80), channel_id=1, source_target_pairs={{10,0},{12,2},{14,4},{18,8},{20,10},{22,12},{26,16},{28,18},{30,20... | collective-permute-start | bytes 49160 | tf_op jit(solution)/shard_map/ppermute | solution.py:263
  325.1 25.8 %collective-permute-start.28 = (bf16[64,8,128]{2,1,0:T(8,128)(2,1)}, bf16[64,8,128]{2,1,0:T(8,128)(2,1)S(1)}, u32[]{:S(2)}, u32[]{:S(2)}) collective-permute-start(bf16[64,8,128]{2,1,0:T(8,128)(2,1)} %get-tuple-element.86), channel_id=1, source_target_pairs={{0,2},{2,4},{4,6},{8,10},{10,12},{12,14},{16,18},{18,20},{20,22},{... | collective-permute-start | bytes 393224 | tf_op jit(solution)/shard_map/ppermute | solution.py:263
  329.1 21.9 %collective-permute-start.29 = (bf16[64,8,128]{2,1,0:T(8,128)(2,1)}, bf16[64,8,128]{2,1,0:T(8,128)(2,1)S(1)}, u32[]{:S(2)}, u32[]{:S(2)}) collective-permute-start(bf16[64,8,128]{2,1,0:T(8,128)(2,1)} %get-tuple-element.87), channel_id=1, source_target_pairs={{2,0},{4,2},{6,4},{10,8},{12,10},{14,12},{18,16},{20,18},{22,20},{... | collective-permute-start | bytes 393224 | tf_op jit(solution)/shard_map/ppermute | solution.py:263
  330.4 9.8 %collective-permute-start.30 = (bf16[4,8,128]{2,1,0:T(8,128)(2,1)}, bf16[4,8,128]{2,1,0:T(8,128)(2,1)S(1)}, u32[]{:S(2)}, u32[]{:S(2)}) collective-permute-start(bf16[4,8,128]{2,1,0:T(8,128)(2,1)} %get-tuple-element.88), channel_id=1, source_target_pairs={{0,10},{2,12},{4,14},{8,18},{10,20},{12,22},{16,26},{18,28},{20,30... | collective-permute-start | bytes 24584 | tf_op jit(solution)/shard_map/ppermute | solution.py:263
  334.6 8.2 %collective-permute-start.31 = (bf16[4,8,128]{2,1,0:T(8,128)(2,1)}, bf16[4,8,128]{2,1,0:T(8,128)(2,1)S(1)}, u32[]{:S(2)}, u32[]{:S(2)}) collective-permute-start(bf16[4,8,128]{2,1,0:T(8,128)(2,1)} %get-tuple-element.89), channel_id=1, source_target_pairs={{2,8},{4,10},{6,12},{10,16},{12,18},{14,20},{18,24},{20,26},{22,28... | collective-permute-start | bytes 24584 | tf_op jit(solution)/shard_map/ppermute | solution.py:263
  335.9 8.8 %collective-permute-start.32 = (bf16[4,8,128]{2,1,0:T(8,128)(2,1)}, bf16[4,8,128]{2,1,0:T(8,128)(2,1)S(1)}, u32[]{:S(2)}, u32[]{:S(2)}) collective-permute-start(bf16[4,8,128]{2,1,0:T(8,128)(2,1)} %get-tuple-element.90), channel_id=1, source_target_pairs={{8,2},{10,4},{12,6},{16,10},{18,12},{20,14},{24,18},{26,20},{28,22... | collective-permute-start | bytes 24584 | tf_op jit(solution)/shard_map/ppermute | solution.py:263
  340.2 10.8 %copy-start.34 = (bf16[4,8,128]{2,1,0:T(8,128)(2,1)}, bf16[4,8,128]{2,1,0:T(8,128)(2,1)S(1)}, u32[]{:S(2)}) copy-start(bf16[4,8,128]{2,1,0:T(8,128)(2,1)S(1)} %collective-permute-done.30.rest_4_) | copy-start | bytes 24580
  340.2 10.7 %collective-permute-start.26 = (bf16[4,64,128]{2,1,0:T(8,128)(2,1)}, bf16[4,64,128]{2,1,0:T(8,128)(2,1)S(1)}, u32[]{:S(2)}, u32[]{:S(2)}) collective-permute-start(bf16[4,64,128]{2,1,0:T(8,128)(2,1)} %get-tuple-element.84), channel_id=1, source_target_pairs={{0,8},{2,10},{4,12},{6,14},{8,16},{10,18},{12,20},{14,22},{16,24},... | collective-permute-start | bytes 196616 | tf_op jit(solution)/shard_map/ppermute | solution.py:263
  342.8 8.1 %collective-permute-start.27 = (bf16[4,64,128]{2,1,0:T(8,128)(2,1)}, bf16[4,64,128]{2,1,0:T(8,128)(2,1)S(1)}, u32[]{:S(2)}, u32[]{:S(2)}) collective-permute-start(bf16[4,64,128]{2,1,0:T(8,128)(2,1)} %get-tuple-element.85), channel_id=1, source_target_pairs={{8,0},{10,2},{12,4},{14,6},{16,8},{18,10},{20,12},{22,14},{24,16},... | collective-permute-start | bytes 196616 | tf_op jit(solution)/shard_map/ppermute | solution.py:263
  344.8 6.1 %collective-permute-start.33 = (bf16[4,8,128]{2,1,0:T(8,128)(2,1)}, bf16[4,8,128]{2,1,0:T(8,128)(2,1)S(1)}, u32[]{:S(2)}, u32[]{:S(2)}) collective-permute-start(bf16[4,8,128]{2,1,0:T(8,128)(2,1)} %get-tuple-element.91), channel_id=1, source_target_pairs={{10,0},{12,2},{14,4},{18,8},{20,10},{22,12},{26,16},{28,18},{30,20... | collective-permute-start | bytes 24584 | tf_op jit(solution)/shard_map/ppermute | solution.py:263
  351.7 27.6 %copy-start.1 = (s32[32,512]{1,0:T(8,128)S(1)}, s32[32,512]{1,0:T(8,128)}, u32[]{:S(2)}) copy-start(s32[32,512]{1,0:T(8,128)} %param.9) | copy-start | bytes 196612
  (26 other events, 50.9 us)

commit v2 on v1

--- a/solution.py
+++ b/solution.py
@@ -1,4 +1,5 @@
 import functools
+import math
 
 import jax
 import jax.numpy as jnp
@@ -20,18 +21,14 @@
 
 
 def standardize(values):
-    centred = values - jnp.mean(values, -1, keepdims=True)
-    variance = jnp.mean(centred * centred, -1, keepdims=True)
-    inverse = lax.rsqrt(variance + epsilon)
+    count = values.shape[-1]
+    centred = values - jnp.sum(values, -1, keepdims=True) * (1.0 / count)
+    inverse = lax.rsqrt(jnp.sum(centred * centred, -1, keepdims=True) + epsilon * count)
     return centred * inverse, inverse
 
 
 def elu(values):
-    return jnp.where(values > 0, values, jnp.exp(jnp.minimum(values, 0.0)) - 1.0)
-
-
-def slope_of(values):
-    return jnp.where(values > 0, 1.0, jnp.exp(jnp.minimum(values, 0.0)))
+    return jnp.maximum(values, jnp.exp(jnp.minimum(values, 0.0)) - 1.0)
 
 
 def slope_from_elu(activated):
@@ -39,8 +36,8 @@
 
 
 def standardize_back(standard, inverse, upstream):
-    along = jnp.mean(upstream, -1, keepdims=True)
-    across = jnp.mean(upstream * standard, -1, keepdims=True)
+    along = jnp.sum(upstream, -1, keepdims=True) * (1.0 / upstream.shape[-1])
+    across = jnp.sum(upstream * standard, -1, keepdims=True)
     return inverse * (upstream - along - standard * across)
 
 
@@ -51,7 +48,7 @@
 
 
 def store_edges(values, refs, spacing, step, steps):
-    top, bottom, left, right, corner_a, corner_b, corner_c, corner_d = refs
+    top, bottom, left, right = refs
     columns = values.shape[2]
     low = lane_low((ROWS, EDGE, values.shape[3]))
     left[...] = jnp.where(low, values[0, :, :EDGE], values[1, :, :EDGE]).astype(BF16)
@@ -62,18 +59,14 @@
     @pl.when(step < taken)
     def _():
         top[...] = jnp.where(wide, values[0, :, : columns // 2], values[0, :, columns // 2 :]).astype(BF16)
-        corner_a[...] = values[0, :, :EDGE].astype(BF16)
-        corner_b[...] = values[0, :, columns - EDGE :].astype(BF16)
 
     @pl.when(step >= steps - taken)
     def _():
         bottom[...] = jnp.where(wide, values[1, :, : columns // 2], values[1, :, columns // 2 :]).astype(BF16)
-        corner_c[...] = values[1, :, :EDGE].astype(BF16)
-        corner_d[...] = values[1, :, columns - EDGE :].astype(BF16)
 
 
 def fill_padded(padded, centre, halos, spacing):
-    above, below, before, after, corner_a, corner_b, corner_c, corner_d = halos
+    above, below, before, after = halos
     rows, columns, lanes = centre.shape
     half = rows // 2
 
@@ -96,13 +89,13 @@
         return carry
 
     lax.fori_loop(0, half, sides, 0)
-    for halo, one, two, base in ((above, corner_a, corner_b, 0), (below, corner_c, corner_d, spacing + rows)):
+    for halo, base, place in ((above, 0, half), (below, spacing + rows, half + spacing)):
         for row in range(spacing):
             first, second = twice(halo[row].astype(F32))
             padded[base + row, PAD : PAD + columns // 2] = first
             padded[base + row, PAD + columns // 2 : PAD + columns] = second
-            padded[base + row, PAD - EDGE : PAD] = one[row]
-            padded[base + row, PAD + columns : PAD + columns + EDGE] = two[row]
+            padded[base + row, PAD - EDGE : PAD] = twice(before[place + row].astype(F32))[1]
+            padded[base + row, PAD + columns : PAD + columns + EDGE] = twice(after[place + row].astype(F32))[0]
 
 
 def convolve(padded, kernel, taps, spacing, step, half, columns):
@@ -117,8 +110,14 @@
     joined = jnp.concatenate(parts, axis=0).reshape(2 * ROWS * width, 2 * lanes)
     taps[...] = jnp.dot(joined, kernel[...], preferred_element_type=F32).reshape(2 * ROWS, width, 3 * lanes)
     total = taps[:, PAD : PAD + columns, lanes : 2 * lanes]
-    total = total + taps[:, PAD - spacing : PAD - spacing + columns, :lanes]
-    total = total + taps[:, PAD + spacing : PAD + spacing + columns, 2 * lanes :]
+    if spacing % EDGE:
+        outer = taps[:, PAD - EDGE : PAD + columns, :lanes]
+        start = PAD - EDGE + 2 * spacing
+        outer = outer + taps[:, start : start + columns + EDGE, 2 * lanes :]
+        total = total + outer[:, EDGE - spacing : EDGE - spacing + columns]
+    else:
+        total = total + taps[:, PAD - spacing : PAD - spacing + columns, :lanes]
+        total = total + taps[:, PAD + spacing : PAD + spacing + columns, 2 * lanes :]
     return total.reshape(2 * ROWS * columns, lanes)
 
 
@@ -134,9 +133,9 @@
 
 
 def middle_kernel(near, far, steps, centre, *rest):
-    halos, rest = rest[:8], rest[8:]
+    halos, rest = rest[:4], rest[4:]
     features, kernel, up, gain, down, stream_out, activated_out, squeezed, *rest = rest
-    edges, (padded, taps) = rest[:8], rest[8:]
+    edges, (padded, taps) = rest[:4], rest[4:]
     step = pl.program_id(0)
     half, columns = centre.shape[0] // 2, centre.shape[1]
 
@@ -154,7 +153,7 @@
 
 
 def head_kernel(near, steps, centre, *rest):
-    halos, rest = rest[:8], rest[8:]
+    halos, rest = rest[:4], rest[4:]
     stream_in, kernel, up, gain, head, bias, stream_out, activated_out, by_row, by_column, padded, taps = rest
     step = pl.program_id(0)
     half, columns = centre.shape[0] // 2, centre.shape[1]
@@ -178,15 +177,20 @@
 
 
 def loss_kernel(
-    spacing, steps, by_row, facing, targets, stream, activated, gain, head, group, up, grad_out, conv_out, *rest
+    spacing, steps, inner, pieces, by_row, *rest
 ):
-    edges, (turned,) = rest[:8], rest[8:]
+    facing, rest = rest[: sum(pieces)], rest[sum(pieces) :]
+    targets, stream, activated, gain, head, group, up, grad_out, conv_out, *rest = rest
+    edges, (turned,) = rest[:4], rest[4:]
     step = pl.program_id(0)
-    inner = facing.shape[1] // ROWS
 
     @pl.when(step % inner == 0)
     def _():
-        turned[...] = jnp.swapaxes(facing[...].astype(F32), 0, 1)
+        place = taken = 0
+        for count in pieces:
+            piece = sum(array[...].astype(F32) for array in facing[taken : taken + count])
+            turned[:, place : place + piece.shape[0]] = jnp.swapaxes(piece, 0, 1)
+            place, taken = place + piece.shape[0], taken + count
 
     start = (step % inner) * ROWS
     columns, lanes = by_row.shape[1:]
@@ -217,14 +221,15 @@
     lowered = lowered * slope_from_elu(strip(squeezed).astype(F32))
     entered = jnp.dot(lowered.astype(BF16), down[...], preferred_element_type=F32)
     standard, inverse = standardize(strip(stream).astype(F32))
-    entered = entered * slope_of(standard * gain[...])
-    return strip(upstream) + standardize_back(standard, inverse, entered * gain[...])
+    scale = gain[...]
+    entered = entered * (jnp.exp2(jnp.minimum(standard * (scale * math.log2(math.e)), 0.0)) * scale)
+    return strip(upstream) + standardize_back(standard, inverse, entered)
 
 
 def back_kernel(near, far, steps, centre, *rest):
-    halos, rest = rest[:8], rest[8:]
+    halos, rest = rest[:4], rest[4:]
     kernel, squeezed, down, stream, gain, upstream, activated, up, grad_out, conv_out, *rest = rest
-    edges, (padded, taps) = rest[:8], rest[8:]
+    edges, (padded, taps) = rest[:4], rest[4:]
     step = pl.program_id(0)
 
     @pl.when(step == 0)
@@ -241,7 +246,7 @@
 
 
 def final_kernel(near, centre, *rest):
-    halos, rest = rest[:8], rest[8:]
+    halos, rest = rest[:4], rest[4:]
     kernel, squeezed, down, stream, gain, upstream, grad_out, padded, taps = rest
     step = pl.program_id(0)
 
@@ -253,28 +258,18 @@
     grad_out[...] = grad.reshape(grad_out.shape)
 
 
-def shifted(values, row_move, col_move):
-    rows, cols = lax.axis_size("row"), lax.axis_size("col")
-    pairs = []
-    for row in range(rows):
-        for col in range(cols):
-            if 0 <= row + row_move < rows and 0 <= col + col_move < cols:
-                pairs.append((row * cols + col, (row + row_move) * cols + col + col_move))
-    return lax.ppermute(values, ("row", "col"), pairs)
+def shifted(values, axis, move):
+    count = lax.axis_size(axis)
+    return lax.ppermute(values, axis, [(i, i + move) for i in range(count) if 0 <= i + move < count])
 
 
 def exchange(edges):
-    top, bottom, left, right, corner_a, corner_b, corner_c, corner_d = edges
-    return (
-        shifted(bottom, 1, 0),
-        shifted(top, -1, 0),
-        shifted(right, 0, 1),
-        shifted(left, 0, -1),
-        shifted(corner_d, 1, 1),
-        shifted(corner_c, 1, -1),
-        shifted(corner_b, -1, 1),
-        shifted(corner_a, -1, -1),
-    )
+    top, bottom, left, right = edges
+    above = shifted(bottom, "row", 1)
+    below = shifted(top, "row", -1)
+    before = jnp.concatenate([right, above[:, -EDGE:], below[:, -EDGE:]], axis=0)
+    after = jnp.concatenate([left, above[:, :EDGE], below[:, :EDGE]], axis=0)
+    return above, below, shifted(before, "col", 1), shifted(after, "col", -1)
 
 
 def facing_tile(tile):
@@ -305,12 +300,28 @@
 
 
 def facing_logits(by_column):
-    if lax.axis_size("row") == lax.axis_size("col"):
-        return facing_tile(by_column)
+    rows, cols = lax.axis_size("row"), lax.axis_size("col")
+    if rows == cols and rows % 2 == 0:
+        cut = by_column.shape[0] * 5 // 128 * 16
+        straight, around = by_column[:cut], by_column[cut:]
+        places = [(row, col) for row in range(rows) for col in range(cols)]
+        part = rows // 2
+        far = [(row, col) for row, col in places if row // part != col // part]
+        close = [(row, col) for row, col in places if row // part == col // part]
+        both = ("row", "col")
+        number = lambda row, col: row * cols + col
+        other = lambda row: (row + part) % rows
+        hop = lax.ppermute(around, both, [(number(row, col), number(other(row), col)) for row, col in far])
+        straight = lax.ppermute(straight, both, [(number(row, col), number(col, row)) for row, col in places])
+        near = lax.ppermute(around, both, [(number(row, col), number(col, row)) for row, col in close])
+        hop = lax.ppermute(hop, both, [(number(other(row), col), number(col, row)) for row, col in far])
+        return [[straight], [hop, near]]
+    if rows == cols:
+        return [[facing_tile(by_column)]]
     bins = by_column.shape[2] // 2
     tile = facing_tile(jnp.concatenate([by_column[..., :bins], by_column[..., bins:]], axis=1))
     half = tile.shape[1] // 2
-    return jnp.concatenate([tile[:, :half], tile[:, half:]], axis=2)
+    return [[jnp.concatenate([tile[:, :half], tile[:, half:]], axis=2)]]
 
 
 def dilated_weights(kernel):
@@ -347,7 +358,7 @@
     lanes = 2 * narrow
     near, far = 4, 8
 
-    gains = [norm_gain[index : index + 1] for index in range(3)]
+    gains = [norm_gain[index : index + 1] * math.sqrt(channels) for index in range(3)]
     downs = [doubled_columns(w_down[index]) for index in range(2)]
     downs_back = [padded_rows(w_down[index].T) for index in range(2)]
     ups = [padded_rows(w_up[index]) for index in range(2)]
@@ -379,10 +390,6 @@
             ((spacing, columns // 2, lanes), last),
             ((half, EDGE, lanes), each),
             ((half, EDGE, lanes), each),
-            ((spacing, EDGE, lanes), first),
-            ((spacing, EDGE, lanes), first),
-            ((spacing, EDGE, lanes), last),
-            ((spacing, EDGE, lanes), last),
         ]
         shapes = [jax.ShapeDtypeStruct(shape, BF16) for shape, index in entries]
         specs = [pl.BlockSpec((ROWS,) + shape[1:], index) for shape, index in entries]
@@ -431,6 +438,8 @@
         cost(0, 4),
         "entry",
     )
+    own_labels = lax.all_to_all(labels, "col", split_axis=1, concat_axis=0, tiled=True)
+    squeezed_1, own_labels = lax.optimization_barrier((squeezed_1, own_labels))
     halos = exchange(sent)
 
     def tile(array):
@@ -450,6 +459,9 @@
     )
     halos = exchange(sent)
 
+    facing_labels = facing_tile(own_labels)
+    squeezed_2, facing_labels = lax.optimization_barrier((squeezed_2, facing_labels))
+    facing_labels = facing_labels.T
     centre = tile(squeezed_2)
     by_row_spec = pl.BlockSpec((ROWS, columns, 2 * bins), lambda step: (step, 0, 0))
     stream_2, activated_2, by_row, by_column = call(
@@ -475,8 +487,6 @@
     )
     facing = facing_logits(by_column.reshape(rows, columns // 2, 2 * bins))
 
-    own_labels = lax.all_to_all(labels, "col", split_axis=1, concat_axis=0, tiled=True)
-    facing_labels = facing_tile(own_labels).T
     numbers = jnp.arange(bins, dtype=jnp.int32)
 
     def onehot(values):
@@ -491,12 +501,14 @@
     ).astype(BF16)
 
     inner = 16 // ROWS
+    mirrored_logits = [array for piece in facing for array in piece]
     grad_2, conv_grad_2, *sent = call(
-        functools.partial(loss_kernel, far, steps),
-        (by_row, facing, targets, stream_2, activated_2, gains[2], head_back, group, ups_back[1]),
+        functools.partial(loss_kernel, far, steps, inner, tuple(len(piece) for piece in facing)),
+        (by_row, *mirrored_logits, targets, stream_2, activated_2, gains[2], head_back, group, ups_back[1]),
         [
             by_row_spec,
-            pl.BlockSpec((columns, ROWS * inner, 2 * bins), lambda step: (0, step // inner, 0)),
+            *(pl.BlockSpec((array.shape[0], ROWS * inner, 2 * bins), lambda step: (0, step // inner, 0))
+              for array in mirrored_logits),
             by_row_spec,
             bf_spec,
             strip_spec(lanes),

time: 383 us -> 318 us (0.83)
  waiting for transfers between devices: 107 us -> 43.3 us
  other arithmetic: 11.8 us -> 20.7 us
  starting transfers between devices: 89.4 us -> 80.9 us
    all_to_all x1, waiting for transfers between devices: 87.9 us -> 0.01 us  [shards(): lax.all_to_all(labels, 'col', split_axis=1, concat_axis=0, tiled=True)]
    ppermute x32 -> x20, waiting for transfers between devices: 15.7 us -> 40.3 us  [the longest x1 16 us: facing_logits(): lax.ppermute(around, both, [(number(row, col), number(col, row)) for row,...]
    concatenate x0 -> x8, other arithmetic: none -> 7.55 us  [the longest x4 3.84 us: exchange(): after = jnp.concatenate([left, above[:, :EDGE], below[:, :EDGE]], axis=0)]
    ppermute x32 -> x20, starting transfers between devices: 81.2 us -> 74.4 us  [the longest x16 62.1 us: shifted(): lax.ppermute(values, axis, [(i, i + move) for i in range(count) if 0 <= i...]
  transfers between devices with their start and end apart: 35 -> 22, of which waited for: 8 -> 10; matrix products, arithmetic and copies ran while one was open for 5% -> 8% of each run, Pallas kernels for 0% -> 0%
where the time goes in v2:
time: 318 us; the launch traced here: 314 us
  Pallas kernels  152 us (48%)
  starting transfers between devices  80.9 us (25%)
  waiting for transfers between devices  43.3 us (14%)
  other arithmetic  20.7 us (7%)
  local copies, waits for them, and re-layouts  16.9 us (5%)
    pallas_call x6, Pallas kernels, call(): pl.pallas_call(body, grid=(steps,), in_specs=specs, out_specs=out_specs,...  152 us
    ppermute x16, starting transfers between devices, shifted(): lax.ppermute(values, axis, [(i, i + move) for i in range(count) if 0 <= i...  62.1 us
    ppermute x1, waiting for transfers between devices, facing_logits(): lax.ppermute(around, both, [(number(row, col), number(col, row)) for row,...  16 us
    ppermute x16, waiting for transfers between devices, shifted(): lax.ppermute(values, axis, [(i, i + move) for i in range(count) if 0 <= i...  13.8 us
    ppermute x1, waiting for transfers between devices, facing_logits(): lax.ppermute(around, both, [(number(row, col), number(other(row), col)) f...  10.5 us
  transfers between devices with their start and end apart: 22, of which 10 were waited for; matrix products, arithmetic and copies ran while one was open for 8% of the time, Pallas kernels for 0%

profile of v2, /device:TPU:1, one launch (start us, length us, event | category | flops | bytes accessed | tf_op | source)
XLA Modules:
  0.0 314.0 jit_solution(11679568986613081579)
XLA Ops:
  1.5 1.4 slice_multiply_fusion
  2.9 14.3 %entry.1 = (bf16[2,64,128,128]{3,2,1,0:T(8,128)(2,1)}, bf16[4,64,128]{2,1,0:T(8,128)(2,1)}, bf16[4,64,128]{2,1,0:T(8,128)(2,1)}, bf16[64,8,128]{2,1,0:T(8,128)(2,1)}, bf16[64,8,128]{2,1,0:T(8,128)(2,1)}) custom-call(bf16[2,64,128,128]{3,2,1,0:T(8,128)(2,1)} %bitcast.75, f32[1,128]{1,0:T(1,128)} %get-tuple-element.100.gain.rest_8_, bf16[128,128]{1,0:T(8,128)(2,1)} %copy.53.down), custom_call_target="tpu_custom_call" | custom-call | flops 536870912 | bytes 8388608 | tf_op jit(solution)/shard_map/entry/pallas_call | solution.py:414
  17.2 4.5 %collective-permute-start = (bf16[4,64,128]{2,1,0:T(8,128)(2,1)}, bf16[4,64,128]{2,1,0:T(8,128)(2,1)S(1)}, u32[]{:S(2)}, u32[]{:S(2)}) collective-permute-start(bf16[4,64,128]{2,1,0:T(8,128)(2,1)} %get-tuple-element.39), channel_id=1, source_target_pairs={{0,8},{8,16},{16,24},{1,9},{9,17},{17,25},{2,10},{10,18},{18,26},{... | collective-permute-start | bytes 196616 | tf_op jit(solution)/shard_map/ppermute | solution.py:263
  21.7 1.9 collective-permute-start.1
  24.3 4.6 %all-to-all-start = ((s32[32,4,128]{2,0,1:T(8,128)}), s32[32,4,128]{2,0,1:T(8,128)S(1)}, u32[]{:S(2)}, u32[]{:S(2)}) async-start(s32[32,4,128]{2,0,1:T(8,128)} %copy_bitcast_fusion.4), calls=%async_computation | async-start | bytes 131072 | tf_op jit(solution)/shard_map/all_to_all | solution.py:441
  29.0 0.9 pad_maximum_fusion.6
  29.9 1.3 collective-permute-start.3
  31.2 0.9 pad_maximum_fusion.5
  32.2 4.0 %collective-permute-start.2 = (bf16[72,8,128]{2,1,0:T(8,128)(2,1)S(1)}, bf16[72,8,128]{2,1,0:T(8,128)(2,1)S(1)}, u32[]{:S(2)}, u32[]{:S(2)}) collective-permute-start(bf16[72,8,128]{2,1,0:T(8,128)(2,1)S(1)} %pad_maximum_fusion.5), channel_id=1, source_target_pairs={{0,2},{2,4},{4,6},{1,3},{3,5},{5,7},{8,10},{10,12},{12,14},{9,11},... | collective-permute-start | bytes 442376 | tf_op jit(solution)/shard_map/ppermute | solution.py:263
  39.6 28.0 %middle.1 = (f32[2,64,128,128]{3,2,1,0:T(8,128)}, bf16[2,64,128,128]{3,2,1,0:T(8,128)(2,1)}, bf16[2,64,128,128]{3,2,1,0:T(8,128)(2,1)}, bf16[8,64,128]{2,1,0:T(8...) custom-call(bf16[128,128,128]{2,1,0:T(8,128)(2,1)} %bitcast.78, ...), custom_call_target="tpu_custom_call" | custom-call | flops 1744830464 | bytes 25165824 | tf_op jit(solution)/shard_map/middle/pallas_call | solution.py:414
  67.6 4.4 %collective-permute-start.5 = (bf16[8,64,128]{2,1,0:T(8,128)(2,1)}, bf16[8,64,128]{2,1,0:T(8,128)(2,1)S(1)}, u32[]{:S(2)}, u32[]{:S(2)}) collective-permute-start(bf16[8,64,128]{2,1,0:T(8,128)(2,1)} %get-tuple-element.46), channel_id=1, source_target_pairs={{0,8},{8,16},{16,24},{1,9},{9,17},{17,25},{2,10},{10,18},{18,26},{... | collective-permute-start | bytes 393224 | tf_op jit(solution)/shard_map/ppermute | solution.py:263
  72.1 1.9 collective-permute-start.6
  74.2 4.4 %collective-permute-done.6.rest_1_ = bf16[8,64,128]{2,1,0:T(8,128)(2,1)S(1)} collective-permute-done((bf16[8,64,128]{2,1,0:T(8,128)(2,1)}, bf16[8,64,128]{2,1,0:T(8,128)(2,1)S(1)}, u32[]{:S(2)}, u32[]{:S(2)}) %collective-permute-start.6) | collective-permute-done | bytes 131104 | tf_op jit(solution)/shard_map/ppermute | solution.py:263
  78.6 1.0 pad_maximum_fusion.2
  79.6 1.3 collective-permute-start.8
  80.9 0.9 pad_maximum_fusion.1
  81.8 4.7 %collective-permute-start.7 = (bf16[80,8,128]{2,1,0:T(8,128)(2,1)S(1)}, bf16[80,8,128]{2,1,0:T(8,128)(2,1)S(1)}, u32[]{:S(2)}, u32[]{:S(2)}) collective-permute-start(bf16[80,8,128]{2,1,0:T(8,128)(2,1)S(1)} %pad_maximum_fusion.1), channel_id=1, source_target_pairs={{0,2},{2,4},{4,6},{1,3},{3,5},{5,7},{8,10},{10,12},{12,14},{9,11},... | collective-permute-start | bytes 491528 | tf_op jit(solution)/shard_map/ppermute | solution.py:263
  88.7 1.9 collective-permute-start.4
  91.3 3.0 collective-permute-done.4
  95.0 29.1 %head.1 = (f32[2,64,128,128]{3,2,1,0:T(8,128)}, bf16[2,64,128,128]{3,2,1,0:T(8,128)(2,1)}, bf16[64,128,128]{2,1,0:T(8,128)(2,1)}, bf16[2,64,64,128]{3,2,1,0:T(8,128)(2,1)}) custom-call(bf16[128,128,128]{2,1,0:T(8,128)(2,1)} %bitcast.79, bf16[8,64,128]{2,1,0:T(8,128)(2,1)} %copy-done.6, bf16[8,64,128]{2,1,0:T(8,128)(2,1)} %copy-done.7, ...), custom_call_target="tpu_custom_call" | custom-call | flops 1744830464 | bytes 29360128 | tf_op jit(solution)/shard_map/head/pallas_call | solution.py:414
  124.1 2.1 slice.139
  126.2 1.3 collective-permute-start.10
  127.6 1.4 slice.138
  129.0 1.9 collective-permute-start.9
  132.3 3.6 %collective-permute-start.12 = (bf16[48,64,128]{2,1,0:T(8,128)(2,1)}, bf16[48,64,128]{2,1,0:T(8,128)(2,1)}, u32[]{:S(2)}, u32[]{:S(2)}) collective-permute-start(bf16[48,64,128]{2,1,0:T(8,128)(2,1)} %slice.139), channel_id=1, source_target_pairs={{0,0},{2,8},{8,2},{10,10},{20,20},{22,28},{28,22},{30,30},{1,1},{3... | collective-permute-start | bytes 2359304 | tf_op jit(solution)/shard_map/ppermute | solution.py:316
  135.9 10.5 %collective-permute-done.10 = bf16[48,64,128]{2,1,0:T(8,128)(2,1)} collective-permute-done((bf16[48,64,128]{2,1,0:T(8,128)(2,1)}, bf16[48,64,128]{2,1,0:T(8,128)(2,1)}, u32[]{:S(2)}, u32[]{:S(2)}) %collective-permute-start.10) | collective-permute-done | bytes 786464 | tf_op jit(solution)/shard_map/ppermute | solution.py:314
  146.4 5.5 %collective-permute-start.11 = (bf16[48,64,128]{2,1,0:T(8,128)(2,1)}, bf16[48,64,128]{2,1,0:T(8,128)(2,1)}, u32[]{:S(2)}, u32[]{:S(2)}) collective-permute-start(bf16[48,64,128]{2,1,0:T(8,128)(2,1)} %collective-permute-done.10), channel_id=1, source_target_pairs={{20,16},{22,24},{28,18},{30,26},{0,4},{2,12},{8,6},{10,14},{21,17}... | collective-permute-start | bytes 2359304 | tf_op jit(solution)/shard_map/ppermute | solution.py:317
  152.1 2.8 multiply_convert_fusion
  154.9 2.8 multiply_convert_fusion.1
  157.7 2.5 pad_maximum_fusion.rest_3_
  160.2 16.0 %collective-permute-done.12.rest_2_ = bf16[48,64,128]{2,1,0:T(8,128)(2,1)} collective-permute-done((bf16[48,64,128]{2,1,0:T(8,128)(2,1)}, bf16[48,64,128]{2,1,0:T(8,128)(2,1)}, u32[]{:S(2)}, u32[]{:S(2)}) %collective-permute-start.12) | collective-permute-done | bytes 786464 | tf_op jit(solution)/shard_map/ppermute | solution.py:316
  176.2 1.1 copy-done.2
  177.4 22.3 %loss.1 = (f32[2,64,128,128]{3,2,1,0:T(8,128)}, bf16[2,64,128,128]{3,2,1,0:T(8,128)(2,1)}, bf16[8,64,128]{2,1,0:T(8,128)(2,1)}, bf16[8,64,128]{2,1,0:T(8,128)(2,...) custom-call(bf16[64,128,128]{2,1,0:T(8,128)(2,1)} %get-tuple-element.51.by_row, ...), custom_call_target="tpu_custom_call" | custom-call | flops 536870912 | bytes 37748736 | tf_op jit(solution)/shard_map/loss/pallas_call | solution.py:414
  199.7 20.1 %collective-permute-start.13 = (bf16[8,64,128]{2,1,0:T(8,128)(2,1)}, bf16[8,64,128]{2,1,0:T(8,128)(2,1)S(1)}, u32[]{:S(2)}, u32[]{:S(2)}) collective-permute-start(bf16[8,64,128]{2,1,0:T(8,128)(2,1)} %get-tuple-element.57), channel_id=1, source_target_pairs={{0,8},{8,16},{16,24},{1,9},{9,17},{17,25},{2,10},{10,18},{18,26},{... | collective-permute-start | bytes 393224 | tf_op jit(solution)/shard_map/ppermute | solution.py:263
  219.8 1.9 collective-permute-start.14
  222.1 4.3 %collective-permute-done.14.rest_1_ = bf16[8,64,128]{2,1,0:T(8,128)(2,1)S(1)} collective-permute-done((bf16[8,64,128]{2,1,0:T(8,128)(2,1)}, bf16[8,64,128]{2,1,0:T(8,128)(2,1)S(1)}, u32[]{:S(2)}, u32[]{:S(2)}) %collective-permute-start.14) | collective-permute-done | bytes 131104 | tf_op jit(solution)/shard_map/ppermute | solution.py:263
  226.3 1.0 pad_maximum_fusion.4
  227.3 1.3 collective-permute-start.16
  228.6 0.9 pad_maximum_fusion.3
  229.6 4.0 %collective-permute-start.15 = (bf16[80,8,128]{2,1,0:T(8,128)(2,1)S(1)}, bf16[80,8,128]{2,1,0:T(8,128)(2,1)S(1)}, u32[]{:S(2)}, u32[]{:S(2)}) collective-permute-start(bf16[80,8,128]{2,1,0:T(8,128)(2,1)S(1)} %pad_maximum_fusion.3), channel_id=1, source_target_pairs={{0,2},{2,4},{4,6},{1,3},{3,5},{5,7},{8,10},{10,12},{12,14},{9,11},... | collective-permute-start | bytes 491528 | tf_op jit(solution)/shard_map/ppermute | solution.py:263
  236.7 31.0 %back.1 = (f32[2,64,128,128]{3,2,1,0:T(8,128)}, bf16[2,64,128,128]{3,2,1,0:T(8,128)(2,1)}, bf16[4,64,128]{2,1,0:T(8,128)(2,1)}, bf16[4,64,128]{2,1,0:T(8,128)(2,...) custom-call(bf16[128,128,128]{2,1,0:T(8,128)(2,1)} %bitcast.80, bf16[8,64,128]{2,1,0:T(8,128)(2,1)} %copy-done.4, ...), custom_call_target="tpu_custom_call" | custom-call | flops 1744830464 | bytes 41943040 | tf_op jit(solution)/shard_map/back/pallas_call | solution.py:414
  267.7 2.8 collective-permute-start.17
  270.5 1.9 collective-permute-start.18
  272.4 3.8 %collective-permute-done.18.rest_1_ = bf16[4,64,128]{2,1,0:T(8,128)(2,1)S(1)} collective-permute-done((bf16[4,64,128]{2,1,0:T(8,128)(2,1)}, bf16[4,64,128]{2,1,0:T(8,128)(2,1)S(1)}, u32[]{:S(2)}, u32[]{:S(2)}) %collective-permute-start.18) | collective-permute-done | bytes 65568 | tf_op jit(solution)/shard_map/ppermute | solution.py:263
  276.3 0.9 pad_maximum_fusion.8
  277.2 1.3 collective-permute-start.20
  279.4 4.7 %collective-permute-start.19 = (bf16[72,8,128]{2,1,0:T(8,128)(2,1)S(1)}, bf16[72,8,128]{2,1,0:T(8,128)(2,1)S(1)}, u32[]{:S(2)}, u32[]{:S(2)}) collective-permute-start(bf16[72,8,128]{2,1,0:T(8,128)(2,1)S(1)} %pad_maximum_fusion.7), channel_id=1, source_target_pairs={{0,2},{2,4},{4,6},{1,3},{3,5},{5,7},{8,10},{10,12},{12,14},{9,11},... | collective-permute-start | bytes 442376 | tf_op jit(solution)/shard_map/ppermute | solution.py:263
  286.9 27.0 %final.1 = f32[2,64,128,128]{3,2,1,0:T(8,128)} custom-call(bf16[128,128,128]{2,1,0:T(8,128)(2,1)} %bitcast.81, bf16[4,64,128]{2,1,0:T(8,128)(2,1)} %copy-done.18, bf16[4,64,128]{2,1,0:T(8,128)(2,1)} %copy-done.19, bf16[72,8,128]{2,1,0:T(8,128)(2,1)} %copy-done.13, bf16[72,8,128]{2,1,0:T(8,128)(2,1)} %copy-done.12, bf16[256,384]{1,0:T(8,128)(2,1)} %pad.36.rest_4_, ...), custom_call_target="tpu_custom_call" | custom-call | flops 1744830464 | bytes 33554432 | tf_op jit(solution)/shard_map/final/pallas_call | solution.py:414
  (110 shorter events, 18.1 us)
Async XLA Ops:
  0.0 23.7 %copy-start = (s32[32,512]{1,0:T(8,128)S(1)}, s32[32,512]{1,0:T(8,128)}, u32[]{:S(2)}) copy-start(s32[32,512]{1,0:T(8,128)} %param.9) | copy-start | bytes 196612
  0.0 28.9 %copy-start.3 = (bf16[2,3,3,64,64]{4,3,2,1,0:T(8,128)(2,1)S(1)}, bf16[2,3,3,64,64]{4,3,2,1,0:T(8,128)(2,1)}, u32[]{:S(2)}) copy-start(bf16[2,3,3,64,64]{4,3,2,1,0:T(8,128)(2,1)} %param.12) | copy-start | bytes 442372
  0.0 28.9 %copy-start.21 = (bf16[2,64,128]{2,1,0:T(8,128)(2,1)S(1)}, bf16[2,64,128]{2,1,0:T(8,128)(2,1)}, u32[]{:S(2)}) copy-start(bf16[2,64,128]{2,1,0:T(8,128)(2,1)} %param.13) | copy-start | bytes 98308
  17.2 11.7 %collective-permute-start = (bf16[4,64,128]{2,1,0:T(8,128)(2,1)}, bf16[4,64,128]{2,1,0:T(8,128)(2,1)S(1)}, u32[]{:S(2)}, u32[]{:S(2)}) collective-permute-start(bf16[4,64,128]{2,1,0:T(8,128)(2,1)} %get-tuple-element.39), channel_id=1, source_target_pairs={{0,8},{8,16},{16,24},{1,9},{9,17},{17,25},{2,10},{10,18},{18,26},{... | collective-permute-start | bytes 196616 | tf_op jit(solution)/shard_map/ppermute | solution.py:263
  21.7 7.2 %collective-permute-start.1 = (bf16[4,64,128]{2,1,0:T(8,128)(2,1)}, bf16[4,64,128]{2,1,0:T(8,128)(2,1)S(1)}, u32[]{:S(2)}, u32[]{:S(2)}) collective-permute-start(bf16[4,64,128]{2,1,0:T(8,128)(2,1)} %get-tuple-element.40), channel_id=1, source_target_pairs={{8,0},{16,8},{24,16},{9,1},{17,9},{25,17},{10,2},{18,10},{26,18},{... | collective-permute-start | bytes 196616 | tf_op jit(solution)/shard_map/ppermute | solution.py:263
  24.3 14.3 %all-to-all-start = ((s32[32,4,128]{2,0,1:T(8,128)}), s32[32,4,128]{2,0,1:T(8,128)S(1)}, u32[]{:S(2)}, u32[]{:S(2)}) async-start(s32[32,4,128]{2,0,1:T(8,128)} %copy_bitcast_fusion.4), calls=%async_computation | async-start | bytes 131072 | tf_op jit(solution)/shard_map/all_to_all | solution.py:441
  28.9 10.0 %copy-start.16 = (bf16[4,64,128]{2,1,0:T(8,128)(2,1)}, bf16[4,64,128]{2,1,0:T(8,128)(2,1)S(1)}, u32[]{:S(2)}) copy-start(bf16[4,64,128]{2,1,0:T(8,128)(2,1)S(1)} %collective-permute-done.rest_0_) | copy-start | bytes 196612
  29.0 10.0 %copy-start.17 = (bf16[4,64,128]{2,1,0:T(8,128)(2,1)}, bf16[4,64,128]{2,1,0:T(8,128)(2,1)S(1)}, u32[]{:S(2)}) copy-start(bf16[4,64,128]{2,1,0:T(8,128)(2,1)S(1)} %collective-permute-done.1.rest_1_) | copy-start | bytes 196612
  29.9 8.6 %collective-permute-start.3 = (bf16[72,8,128]{2,1,0:T(8,128)(2,1)S(1)}, bf16[72,8,128]{2,1,0:T(8,128)(2,1)S(1)}, u32[]{:S(2)}, u32[]{:S(2)}) collective-permute-start(bf16[72,8,128]{2,1,0:T(8,128)(2,1)S(1)} %pad_maximum_fusion.6), channel_id=1, source_target_pairs={{2,0},{4,2},{6,4},{3,1},{5,3},{7,5},{10,8},{12,10},{14,12},{11,9},... | collective-permute-start | bytes 442376 | tf_op jit(solution)/shard_map/ppermute | solution.py:263
  32.2 6.8 %collective-permute-start.2 = (bf16[72,8,128]{2,1,0:T(8,128)(2,1)S(1)}, bf16[72,8,128]{2,1,0:T(8,128)(2,1)S(1)}, u32[]{:S(2)}, u32[]{:S(2)}) collective-permute-start(bf16[72,8,128]{2,1,0:T(8,128)(2,1)S(1)} %pad_maximum_fusion.5), channel_id=1, source_target_pairs={{0,2},{2,4},{4,6},{1,3},{3,5},{5,7},{8,10},{10,12},{12,14},{9,11},... | collective-permute-start | bytes 442376 | tf_op jit(solution)/shard_map/ppermute | solution.py:263
  38.6 0.7 copy-start.14
  38.9 0.7 copy-start.15
  39.6 32.4 %copy-start.20 = (bf16[128,64]{0,1:T(8,128)(2,1)S(1)}, bf16[128,64]{0,1:T(8,128)(2,1)}, u32[]{:S(2)}) copy-start(bf16[128,64]{0,1:T(8,128)(2,1)} %param.14) | copy-start | bytes 49156
  39.6 51.0 %copy-start.22 = (f32[64]{0:T(128)S(1)}, f32[64]{0:T(128)}, u32[]{:S(2)}) copy-start(f32[64]{0:T(128)} %param.15) | copy-start | bytes 772
  67.6 6.7 %collective-permute-start.5 = (bf16[8,64,128]{2,1,0:T(8,128)(2,1)}, bf16[8,64,128]{2,1,0:T(8,128)(2,1)S(1)}, u32[]{:S(2)}, u32[]{:S(2)}) collective-permute-start(bf16[8,64,128]{2,1,0:T(8,128)(2,1)} %get-tuple-element.46), channel_id=1, source_target_pairs={{0,8},{8,16},{16,24},{1,9},{9,17},{17,25},{2,10},{10,18},{18,26},{... | collective-permute-start | bytes 393224 | tf_op jit(solution)/shard_map/ppermute | solution.py:263
  72.1 6.5 %collective-permute-start.6 = (bf16[8,64,128]{2,1,0:T(8,128)(2,1)}, bf16[8,64,128]{2,1,0:T(8,128)(2,1)S(1)}, u32[]{:S(2)}, u32[]{:S(2)}) collective-permute-start(bf16[8,64,128]{2,1,0:T(8,128)(2,1)} %get-tuple-element.47), channel_id=1, source_target_pairs={{8,0},{16,8},{24,16},{9,1},{17,9},{25,17},{10,2},{18,10},{26,18},{... | collective-permute-start | bytes 393224 | tf_op jit(solution)/shard_map/ppermute | solution.py:263
  74.2 20.1 %copy-start.6 = (bf16[8,64,128]{2,1,0:T(8,128)(2,1)}, bf16[8,64,128]{2,1,0:T(8,128)(2,1)S(1)}, u32[]{:S(2)}) copy-start(bf16[8,64,128]{2,1,0:T(8,128)(2,1)S(1)} %collective-permute-done.5.rest_0_) | copy-start | bytes 393220
  78.6 15.7 %copy-start.7 = (bf16[8,64,128]{2,1,0:T(8,128)(2,1)}, bf16[8,64,128]{2,1,0:T(8,128)(2,1)S(1)}, u32[]{:S(2)}) copy-start(bf16[8,64,128]{2,1,0:T(8,128)(2,1)S(1)} %collective-permute-done.6.rest_1_) | copy-start | bytes 393220
  79.6 14.7 %collective-permute-start.8 = (bf16[80,8,128]{2,1,0:T(8,128)(2,1)S(1)}, bf16[80,8,128]{2,1,0:T(8,128)(2,1)S(1)}, u32[]{:S(2)}, u32[]{:S(2)}) collective-permute-start(bf16[80,8,128]{2,1,0:T(8,128)(2,1)S(1)} %pad_maximum_fusion.2), channel_id=1, source_target_pairs={{2,0},{4,2},{6,4},{3,1},{5,3},{7,5},{10,8},{12,10},{14,12},{11,9},... | collective-permute-start | bytes 491528 | tf_op jit(solution)/shard_map/ppermute | solution.py:263
  81.8 12.5 %collective-permute-start.7 = (bf16[80,8,128]{2,1,0:T(8,128)(2,1)S(1)}, bf16[80,8,128]{2,1,0:T(8,128)(2,1)S(1)}, u32[]{:S(2)}, u32[]{:S(2)}) collective-permute-start(bf16[80,8,128]{2,1,0:T(8,128)(2,1)S(1)} %pad_maximum_fusion.1), channel_id=1, source_target_pairs={{0,2},{2,4},{4,6},{1,3},{3,5},{5,7},{8,10},{10,12},{12,14},{9,11},... | collective-permute-start | bytes 491528 | tf_op jit(solution)/shard_map/ppermute | solution.py:263
  88.7 5.6 %collective-permute-start.4 = (s32[128,128]{1,0:T(8,128)S(1)}, s32[128,128]{1,0:T(8,128)S(1)}, u32[]{:S(2)}, u32[]{:S(2)}) collective-permute-start(s32[128,128]{1,0:T(8,128)S(1)} %bitcast.92), channel_id=1, source_target_pairs={{0,0},{2,8},{4,16},{6,24},{8,2},{10,10},{12,18},{14,26},{16,4},{18... | collective-permute-start | bytes 196616 | tf_op jit(solution)/shard_map/ppermute | solution.py:279
  94.3 0.7 copy-start.8
  94.3 0.7 copy-start.9
  126.2 20.2 %collective-permute-start.10 = (bf16[48,64,128]{2,1,0:T(8,128)(2,1)}, bf16[48,64,128]{2,1,0:T(8,128)(2,1)}, u32[]{:S(2)}, u32[]{:S(2)}) collective-permute-start(bf16[48,64,128]{2,1,0:T(8,128)(2,1)} %slice.139), channel_id=1, source_target_pairs={{4,20},{6,22},{12,28},{14,30},{16,0},{18,2},{24,8},{26,10},{5,21},... | collective-permute-start | bytes 2359304 | tf_op jit(solution)/shard_map/ppermute | solution.py:314
  129.0 47.2 %collective-permute-start.9 = (bf16[80,64,128]{2,1,0:T(8,128)(2,1)S(1)}, bf16[80,64,128]{2,1,0:T(8,128)(2,1)S(1)}, u32[]{:S(2)}, u32[]{:S(2)}) collective-permute-start(bf16[80,64,128]{2,1,0:T(8,128)(2,1)S(1)} %slice.138), channel_id=1, source_target_pairs={{0,0},{2,8},{4,16},{6,24},{8,2},{10,10},{12,18},{14,26},{16,4},{18... | collective-permute-start | bytes 3932168 | tf_op jit(solution)/shard_map/ppermute | solution.py:315
  132.3 43.9 %collective-permute-start.12 = (bf16[48,64,128]{2,1,0:T(8,128)(2,1)}, bf16[48,64,128]{2,1,0:T(8,128)(2,1)}, u32[]{:S(2)}, u32[]{:S(2)}) collective-permute-start(bf16[48,64,128]{2,1,0:T(8,128)(2,1)} %slice.139), channel_id=1, source_target_pairs={{0,0},{2,8},{8,2},{10,10},{20,20},{22,28},{28,22},{30,30},{1,1},{3... | collective-permute-start | bytes 2359304 | tf_op jit(solution)/shard_map/ppermute | solution.py:316
  146.4 29.8 %collective-permute-start.11 = (bf16[48,64,128]{2,1,0:T(8,128)(2,1)}, bf16[48,64,128]{2,1,0:T(8,128)(2,1)}, u32[]{:S(2)}, u32[]{:S(2)}) collective-permute-start(bf16[48,64,128]{2,1,0:T(8,128)(2,1)} %collective-permute-done.10), channel_id=1, source_target_pairs={{20,16},{22,24},{28,18},{30,26},{0,4},{2,12},{8,6},{10,14},{21,17}... | collective-permute-start | bytes 2359304 | tf_op jit(solution)/shard_map/ppermute | solution.py:317
  176.2 1.1 copy-start.2
  199.7 22.4 %collective-permute-start.13 = (bf16[8,64,128]{2,1,0:T(8,128)(2,1)}, bf16[8,64,128]{2,1,0:T(8,128)(2,1)S(1)}, u32[]{:S(2)}, u32[]{:S(2)}) collective-permute-start(bf16[8,64,128]{2,1,0:T(8,128)(2,1)} %get-tuple-element.57), channel_id=1, source_target_pairs={{0,8},{8,16},{16,24},{1,9},{9,17},{17,25},{2,10},{10,18},{18,26},{... | collective-permute-start | bytes 393224 | tf_op jit(solution)/shard_map/ppermute | solution.py:263
  219.8 6.5 %collective-permute-start.14 = (bf16[8,64,128]{2,1,0:T(8,128)(2,1)}, bf16[8,64,128]{2,1,0:T(8,128)(2,1)S(1)}, u32[]{:S(2)}, u32[]{:S(2)}) collective-permute-start(bf16[8,64,128]{2,1,0:T(8,128)(2,1)} %get-tuple-element.58), channel_id=1, source_target_pairs={{8,0},{16,8},{24,16},{9,1},{17,9},{25,17},{10,2},{18,10},{26,18},{... | collective-permute-start | bytes 393224 | tf_op jit(solution)/shard_map/ppermute | solution.py:263
  222.1 14.0 %copy-start.4 = (bf16[8,64,128]{2,1,0:T(8,128)(2,1)}, bf16[8,64,128]{2,1,0:T(8,128)(2,1)S(1)}, u32[]{:S(2)}) copy-start(bf16[8,64,128]{2,1,0:T(8,128)(2,1)S(1)} %collective-permute-done.13.rest_0_) | copy-start | bytes 393220
  226.3 9.7 %copy-start.5 = (bf16[8,64,128]{2,1,0:T(8,128)(2,1)}, bf16[8,64,128]{2,1,0:T(8,128)(2,1)S(1)}, u32[]{:S(2)}) copy-start(bf16[8,64,128]{2,1,0:T(8,128)(2,1)S(1)} %collective-permute-done.14.rest_1_) | copy-start | bytes 393220
  227.3 8.7 %collective-permute-start.16 = (bf16[80,8,128]{2,1,0:T(8,128)(2,1)S(1)}, bf16[80,8,128]{2,1,0:T(8,128)(2,1)S(1)}, u32[]{:S(2)}, u32[]{:S(2)}) collective-permute-start(bf16[80,8,128]{2,1,0:T(8,128)(2,1)S(1)} %pad_maximum_fusion.4), channel_id=1, source_target_pairs={{2,0},{4,2},{6,4},{3,1},{5,3},{7,5},{10,8},{12,10},{14,12},{11,9},... | collective-permute-start | bytes 491528 | tf_op jit(solution)/shard_map/ppermute | solution.py:263
  229.6 6.5 %collective-permute-start.15 = (bf16[80,8,128]{2,1,0:T(8,128)(2,1)S(1)}, bf16[80,8,128]{2,1,0:T(8,128)(2,1)S(1)}, u32[]{:S(2)}, u32[]{:S(2)}) collective-permute-start(bf16[80,8,128]{2,1,0:T(8,128)(2,1)S(1)} %pad_maximum_fusion.3), channel_id=1, source_target_pairs={{0,2},{2,4},{4,6},{1,3},{3,5},{5,7},{8,10},{10,12},{12,14},{9,11},... | collective-permute-start | bytes 491528 | tf_op jit(solution)/shard_map/ppermute | solution.py:263
  236.0 0.7 copy-start.10
  236.0 0.7 copy-start.11
  267.7 4.7 %collective-permute-start.17 = (bf16[4,64,128]{2,1,0:T(8,128)(2,1)}, bf16[4,64,128]{2,1,0:T(8,128)(2,1)S(1)}, u32[]{:S(2)}, u32[]{:S(2)}) collective-permute-start(bf16[4,64,128]{2,1,0:T(8,128)(2,1)} %get-tuple-element.64), channel_id=1, source_target_pairs={{0,8},{8,16},{16,24},{1,9},{9,17},{17,25},{2,10},{10,18},{18,26},{... | collective-permute-start | bytes 196616 | tf_op jit(solution)/shard_map/ppermute | solution.py:263
  270.5 5.8 %collective-permute-start.18 = (bf16[4,64,128]{2,1,0:T(8,128)(2,1)}, bf16[4,64,128]{2,1,0:T(8,128)(2,1)S(1)}, u32[]{:S(2)}, u32[]{:S(2)}) collective-permute-start(bf16[4,64,128]{2,1,0:T(8,128)(2,1)} %get-tuple-element.65), channel_id=1, source_target_pairs={{8,0},{16,8},{24,16},{9,1},{17,9},{25,17},{10,2},{18,10},{26,18},{... | collective-permute-start | bytes 196616 | tf_op jit(solution)/shard_map/ppermute | solution.py:263
  272.4 13.9 %copy-start.18 = (bf16[4,64,128]{2,1,0:T(8,128)(2,1)}, bf16[4,64,128]{2,1,0:T(8,128)(2,1)S(1)}, u32[]{:S(2)}) copy-start(bf16[4,64,128]{2,1,0:T(8,128)(2,1)S(1)} %collective-permute-done.17.rest_0_) | copy-start | bytes 196612
  276.3 10.0 %copy-start.19 = (bf16[4,64,128]{2,1,0:T(8,128)(2,1)}, bf16[4,64,128]{2,1,0:T(8,128)(2,1)S(1)}, u32[]{:S(2)}) copy-start(bf16[4,64,128]{2,1,0:T(8,128)(2,1)S(1)} %collective-permute-done.18.rest_1_) | copy-start | bytes 196612
  277.2 8.6 %collective-permute-start.20 = (bf16[72,8,128]{2,1,0:T(8,128)(2,1)S(1)}, bf16[72,8,128]{2,1,0:T(8,128)(2,1)S(1)}, u32[]{:S(2)}, u32[]{:S(2)}) collective-permute-start(bf16[72,8,128]{2,1,0:T(8,128)(2,1)S(1)} %pad_maximum_fusion.8), channel_id=1, source_target_pairs={{2,0},{4,2},{6,4},{3,1},{5,3},{7,5},{10,8},{12,10},{14,12},{11,9},... | collective-permute-start | bytes 442376 | tf_op jit(solution)/shard_map/ppermute | solution.py:263
  279.4 6.8 %collective-permute-start.19 = (bf16[72,8,128]{2,1,0:T(8,128)(2,1)S(1)}, bf16[72,8,128]{2,1,0:T(8,128)(2,1)S(1)}, u32[]{:S(2)}, u32[]{:S(2)}) collective-permute-start(bf16[72,8,128]{2,1,0:T(8,128)(2,1)S(1)} %pad_maximum_fusion.7), channel_id=1, source_target_pairs={{0,2},{2,4},{4,6},{1,3},{3,5},{5,7},{8,10},{10,12},{12,14},{9,11},... | collective-permute-start | bytes 442376 | tf_op jit(solution)/shard_map/ppermute | solution.py:263
  285.8 0.7 copy-start.12
  286.3 0.7 copy-start.13
  286.9 27.1 %copy-start.1 = (s32[32,512]{1,0:T(8,128)S(1)}, s32[32,512]{1,0:T(8,128)}, u32[]{:S(2)}) copy-start(s32[32,512]{1,0:T(8,128)} %param.9) | copy-start | bytes 196612

commit v3 on v2

v3 whole, which is shorter than its diff:
```python
import functools
import math

import jax
import jax.numpy as jnp
from jax import lax
from jax.experimental import pallas as pl
from jax.experimental.pallas import tpu as pltpu
from jax.sharding import PartitionSpec as P

epsilon = 1e-05
F32 = jnp.float32
BF16 = jnp.bfloat16
BLOCK = 16
ROWS = 16
EDGE = 8
PAD = 16


def lane_low(shape):
    return lax.broadcasted_iota(jnp.int32, shape, len(shape) - 1) < shape[-1] // 2


def lane_sums(values, ones):
    return jnp.sum(values, -1, keepdims=True)


def standardize(centred, ones):
    inverse = lax.rsqrt(lane_sums(centred * centred, ones) + epsilon * centred.shape[-1])
    return centred * inverse, inverse


def elu(values):
    return jnp.maximum(values, jnp.exp(jnp.minimum(values, 0.0)) - 1.0)


def slope_from_elu(activated):
    return 1.0 + jnp.minimum(activated, 0.0)


def standardize_back(standard, inverse, upstream, ones):
    return inverse * (upstream - standard * lane_sums(upstream * standard, ones))


def side_by_side(values):
    count = values.shape[0] // 2
    return jnp.concatenate([values[:count], values[count:]], axis=1)


def stacked(values):
    width = values.shape[1] // 2
    return jnp.concatenate([values[:, :width], values[:, width:]], axis=0)


def swapped(values):
    flat = values.reshape(-1, values.shape[-1])
    return pltpu.roll(flat, flat.shape[1] // 2, 1).reshape(values.shape)


def squeeze(centred, ones, gain, down):
    standard, unused = standardize(centred, ones)
    entered = elu(standard * gain).astype(BF16)
    return elu(jnp.dot(side_by_side(entered), down, preferred_element_type=F32))


def widened(activated, weight):
    return stacked(jnp.dot(jnp.concatenate([activated, activated], axis=1), weight, preferred_element_type=F32))


def store_edges(values, refs, spacing, step, steps):
    top, bottom, left, right = refs
    middle = values.shape[1] // 2
    left[...] = values[:, :EDGE].astype(BF16)
    right[...] = values[:, values.shape[1] - EDGE :].astype(BF16)
    count = min(ROWS, spacing)
    low = lane_low((count, middle, values.shape[2]))
    taken = spacing // count

    @pl.when(step < taken)
    def _():
        sent = values[:count]
        rows = pl.ds(jnp.minimum(step, taken - 1) * count, count)
        top[rows] = jnp.where(low, sent[:, :middle], swapped(sent[:, middle:])).astype(BF16)

    @pl.when(step >= steps - taken)
    def _():
        sent = values[ROWS - count :]
        rows = pl.ds(jnp.maximum(step - (steps - taken), 0) * count, count)
        bottom[rows] = jnp.where(low, swapped(sent[:, :middle]), sent[:, middle:]).astype(BF16)


def fill_padded(padded, centre, halos, spacing):
    above, below, before, after = halos
    half, columns, lanes = centre.shape
    middle = columns // 2

    def lay(row, carry):
        padded[spacing + row, PAD : PAD + columns] = centre[row]
        padded[spacing + row, PAD - EDGE : PAD] = before[row]
        padded[spacing + row, PAD + columns : PAD + columns + EDGE] = after[row]
        return carry

    lax.fori_loop(0, half, lay, 0)
    wide, slim = lane_low((middle, lanes)), lane_low((EDGE, lanes))

    def put(row, start, low, first, second):
        padded[row, start : start + low.shape[0]] = jnp.where(low, first, second).astype(BF16)

    def read(array, row):
        return array[row].astype(F32)

    for row in range(spacing):
        own = swapped(read(centre, half - spacing + row))
        sent = read(above, row)
        put(row, PAD, wide, sent, own[:middle])
        put(row, PAD + middle, wide, swapped(sent), own[middle:])
        edge = half - spacing + row
        put(row, PAD - EDGE, slim, swapped(read(before, half + row)), swapped(read(before, edge)))
        put(row, PAD + columns, slim, read(after, half + row), swapped(read(after, edge)))
        place = spacing + half + row
        own = swapped(read(centre, row))
        sent = read(below, row)
        put(place, PAD, wide, own[:middle], swapped(sent))
        put(place, PAD + middle, wide, own[middle:], sent)
        corner = half + spacing + row
        put(place, PAD - EDGE, slim, swapped(read(before, row)), read(before, corner))
        put(place, PAD + columns, slim, swapped(read(after, row)), swapped(read(after, corner)))


def convolve(padded, kernel, taps, spacing, step, columns):
    width = columns + 2 * PAD
    lanes = padded.shape[2]
    parts = [padded[pl.ds(step * ROWS + tap * spacing, ROWS)] for tap in range(3)]
    joined = jnp.concatenate(parts, axis=2).reshape(ROWS * width, 3 * lanes)
    taps[...] = jnp.dot(joined, kernel[...], preferred_element_type=F32).reshape(ROWS, width, 3 * lanes)
    total = taps[:, PAD : PAD + columns, lanes : 2 * lanes]
    if spacing % EDGE:
        outer = taps[:, PAD - EDGE : PAD + columns, :lanes]
        start = PAD - EDGE + 2 * spacing
        outer = outer + taps[:, start : start + columns + EDGE, 2 * lanes :]
        total = total + outer[:, EDGE - spacing : EDGE - spacing + columns]
    else:
        total = total + taps[:, PAD - spacing : PAD - spacing + columns, :lanes]
        total = total + taps[:, PAD + spacing : PAD + spacing + columns, 2 * lanes :]
    return total.reshape(ROWS * columns, lanes)


def strip(reference):
    return reference[...].reshape(-1, reference.shape[-1])


def over_strips(body, kinds, *refs):
    inner = BLOCK // ROWS

    def one(place, carry):
        rows = pl.ds(place * ROWS, ROWS)
        views = []
        for kind, ref in zip(kinds, refs):
            views.append(ref.at[:, rows] if kind == "halves" else ref.at[rows] if kind == "rows" else ref)
        body(pl.program_id(0) * inner + place, *views)
        return carry

    lax.fori_loop(0, inner, one, 0)


def entry_kernel(spacing, steps, step, features, centring, ones, gain, down, squeezed, *edges):
    centred = jnp.dot(strip(features), centring[...], preferred_element_type=F32)
    values = squeeze(centred, ones, gain[...], down[...]).reshape(squeezed.shape)
    squeezed[...] = values.astype(BF16)
    store_edges(values, edges, spacing, step, steps)


def middle_kernel(near, far, steps, step, centre, *rest):
    halos, rest = rest[:4], rest[4:]
    features, centring, ones, kernel, up, gain, down, stream_out, activated_out, squeezed, *rest = rest
    edges, (padded, taps) = rest[:4], rest[4:]
    columns = centre.shape[1]

    @pl.when(step == 0)
    def _():
        fill_padded(padded, centre, halos, near)

    activated = elu(convolve(padded, kernel, taps, near, step, columns)).astype(BF16)
    activated_out[...] = activated.reshape(activated_out.shape)
    stream = jnp.dot(strip(features), centring[...], preferred_element_type=F32) + widened(activated, up[...])
    stream_out[...] = stream.reshape(stream_out.shape)
    values = squeeze(stream, ones, gain[...], down[...]).reshape(squeezed.shape)
    squeezed[...] = values.astype(BF16)
    store_edges(values, edges, far, step, steps)


def head_kernel(near, steps, step, centre, *rest):
    halos, rest = rest[:4], rest[4:]
    stream_in, ones, kernel, up, gain, head, bias, stream_out, activated_out, by_row, by_column, padded, taps = rest
    columns = centre.shape[1]

    @pl.when(step == 0)
    def _():
        fill_padded(padded, centre, halos, near)

    activated = elu(convolve(padded, kernel, taps, near, step, columns)).astype(BF16)
    activated_out[...] = activated.reshape(activated_out.shape)
    stream = strip(stream_in) + widened(activated, up[...])
    stream_out[...] = stream.reshape(stream_out.shape)
    standard, unused = standardize(stream, ones)
    entered = (standard * gain[...]).astype(BF16).reshape(2, ROWS, columns, stream.shape[1])
    pairs = jnp.concatenate([entered[0], entered[1]], axis=2).reshape(ROWS * columns, -1)
    logits = jnp.dot(pairs, head[...], preferred_element_type=F32) + bias[...]
    by_row[...] = logits.astype(BF16).reshape(by_row.shape)
    pairs = jnp.concatenate([entered[:, :, : columns // 2], entered[:, :, columns // 2 :]], axis=3)
    logits = jnp.dot(pairs.reshape(ROWS * columns, -1), head[...], preferred_element_type=F32) + bias[...]
    by_column[...] = logits.astype(BF16).reshape(by_column.shape)


def loss_kernel(
    spacing, steps, inner, pieces, step, by_row, *rest
):
    facing, rest = rest[: sum(pieces)], rest[sum(pieces) :]
    targets, stream, activated, ones, head, group, up, grad_out, conv_out, *rest = rest
    edges, (turned,) = rest[:4], rest[4:]

    @pl.when(step % inner == 0)
    def _():
        place = taken = 0
        for count in pieces:
            piece = sum(array[...].astype(F32) for array in facing[taken : taken + count])
            turned[:, place : place + piece.shape[0]] = jnp.swapaxes(piece, 0, 1)
            place, taken = place + piece.shape[0], taken + count

    start = (step % inner) * ROWS
    columns, lanes = by_row.shape[1:]
    symmetric = 0.5 * (by_row[...].astype(F32) + turned[pl.ds(start, ROWS)])
    exponent = jnp.exp(symmetric).reshape(ROWS * columns, lanes)
    upper = exponent.astype(BF16)
    lower = (exponent - upper.astype(F32)).astype(BF16)
    total = jnp.dot(upper, group[...], preferred_element_type=F32) + jnp.dot(
        lower, group[...], preferred_element_type=F32
    )
    logit_grad = (exponent / total - targets[...].astype(F32).reshape(exponent.shape)).astype(BF16)
    back = widened(logit_grad, head[...])
    standard, inverse = standardize(strip(stream), ones)
    grad = standardize_back(standard, inverse, back, ones)
    grad_out[...] = grad.reshape(grad_out.shape)
    values = jnp.dot(side_by_side(grad.astype(BF16)), up[...], preferred_element_type=F32)
    values = values * slope_from_elu(strip(activated).astype(F32))
    values = values.reshape(conv_out.shape)
    conv_out[...] = values.astype(BF16)
    store_edges(values, edges, spacing, step, steps)


def back_strip(spacing, step, centre, padded, taps, kernel, squeezed, down, centred, ones, gain, upstream):
    columns = centre.shape[1]
    lowered = convolve(padded, kernel, taps, spacing, step, columns)
    lowered = lowered * slope_from_elu(strip(squeezed).astype(F32))
    entered = stacked(jnp.dot(lowered.astype(BF16), down[...], preferred_element_type=F32))
    standard, inverse = standardize(centred, ones)
    scale = gain[...]
    entered = entered * (jnp.exp2(jnp.minimum(standard * (scale * math.log2(math.e)), 0.0)) * scale)
    entered = entered - jnp.sum(entered, -1, keepdims=True) * (1.0 / entered.shape[-1])
    return strip(upstream) + standardize_back(standard, inverse, entered, ones)


def back_kernel(near, far, steps, step, centre, *rest):
    halos, rest = rest[:4], rest[4:]
    kernel, squeezed, down, stream, ones, gain, upstream, activated, up, grad_out, conv_out, *rest = rest
    edges, (padded, taps) = rest[:4], rest[4:]

    @pl.when(step == 0)
    def _():
        fill_padded(padded, centre, halos, near)

    grad = back_strip(near, step, centre, padded, taps, kernel, squeezed, down, strip(stream), ones, gain, upstream)
    grad_out[...] = grad.reshape(grad_out.shape)
    values = jnp.dot(side_by_side(grad.astype(BF16)), up[...], preferred_element_type=F32)
    values = values * slope_from_elu(strip(activated).astype(F32))
    values = values.reshape(conv_out.shape)
    conv_out[...] = values.astype(BF16)
    store_edges(values, edges, far, step, steps)


def final_kernel(near, step, centre, *rest):
    halos, rest = rest[:4], rest[4:]
    kernel, squeezed, down, features, centring, ones, gain, upstream, grad_out, padded, taps = rest

    @pl.when(step == 0)
    def _():
        fill_padded(padded, centre, halos, near)

    centred = jnp.dot(strip(features), centring[...], preferred_element_type=F32)
    grad = back_strip(near, step, centre, padded, taps, kernel, squeezed, down, centred, ones, gain, upstream)
    grad_out[...] = grad.reshape(grad_out.shape)


def shifted(values, axis, move):
    count = lax.axis_size(axis)
    return lax.ppermute(values, axis, [(i, i + move) for i in range(count) if 0 <= i + move < count])


def exchange(edges):
    top, bottom, left, right = edges
    above = shifted(bottom, "row", 1)
    below = shifted(top, "row", -1)
    before = jnp.concatenate([right, above[:, -EDGE:], below[:, -EDGE:]], axis=0)
    after = jnp.concatenate([left, above[:, :EDGE], below[:, :EDGE]], axis=0)
    return above, below, shifted(before, "col", 1), shifted(after, "col", -1)


def facing_tile(tile):
    rows, cols = lax.axis_size("row"), lax.axis_size("col")
    if rows == cols:
        pairs = [(row * cols + col, col * cols + row) for row in range(rows) for col in range(cols)]
        return lax.ppermute(tile, ("row", "col"), pairs)
    if cols % rows:
        raise ValueError("unsupported mesh")
    times = cols // rows
    height = tile.shape[0] // times
    place = lax.axis_index("col") % times
    received = []
    for turn in range(times):
        piece = lax.dynamic_slice_in_dim(tile, ((place + turn) % times) * height, height, axis=0)
        pairs = [
            (row * cols + col, (col // times) * cols + times * row + (col % times + turn) % times)
            for row in range(rows)
            for col in range(cols)
        ]
        received.append(lax.ppermute(piece, ("row", "col"), pairs))
    stacked = jnp.stack(received)
    pieces = [
        lax.dynamic_index_in_dim(stacked, (place - source) % times, axis=0, keepdims=False)
        for source in range(times)
    ]
    return jnp.concatenate(pieces, axis=1)


def facing_logits(by_column):
    rows, cols = lax.axis_size("row"), lax.axis_size("col")
    if rows == cols and rows % 2 == 0:
        cut = by_column.shape[0] * 5 // 128 * 16
        straight, around = by_column[:cut], by_column[cut:]
        places = [(row, col) for row in range(rows) for col in range(cols)]
        part = rows // 2
        far = [(row, col) for row, col in places if row // part != col // part]
        close = [(row, col) for row, col in places if row // part == col // part]
        both = ("row", "col")
        number = lambda row, col: row * cols + col
        other = lambda row: (row + part) % rows
        hop = lax.ppermute(around, both, [(number(row, col), number(other(row), col)) for row, col in far])
        straight = lax.ppermute(straight, both, [(number(row, col), number(col, row)) for row, col in places])
        near = lax.ppermute(around, both, [(number(row, col), number(col, row)) for row, col in close])
        hop = lax.ppermute(hop, both, [(number(other(row), col), number(col, row)) for row, col in far])
        return [[straight], [hop, near]]
    if rows == cols:
        return [[facing_tile(by_column)]]
    bins = by_column.shape[2] // 2
    tile = facing_tile(jnp.concatenate([by_column[..., :bins], by_column[..., bins:]], axis=1))
    half = tile.shape[1] // 2
    return [[jnp.concatenate([tile[:, :half], tile[:, half:]], axis=2)]]


def dilated_weights(kernel):
    both = jnp.eye(2, dtype=kernel.dtype)[None, :, None, None, :, None]
    spread = jnp.transpose(kernel, (0, 2, 1, 3))[:, None, :, :, None, :] * both
    return spread.reshape(6 * kernel.shape[2], 6 * kernel.shape[3])


def mirrored(kernel):
    return jnp.swapaxes(kernel[::-1, ::-1], 2, 3)


def diagonal(weight):
    zeros = jnp.zeros_like(weight)
    return jnp.concatenate(
        [jnp.concatenate([weight, zeros], axis=1), jnp.concatenate([zeros, weight], axis=1)], axis=0
    )


def two_parts(weight):
    centred = weight - jnp.mean(weight, axis=1, keepdims=True)
    upper = lax.reduce_precision(centred, 8, 7)
    return jnp.concatenate([diagonal(upper), diagonal(centred - upper)], axis=0).astype(BF16)


def shards(features, labels, norm_gain, w_down, w_conv, w_up, w_head, head_bias):
    rows, columns, channels = features.shape
    narrow = w_down.shape[2]
    bins = w_head.shape[1]
    half = rows // 2
    steps = half // ROWS
    lanes = 2 * narrow
    near, far = 4, 8

    gains = [norm_gain[index : index + 1] * math.sqrt(channels) for index in range(3)]
    downs = [diagonal(w_down[index]) for index in range(2)]
    downs_back = [diagonal(w_down[index].T) for index in range(2)]
    centring = (jnp.eye(channels) - 1.0 / channels).astype(BF16)
    ones = jnp.ones((channels, channels), BF16)
    ups = [two_parts(w_up[index].astype(F32)) for index in range(2)]
    ups_back = [diagonal(w_up[index].T) for index in range(2)]
    convs = [dilated_weights(w_conv[index]) for index in range(2)]
    convs_back = [dilated_weights(mirrored(w_conv[index])) for index in range(2)]
    head = diagonal(w_head)
    head_back = two_parts(w_head.T.astype(F32) * gains[2])
    bias = jnp.concatenate([head_bias, head_bias])[None]
    group = diagonal(jnp.ones((bins, bins), BF16))

    def whole(array):
        zeros = (0,) * len(array.shape)
        return "whole", pl.BlockSpec(array.shape, lambda step: zeros)

    def strip_spec(width):
        return "halves", pl.BlockSpec((2, BLOCK, columns, width), lambda step: (0, step, 0, 0))

    def halves(dtype, width):
        return jax.ShapeDtypeStruct((2, half, columns, width), dtype)

    pair_spec = "rows", pl.BlockSpec((BLOCK, columns, lanes), lambda step: (step, 0, 0))
    pair_shape = jax.ShapeDtypeStruct((half, columns, lanes), BF16)

    def edges(spacing):
        shapes = [jax.ShapeDtypeStruct((spacing, columns // 2, lanes), BF16)] * 2
        shapes += [jax.ShapeDtypeStruct((half, EDGE, lanes), BF16)] * 2
        sides = "rows", pl.BlockSpec((BLOCK, EDGE, lanes), lambda step: (step, 0, 0))
        return shapes, [whole(shapes[0]), whole(shapes[1]), sides, sides]

    def scratch(spacing):
        width = columns + 2 * PAD
        return [
            pltpu.VMEM((half + 2 * spacing, width, lanes), BF16),
            pltpu.VMEM((ROWS, width, 3 * lanes), F32),
        ]

    def cost(convolutions, passes):
        pixels = rows * columns
        return pl.CostEstimate(
            flops=pixels * (convolutions * 18 * narrow * narrow + 4 * narrow * channels),
            bytes_accessed=pixels * channels * passes,
            transcendentals=pixels * channels,
        )

    def call(body, inputs, specs, shapes, out_specs, scratch_shapes, estimate, name):
        kinds = [kind for kind, spec in specs + out_specs] + ["whole"] * len(scratch_shapes)
        return pl.pallas_call(
            functools.partial(over_strips, body, kinds),
            grid=(half // BLOCK,),
            in_specs=[spec for kind, spec in specs],
            out_specs=[spec for kind, spec in out_specs],
            out_shape=shapes,
            scratch_shapes=scratch_shapes,
            compiler_params=pltpu.CompilerParams(vmem_limit_bytes=56 * 1024 * 1024),
            cost_estimate=estimate,
            name=name,
        )(*inputs)

    split = features.reshape(2, half, columns, channels)
    bf_spec = strip_spec(channels)
    near_shapes, near_specs = edges(near)
    far_shapes, far_specs = edges(far)

    squeezed_1, *sent = call(
        functools.partial(entry_kernel, near, steps),
        (split, centring, ones, gains[0], downs[0]),
        [bf_spec] + [whole(array) for array in (centring, ones, gains[0], downs[0])],
        [pair_shape] + near_shapes,
        [pair_spec] + near_specs,
        [],
        cost(0, 4),
        "entry",
    )
    own_labels = lax.all_to_all(labels, "col", split_axis=1, concat_axis=0, tiled=True)
    squeezed_1, own_labels = lax.optimization_barrier((squeezed_1, own_labels))
    halos = exchange(sent)

    centre = squeezed_1
    stream_1, activated_1, squeezed_2, *sent = call(
        functools.partial(middle_kernel, near, far, steps),
        (centre, *halos, split, centring, ones, convs[0], ups[0], gains[1], downs[1]),
        [whole(centre)] + [whole(halo) for halo in halos] + [bf_spec]
        + [whole(array) for array in (centring, ones, convs[0], ups[0], gains[1], downs[1])],
        [halves(F32, channels), pair_shape, pair_shape] + far_shapes,
        [strip_spec(channels), pair_spec, pair_spec] + far_specs,
        scratch(near),
        cost(1, 12),
        "middle",
    )
    halos = exchange(sent)

    facing_labels = facing_tile(own_labels)
    squeezed_2, facing_labels = lax.optimization_barrier((squeezed_2, facing_labels))
    facing_labels = facing_labels.T
    centre = squeezed_2
    by_row_spec = "rows", pl.BlockSpec((BLOCK, columns, 2 * bins), lambda step: (step, 0, 0))
    stream_2, activated_2, by_row, by_column = call(
        functools.partial(head_kernel, far, steps),
        (centre, *halos, stream_1, ones, convs[1], ups[1], gains[2], head, bias),
        [whole(centre)] + [whole(halo) for halo in halos] + [bf_spec]
        + [whole(array) for array in (ones, convs[1], ups[1], gains[2], head, bias)],
        [
            halves(F32, channels),
            pair_shape,
            jax.ShapeDtypeStruct((half, columns, 2 * bins), BF16),
            jax.ShapeDtypeStruct((2, half, columns // 2, 2 * bins), BF16),
        ],
        [
            strip_spec(channels),
            pair_spec,
            by_row_spec,
            ("halves", pl.BlockSpec((2, BLOCK, columns // 2, 2 * bins), lambda step: (0, step, 0, 0))),
        ],
        scratch(far),
        cost(1, 14),
        "head",
    )
    facing = facing_logits(by_column.reshape(rows, columns // 2, 2 * bins))

    numbers = jnp.arange(bins, dtype=jnp.int32)

    def onehot(values):
        return (values[:, :, None] == numbers).astype(F32)

    targets = jnp.concatenate(
        [
            0.5 * (onehot(own_labels[part]) + onehot(facing_labels[part]))
            for part in (slice(0, half), slice(half, rows))
        ],
        axis=2,
    ).astype(BF16)

    inner = BLOCK // ROWS
    mirrored_logits = [array for piece in facing for array in piece]
    grad_2, conv_grad_2, *sent = call(
        functools.partial(loss_kernel, far, steps, inner, tuple(len(piece) for piece in facing)),
        (by_row, *mirrored_logits, targets, stream_2, activated_2, ones, head_back, group, ups_back[1]),
        [
            by_row_spec,
            *(("whole", pl.BlockSpec((array.shape[0], BLOCK, 2 * bins), lambda step: (0, step, 0)))
              for array in mirrored_logits),
            by_row_spec,
            bf_spec,
            pair_spec,
        ]
        + [whole(array) for array in (ones, head_back, group, ups_back[1])],
        [halves(F32, channels), pair_shape] + far_shapes,
        [strip_spec(channels), pair_spec] + far_specs,
        [pltpu.VMEM((BLOCK, columns, 2 * bins), F32)],
        cost(0, 18),
        "loss",
    )
    halos = exchange(sent)

    centre = conv_grad_2
    grad_1, conv_grad_1, *sent = call(
        functools.partial(back_kernel, far, near, steps),
        (centre, *halos, convs_back[1], squeezed_2, downs_back[1], stream_1, ones, gains[1], grad_2, activated_1, ups_back[0]),
        [whole(centre)] + [whole(halo) for halo in halos]
        + [
            whole(convs_back[1]),
            pair_spec,
            whole(downs_back[1]),
            bf_spec,
            whole(ones),
            whole(gains[1]),
            bf_spec,
            pair_spec,
            whole(ups_back[0]),
        ],
        [halves(F32, channels), pair_shape] + near_shapes,
        [strip_spec(channels), pair_spec] + near_specs,
        scratch(far),
        cost(1, 20),
        "back",
    )
    halos = exchange(sent)

    centre = conv_grad_1
    (grad_0,) = call(
        functools.partial(final_kernel, near),
        (centre, *halos, convs_back[0], squeezed_1, downs_back[0], split, centring, ones, gains[0], grad_1),
        [whole(centre)] + [whole(halo) for halo in halos]
        + [
            whole(convs_back[0]),
            pair_spec,
            whole(downs_back[0]),
            bf_spec,
            whole(centring),
            whole(ones),
            whole(gains[0]),
            bf_spec,
        ],
        [halves(F32, channels)],
        [strip_spec(channels)],
        scratch(near),
        cost(1, 16),
        "final",
    )
    return grad_0.reshape(features.shape)


def solution(mesh):
    return jax.shard_map(
        shards,
        mesh=mesh,
        in_specs=(
            P(("dp", "row"), "col", None),
            P(("dp", "row", "col"), None),
            P(),
            P(),
            P(),
            P(),
            P(),
            P(),
        ),
        out_specs=P(("dp", "row"), "col", None),
        check_vma=False,
    )
```

time: 318 us -> 267 us (0.84)
  Pallas kernels: 152 us -> 91.7 us
  local copies, waits for them, and re-layouts: 16.9 us -> 22.2 us
  other arithmetic: 20.7 us -> 25.4 us
  waiting for transfers between devices: 43.3 us -> 46.9 us
    pallas_call x6, Pallas kernels: 152 us -> 91.7 us  [call(): pl.pallas_call(functools.partial(over_strips, body, kinds), grid=(half //...]
    ppermute x16, waiting for transfers between devices: 13.8 us -> 19.4 us  [shifted(): lax.ppermute(values, axis, [(i, i + move) for i in range(count) if 0 <= i...]
    pad x8 -> x0, local copies, waits for them, and re-layouts: 5.28 us -> none  [the longest x4 2.81 us: dilated_weights(): return jnp.pad(flat, ((0, kernel.shape[2]), (0, 0)))]
    mul x0 -> x4, local copies, waits for them, and re-layouts: none -> 4.42 us  [dilated_weights(): spread = jnp.transpose(kernel, (0, 2, 1, 3))[:, None, :, :, None, :] * both]
    ppermute x16, starting transfers between devices: 62.1 us -> 57.9 us  [shifted(): lax.ppermute(values, axis, [(i, i + move) for i in range(count) if 0 <= i...]
  transfers between devices with their start and end apart: 22 -> 22, of which waited for: 10 -> 10; matrix products, arithmetic and copies ran while one was open for 8% -> 14% of each run, Pallas kernels for 0% -> 3%
where the time goes in v3:
time: 267 us; the launch traced here: 266 us
  Pallas kernels  91.7 us (34%)
  starting transfers between devices  78.9 us (30%)
  waiting for transfers between devices  46.9 us (18%)
  other arithmetic  25.4 us (10%)
  local copies, waits for them, and re-layouts  22.2 us (8%)
    pallas_call x6, Pallas kernels, call(): pl.pallas_call(functools.partial(over_strips, body, kinds), grid=(half //...  91.7 us
    ppermute x16, starting transfers between devices, shifted(): lax.ppermute(values, axis, [(i, i + move) for i in range(count) if 0 <= i...  57.9 us
    ppermute x16, waiting for transfers between devices, shifted(): lax.ppermute(values, axis, [(i, i + move) for i in range(count) if 0 <= i...  19.4 us
    ppermute x1, waiting for transfers between devices, facing_logits(): lax.ppermute(around, both, [(number(row, col), number(col, row)) for row,...  15.7 us
    ppermute x1, waiting for transfers between devices, facing_logits(): lax.ppermute(around, both, [(number(row, col), number(other(row), col)) f...  8.95 us
    ppermute x1, starting transfers between devices, facing_logits(): lax.ppermute(hop, both, [(number(other(row), col), number(col, row)) for...  6.72 us
    another operation x5, other arithmetic  5.67 us
    all_to_all x1, starting transfers between devices, shards(): lax.all_to_all(labels, 'col', split_axis=1, concat_axis=0, tiled=True)  5.41 us
  transfers between devices with their start and end apart: 22, of which 10 were waited for; matrix products, arithmetic and copies ran while one was open for 14% of the time, Pallas kernels for 3%

profile of v3, /device:TPU:1, one launch (start us, length us, event | category | flops | bytes accessed | tf_op | source)
XLA Modules:
  0.0 265.8 jit_solution(3803167104478006105)
XLA Ops:
  1.5 5.4 %all-to-all-start = ((s32[32,4,128]{2,0,1:T(8,128)}), s32[32,4,128]{2,0,1:T(8,128)S(1)}, u32[]{:S(2)}, u32[]{:S(2)}) async-start(s32[32,4,128]{2,0,1:T(8,128)} %copy_bitcast_fusion), calls=%async_computation | async-start | bytes 131072 | tf_op jit(solution)/shard_map/all_to_all | solution.py:469
  7.5 1.3 fusion.51
  8.8 1.4 slice_bitcast_fusion.6
  11.5 8.3 %entry.1 = (bf16[64,128,128]{2,1,0:T(8,128)(2,1)}, bf16[4,64,128]{2,1,0:T(8,128)(2,1)}, bf16[4,64,128]{2,1,0:T(8,128)(2,1)}, bf16[64,8,128]{2,1,0:T(8,128)(2,1)}, bf16[64,8,128]{2,1,0:T(8,128)(2,1)}) custom-call(bf16[2,64,128,128]{3,2,1,0:T(8,128)(2,1)} %bitcast.55, bf16[128,128]{1,0:T(8,128)(2,1)} %add_convert_fusion.refs_1_.refs_6_.refs_9_, ...), custom_call_target="tpu_custom_call" | custom-call | flops 536870912 | bytes 8388608 | tf_op jit(solution)/shard_map/entry/pallas_call | solution.py:442
  19.9 4.1 %collective-permute-start = (bf16[4,64,128]{2,1,0:T(8,128)(2,1)}, bf16[4,64,128]{2,1,0:T(8,128)(2,1)}, u32[]{:S(2)}, u32[]{:S(2)}) collective-permute-start(bf16[4,64,128]{2,1,0:T(8,128)(2,1)} %get-tuple-element.39), channel_id=1, source_target_pairs={{0,8},{8,16},{16,24},{1,9},{9,17},{17,25},{2,10},{10,18},{18,26},{... | collective-permute-start | bytes 196616 | tf_op jit(solution)/shard_map/ppermute | solution.py:296
  24.0 1.9 collective-permute-start.1
  28.1 2.7 %broadcast_multiply_fusion = (bf16[3,2,64,3,2,64]{5,4,3,2,1,0:T(2,128)(2,1)S(1)}, bf16[3,2,64,3,2,64]{5,4,3,2,1,0:T(2,128)(2,1)S(1)}, bf16[3,2,64,3,2,64]{5,4,3,...) fusion(bf16[3,64,3,64]{3,2,1,0:T(4,128)(2,1)S(1)} %copy.67, bf16[2,2]{1,0:T(2,128)(2,1)} %compare_convert_fusion, ...), kind=kLoop, calls=%fused_computation.15 | loop fusion | flops 589824 | bytes 1474568 | tf_op jit(solution)/shard_map/mul | solution.py:362
  32.3 3.7 %collective-permute-start.2 = (bf16[72,8,128]{2,1,0:T(8,128)(2,1)S(1)}, bf16[72,8,128]{2,1,0:T(8,128)(2,1)S(1)}, u32[]{:S(2)}, u32[]{:S(2)}) collective-permute-start(bf16[72,8,128]{2,1,0:T(8,128)(2,1)S(1)} %pad_maximum_fusion.5), channel_id=1, source_target_pairs={{0,2},{2,4},{4,6},{1,3},{3,5},{5,7},{8,10},{10,12},{12,14},{9,11},... | collective-permute-start | bytes 442376 | tf_op jit(solution)/shard_map/ppermute | solution.py:296
  36.0 1.3 collective-permute-start.3
  39.8 1.1 mul.98.refs_8_
  41.0 1.5 collective-permute-done.3.refs_4_
  43.1 17.1 %middle.1 = (f32[2,64,128,128]{3,2,1,0:T(8,128)}, bf16[64,128,128]{2,1,0:T(8,128)(2,1)}, bf16[64,128,128]{2,1,0:T(8,128)(2,1)}, bf16[8,64,128]{2,1,0:T(8,128)(2,...) custom-call(bf16[64,128,128]{2,1,0:T(8,128)(2,1)} %get-tuple-element.38.refs_0_.refs_6_, ...), custom_call_target="tpu_custom_call" | custom-call | flops 1744830464 | bytes 25165824 | tf_op jit(solution)/shard_map/middle/pallas_call | solution.py:442
  60.3 4.5 %collective-permute-start.5 = (bf16[8,64,128]{2,1,0:T(8,128)(2,1)}, bf16[8,64,128]{2,1,0:T(8,128)(2,1)S(1)}, u32[]{:S(2)}, u32[]{:S(2)}) collective-permute-start(bf16[8,64,128]{2,1,0:T(8,128)(2,1)} %get-tuple-element.46), channel_id=1, source_target_pairs={{0,8},{8,16},{16,24},{1,9},{9,17},{17,25},{2,10},{10,18},{18,26},{... | collective-permute-start | bytes 393224 | tf_op jit(solution)/shard_map/ppermute | solution.py:296
  65.6 1.9 collective-permute-start.6
  67.6 4.5 %collective-permute-done.6.refs_2_ = bf16[8,64,128]{2,1,0:T(8,128)(2,1)S(1)} collective-permute-done((bf16[8,64,128]{2,1,0:T(8,128)(2,1)}, bf16[8,64,128]{2,1,0:T(8,128)(2,1)S(1)}, u32[]{:S(2)}, u32[]{:S(2)}) %collective-permute-start.6) | collective-permute-done | bytes 131104 | tf_op jit(solution)/shard_map/ppermute | solution.py:296
  73.1 3.1 %collective-permute-start.7 = (bf16[80,8,128]{2,1,0:T(8,128)(2,1)S(1)}, bf16[80,8,128]{2,1,0:T(8,128)(2,1)S(1)}, u32[]{:S(2)}, u32[]{:S(2)}) collective-permute-start(bf16[80,8,128]{2,1,0:T(8,128)(2,1)S(1)} %pad_maximum_fusion.1), channel_id=1, source_target_pairs={{0,2},{2,4},{4,6},{1,3},{3,5},{5,7},{8,10},{10,12},{12,14},{9,11},... | collective-permute-start | bytes 491528 | tf_op jit(solution)/shard_map/ppermute | solution.py:296
  77.1 1.3 collective-permute-start.8
  79.3 1.1 mul.102.refs_7_
  80.4 2.1 collective-permute-start.4
  83.1 2.9 %collective-permute-done.4 = s32[128,128]{1,0:T(8,128)S(1)} collective-permute-done((s32[128,128]{1,0:T(8,128)S(1)}, s32[128,128]{1,0:T(8,128)S(1)}, u32[]{:S(2)}, u32[]{:S(2)}) %collective-permute-start.4) | collective-permute-done | bytes 65568 | tf_op jit(solution)/shard_map/ppermute | solution.py:312
  86.7 16.5 %head.1 = (f32[2,64,128,128]{3,2,1,0:T(8,128)}, bf16[64,128,128]{2,1,0:T(8,128)(2,1)}, bf16[64,128,128]{2,1,0:T(8,128)(2,1)}, bf16[2,64,64,128]{3,2,1,0:T(8,128)(2,1)}) custom-call(bf16[64,128,128]{2,1,0:T(8,128)(2,1)} %get-tuple-element.45.refs_0_.refs_6_, bf16[8,64,128]{2,1,0:T(8,128)(2,1)} %copy-done.5, bf16[8,64,128]{2,1,0:T(8,128)(2,1)} %copy-done.7, ...), custom_call_target="tpu_custom_call" | custom-call | flops 1744830464 | bytes 29360128 | tf_op jit(solution)/shard_map/head/pallas_call | solution.py:442
  103.2 2.1 slice.139
  105.3 1.3 collective-permute-start.10
  106.7 2.5 slice.138
  109.2 1.9 collective-permute-start.9
  112.5 3.6 %collective-permute-start.12 = (bf16[48,64,128]{2,1,0:T(8,128)(2,1)}, bf16[48,64,128]{2,1,0:T(8,128)(2,1)S(1)}, u32[]{:S(2)}, u32[]{:S(2)}) collective-permute-start(bf16[48,64,128]{2,1,0:T(8,128)(2,1)} %slice.139), channel_id=1, source_target_pairs={{0,0},{2,8},{8,2},{10,10},{20,20},{22,28},{28,22},{30,30},{1,1},{3... | collective-permute-start | bytes 2359304 | tf_op jit(solution)/shard_map/ppermute | solution.py:349
  116.1 9.0 %collective-permute-done.10 = bf16[48,64,128]{2,1,0:T(8,128)(2,1)} collective-permute-done((bf16[48,64,128]{2,1,0:T(8,128)(2,1)}, bf16[48,64,128]{2,1,0:T(8,128)(2,1)}, u32[]{:S(2)}, u32[]{:S(2)}) %collective-permute-start.10) | collective-permute-done | bytes 786464 | tf_op jit(solution)/shard_map/ppermute | solution.py:347
  125.1 6.7 %collective-permute-start.11 = (bf16[48,64,128]{2,1,0:T(8,128)(2,1)}, bf16[48,64,128]{2,1,0:T(8,128)(2,1)}, u32[]{:S(2)}, u32[]{:S(2)}) collective-permute-start(bf16[48,64,128]{2,1,0:T(8,128)(2,1)} %collective-permute-done.10), channel_id=1, source_target_pairs={{20,16},{22,24},{28,18},{30,26},{0,4},{2,12},{8,6},{10,14},{21,17}... | collective-permute-start | bytes 2359304 | tf_op jit(solution)/shard_map/ppermute | solution.py:350
  132.0 2.8 %multiply_convert_fusion = bf16[64,128,64]{2,1,0:T(8,128)(2,1)S(1)} fusion(s32[64,128]{1,0:T(8,128)S(1)} %copy.65, s32[64,128]{1,0:T(8,128)S(1)} %get-tuple-element.86), kind=kLoop, calls=%fused_computation | loop fusion | flops 3670016 | bytes 1114112 | tf_op jit(solution)/shard_map/convert.13
  134.8 2.8 %multiply_convert_fusion.1 = bf16[64,128,64]{2,1,0:T(8,128)(2,1)S(1)} fusion(s32[64,128]{1,0:T(8,128)S(1)} %copy.64, s32[64,128]{1,0:T(8,128)S(1)} %get-tuple-element.85), kind=kLoop, calls=%fused_computation.3 | loop fusion | flops 3670016 | bytes 1114112 | tf_op jit(solution)/shard_map/convert.12
  137.6 2.5 pad_maximum_fusion.refs_4_
  140.0 15.7 %collective-permute-done.12.refs_3_ = bf16[48,64,128]{2,1,0:T(8,128)(2,1)S(1)} collective-permute-done((bf16[48,64,128]{2,1,0:T(8,128)(2,1)}, bf16[48,64,128]{2,1,0:T(8,128)(2,1)S(1)}, u32[]{:S(2)}, u32[]{:S(2)}) %collective-permute-start.12) | collective-permute-done | bytes 786464 | tf_op jit(solution)/shard_map/ppermute | solution.py:349
  157.1 14.0 %loss.1 = (f32[2,64,128,128]{3,2,1,0:T(8,128)}, bf16[64,128,128]{2,1,0:T(8,128)(2,1)}, bf16[8,64,128]{2,1,0:T(8,128)(2,1)}, bf16[8,64,128]{2,1,0:T(8,128)(2,1)},...) custom-call(bf16[64,128,128]{2,1,0:T(8,128)(2,1)} %get-tuple-element.51.refs_0_, ...), custom_call_target="tpu_custom_call" | custom-call | flops 536870912 | bytes 37748736 | tf_op jit(solution)/shard_map/loss/pallas_call | solution.py:442
  171.1 21.4 %collective-permute-start.13 = (bf16[8,64,128]{2,1,0:T(8,128)(2,1)}, bf16[8,64,128]{2,1,0:T(8,128)(2,1)S(1)}, u32[]{:S(2)}, u32[]{:S(2)}) collective-permute-start(bf16[8,64,128]{2,1,0:T(8,128)(2,1)} %get-tuple-element.57), channel_id=1, source_target_pairs={{0,8},{8,16},{16,24},{1,9},{9,17},{17,25},{2,10},{10,18},{18,26},{... | collective-permute-start | bytes 393224 | tf_op jit(solution)/shard_map/ppermute | solution.py:296
  192.5 1.9 collective-permute-start.14
  194.8 4.2 %collective-permute-done.14.refs_2_ = bf16[8,64,128]{2,1,0:T(8,128)(2,1)S(1)} collective-permute-done((bf16[8,64,128]{2,1,0:T(8,128)(2,1)}, bf16[8,64,128]{2,1,0:T(8,128)(2,1)S(1)}, u32[]{:S(2)}, u32[]{:S(2)}) %collective-permute-start.14) | collective-permute-done | bytes 131104 | tf_op jit(solution)/shard_map/ppermute | solution.py:296
  200.0 2.1 collective-permute-start.15
  203.1 1.5 collective-permute-start.16
  207.0 2.1 collective-permute-done.16.refs_4_
  209.8 18.5 %back.1 = (f32[2,64,128,128]{3,2,1,0:T(8,128)}, bf16[64,128,128]{2,1,0:T(8,128)(2,1)}, bf16[4,64,128]{2,1,0:T(8,128)(2,1)}, bf16[4,64,128]{2,1,0:T(8,128)(2,1)},...) custom-call(bf16[64,128,128]{2,1,0:T(8,128)(2,1)} %get-tuple-element.56.refs_0_, bf16[8,64,128]{2,1,0:T(8,128)(2,1)} %copy-done.6, ...), custom_call_target="tpu_custom_call" | custom-call | flops 1744830464 | bytes 41943040 | tf_op jit(solution)/shard_map/back/pallas_call | solution.py:442
  228.3 3.3 %collective-permute-start.17 = (bf16[4,64,128]{2,1,0:T(8,128)(2,1)}, bf16[4,64,128]{2,1,0:T(8,128)(2,1)S(1)}, u32[]{:S(2)}, u32[]{:S(2)}) collective-permute-start(bf16[4,64,128]{2,1,0:T(8,128)(2,1)} %get-tuple-element.64), channel_id=1, source_target_pairs={{0,8},{8,16},{16,24},{1,9},{9,17},{17,25},{2,10},{10,18},{18,26},{... | collective-permute-start | bytes 196616 | tf_op jit(solution)/shard_map/ppermute | solution.py:296
  231.6 1.9 collective-permute-start.18
  233.6 3.8 %collective-permute-done.18.refs_2_ = bf16[4,64,128]{2,1,0:T(8,128)(2,1)S(1)} collective-permute-done((bf16[4,64,128]{2,1,0:T(8,128)(2,1)}, bf16[4,64,128]{2,1,0:T(8,128)(2,1)S(1)}, u32[]{:S(2)}, u32[]{:S(2)}) %collective-permute-start.18) | collective-permute-done | bytes 65568 | tf_op jit(solution)/shard_map/ppermute | solution.py:296
  238.4 2.6 collective-permute-start.19
  241.9 1.3 collective-permute-start.20
  243.2 1.1 mul.114.refs_5_
  244.9 2.9 %collective-permute-done.20.refs_4_ = bf16[72,8,128]{2,1,0:T(8,128)(2,1)S(1)} collective-permute-done((bf16[72,8,128]{2,1,0:T(8,128)(2,1)S(1)}, bf16[72,8,128]{2,1,0:T(8,128)(2,1)S(1)}, u32[]{:S(2)}, u32[]{:S(2)}) %collective-permute-start.20) | collective-permute-done | bytes 147488 | tf_op jit(solution)/shard_map/ppermute | solution.py:296
  248.5 17.2 %final.1 = f32[2,64,128,128]{3,2,1,0:T(8,128)} custom-call(bf16[64,128,128]{2,1,0:T(8,128)(2,1)} %get-tuple-element.63.refs_0_, bf16[4,64,128]{2,1,0:T(8,128)(2,1)} %copy-done.20, bf16[4,64,128]{2,1,0:T(8,128)(2,1)} %copy-done.21, bf16[72,8,128]{2,1,0:T(8,128)(2,1)} %copy-done.16, bf16[72,8,128]{2,1,0:T(8,128)(2,1)} %copy-done.17, ...), custom_call_target="tpu_custom_call" | custom-call | flops 1744830464 | bytes 33554432 | tf_op jit(solution)/shard_map/final/pallas_call | solution.py:442
  (126 shorter events, 26.6 us)
Async XLA Ops:
  0.0 0.8 copy-start
  0.0 26.5 %copy-start.23 = (bf16[2,64,128]{2,1,0:T(8,128)(2,1)S(1)}, bf16[2,64,128]{2,1,0:T(8,128)(2,1)}, u32[]{:S(2)}) copy-start(bf16[2,64,128]{2,1,0:T(8,128)(2,1)} %param.13) | copy-start | bytes 98308
  0.0 27.4 %copy-start.4 = (bf16[2,3,3,64,64]{4,3,2,1,0:T(8,128)(2,1)S(1)}, bf16[2,3,3,64,64]{4,3,2,1,0:T(8,128)(2,1)}, u32[]{:S(2)}) copy-start(bf16[2,3,3,64,64]{4,3,2,1,0:T(8,128)(2,1)} %param.12) | copy-start | bytes 442372
  1.5 39.5 %all-to-all-start = ((s32[32,4,128]{2,0,1:T(8,128)}), s32[32,4,128]{2,0,1:T(8,128)S(1)}, u32[]{:S(2)}, u32[]{:S(2)}) async-start(s32[32,4,128]{2,0,1:T(8,128)} %copy_bitcast_fusion), calls=%async_computation | async-start | bytes 131072 | tf_op jit(solution)/shard_map/all_to_all | solution.py:469
  19.8 12.5 %copy-start.19 = (bf16[64,8,128]{2,1,0:T(8,128)(2,1)S(1)}, bf16[64,8,128]{2,1,0:T(8,128)(2,1)}, u32[]{:S(2)}) copy-start(bf16[64,8,128]{2,1,0:T(8,128)(2,1)} %get-tuple-element.41) | copy-start | bytes 393220
  19.9 16.1 %copy-start.18 = (bf16[64,8,128]{2,1,0:T(8,128)(2,1)S(1)}, bf16[64,8,128]{2,1,0:T(8,128)(2,1)}, u32[]{:S(2)}) copy-start(bf16[64,8,128]{2,1,0:T(8,128)(2,1)} %get-tuple-element.42) | copy-start | bytes 393220
  19.9 17.6 %copy-start.13 = (bf16[128,64]{0,1:T(8,128)(2,1)S(1)}, bf16[128,64]{0,1:T(8,128)(2,1)}, u32[]{:S(2)}) copy-start(bf16[128,64]{0,1:T(8,128)(2,1)} %param.14) | copy-start | bytes 49156
  19.9 11.0 %collective-permute-start = (bf16[4,64,128]{2,1,0:T(8,128)(2,1)}, bf16[4,64,128]{2,1,0:T(8,128)(2,1)}, u32[]{:S(2)}, u32[]{:S(2)}) collective-permute-start(bf16[4,64,128]{2,1,0:T(8,128)(2,1)} %get-tuple-element.39), channel_id=1, source_target_pairs={{0,8},{8,16},{16,24},{1,9},{9,17},{17,25},{2,10},{10,18},{18,26},{... | collective-permute-start | bytes 196616 | tf_op jit(solution)/shard_map/ppermute | solution.py:296
  24.0 7.6 %collective-permute-start.1 = (bf16[4,64,128]{2,1,0:T(8,128)(2,1)}, bf16[4,64,128]{2,1,0:T(8,128)(2,1)}, u32[]{:S(2)}, u32[]{:S(2)}) collective-permute-start(bf16[4,64,128]{2,1,0:T(8,128)(2,1)} %get-tuple-element.40), channel_id=1, source_target_pairs={{8,0},{16,8},{24,16},{9,1},{17,9},{25,17},{10,2},{18,10},{26,18},{... | collective-permute-start | bytes 196616 | tf_op jit(solution)/shard_map/ppermute | solution.py:296
  27.3 3.5 %copy-start.25 = (f32[64]{0:T(128)S(1)}, f32[64]{0:T(128)}, u32[]{:S(2)}) copy-start(f32[64]{0:T(128)} %broadcast_multiply_fusion.5) | copy-start | bytes 772
  32.3 8.6 %collective-permute-start.2 = (bf16[72,8,128]{2,1,0:T(8,128)(2,1)S(1)}, bf16[72,8,128]{2,1,0:T(8,128)(2,1)S(1)}, u32[]{:S(2)}, u32[]{:S(2)}) collective-permute-start(bf16[72,8,128]{2,1,0:T(8,128)(2,1)S(1)} %pad_maximum_fusion.5), channel_id=1, source_target_pairs={{0,2},{2,4},{4,6},{1,3},{3,5},{5,7},{8,10},{10,12},{12,14},{9,11},... | collective-permute-start | bytes 442376 | tf_op jit(solution)/shard_map/ppermute | solution.py:296
  36.0 6.4 %collective-permute-start.3 = (bf16[72,8,128]{2,1,0:T(8,128)(2,1)S(1)}, bf16[72,8,128]{2,1,0:T(8,128)(2,1)S(1)}, u32[]{:S(2)}, u32[]{:S(2)}) collective-permute-start(bf16[72,8,128]{2,1,0:T(8,128)(2,1)S(1)} %pad_maximum_fusion.6), channel_id=1, source_target_pairs={{2,0},{4,2},{6,4},{3,1},{5,3},{7,5},{10,8},{12,10},{14,12},{11,9},... | collective-permute-start | bytes 442376 | tf_op jit(solution)/shard_map/ppermute | solution.py:296
  40.9 37.5 %copy-start.24 = (f32[128]{0:T(128)S(1)}, f32[128]{0:T(128)}, u32[]{:S(2)}) copy-start(f32[128]{0:T(128)} %get-tuple-element.105) | copy-start | bytes 1540
  41.0 1.5 copy-start.14
  43.1 39.4 %copy-start.26 = (f32[64]{0:T(128)S(1)}, f32[64]{0:T(128)}, u32[]{:S(2)}) copy-start(f32[64]{0:T(128)} %param.15) | copy-start | bytes 772
  60.3 7.3 %collective-permute-start.5 = (bf16[8,64,128]{2,1,0:T(8,128)(2,1)}, bf16[8,64,128]{2,1,0:T(8,128)(2,1)S(1)}, u32[]{:S(2)}, u32[]{:S(2)}) collective-permute-start(bf16[8,64,128]{2,1,0:T(8,128)(2,1)} %get-tuple-element.46), channel_id=1, source_target_pairs={{0,8},{8,16},{16,24},{1,9},{9,17},{17,25},{2,10},{10,18},{18,26},{... | collective-permute-start | bytes 393224 | tf_op jit(solution)/shard_map/ppermute | solution.py:296
  65.6 6.5 %collective-permute-start.6 = (bf16[8,64,128]{2,1,0:T(8,128)(2,1)}, bf16[8,64,128]{2,1,0:T(8,128)(2,1)S(1)}, u32[]{:S(2)}, u32[]{:S(2)}) collective-permute-start(bf16[8,64,128]{2,1,0:T(8,128)(2,1)} %get-tuple-element.47), channel_id=1, source_target_pairs={{8,0},{16,8},{24,16},{9,1},{17,9},{25,17},{10,2},{18,10},{26,18},{... | collective-permute-start | bytes 393224 | tf_op jit(solution)/shard_map/ppermute | solution.py:296
  67.5 18.5 %copy-start.5 = (bf16[8,64,128]{2,1,0:T(8,128)(2,1)}, bf16[8,64,128]{2,1,0:T(8,128)(2,1)S(1)}, u32[]{:S(2)}) copy-start(bf16[8,64,128]{2,1,0:T(8,128)(2,1)S(1)} %collective-permute-done.5.refs_1_) | copy-start | bytes 393220
  72.1 13.9 %copy-start.7 = (bf16[8,64,128]{2,1,0:T(8,128)(2,1)}, bf16[8,64,128]{2,1,0:T(8,128)(2,1)S(1)}, u32[]{:S(2)}) copy-start(bf16[8,64,128]{2,1,0:T(8,128)(2,1)S(1)} %collective-permute-done.6.refs_2_) | copy-start | bytes 393220
  73.1 12.9 %collective-permute-start.7 = (bf16[80,8,128]{2,1,0:T(8,128)(2,1)S(1)}, bf16[80,8,128]{2,1,0:T(8,128)(2,1)S(1)}, u32[]{:S(2)}, u32[]{:S(2)}) collective-permute-start(bf16[80,8,128]{2,1,0:T(8,128)(2,1)S(1)} %pad_maximum_fusion.1), channel_id=1, source_target_pairs={{0,2},{2,4},{4,6},{1,3},{3,5},{5,7},{8,10},{10,12},{12,14},{9,11},... | collective-permute-start | bytes 491528 | tf_op jit(solution)/shard_map/ppermute | solution.py:296
  77.1 8.9 %collective-permute-start.8 = (bf16[80,8,128]{2,1,0:T(8,128)(2,1)S(1)}, bf16[80,8,128]{2,1,0:T(8,128)(2,1)S(1)}, u32[]{:S(2)}, u32[]{:S(2)}) collective-permute-start(bf16[80,8,128]{2,1,0:T(8,128)(2,1)S(1)} %pad_maximum_fusion.2), channel_id=1, source_target_pairs={{2,0},{4,2},{6,4},{3,1},{5,3},{7,5},{10,8},{12,10},{14,12},{11,9},... | collective-permute-start | bytes 491528 | tf_op jit(solution)/shard_map/ppermute | solution.py:296
  80.4 5.6 %collective-permute-start.4 = (s32[128,128]{1,0:T(8,128)S(1)}, s32[128,128]{1,0:T(8,128)S(1)}, u32[]{:S(2)}, u32[]{:S(2)}) collective-permute-start(s32[128,128]{1,0:T(8,128)S(1)} %bitcast.62), channel_id=1, source_target_pairs={{0,0},{2,8},{4,16},{6,24},{8,2},{10,10},{12,18},{14,26},{16,4},{18... | collective-permute-start | bytes 196616 | tf_op jit(solution)/shard_map/ppermute | solution.py:312
  86.0 0.7 copy-start.11
  86.0 0.7 copy-start.12
  105.3 19.8 %collective-permute-start.10 = (bf16[48,64,128]{2,1,0:T(8,128)(2,1)}, bf16[48,64,128]{2,1,0:T(8,128)(2,1)}, u32[]{:S(2)}, u32[]{:S(2)}) collective-permute-start(bf16[48,64,128]{2,1,0:T(8,128)(2,1)} %slice.139), channel_id=1, source_target_pairs={{4,20},{6,22},{12,28},{14,30},{16,0},{18,2},{24,8},{26,10},{5,21},... | collective-permute-start | bytes 2359304 | tf_op jit(solution)/shard_map/ppermute | solution.py:347
  109.2 46.6 %collective-permute-start.9 = (bf16[80,64,128]{2,1,0:T(8,128)(2,1)}, bf16[80,64,128]{2,1,0:T(8,128)(2,1)S(1)}, u32[]{:S(2)}, u32[]{:S(2)}) collective-permute-start(bf16[80,64,128]{2,1,0:T(8,128)(2,1)} %slice.138), channel_id=1, source_target_pairs={{0,0},{2,8},{4,16},{6,24},{8,2},{10,10},{12,18},{14,26},{16,4},{18... | collective-permute-start | bytes 3932168 | tf_op jit(solution)/shard_map/ppermute | solution.py:348
  112.5 43.3 %collective-permute-start.12 = (bf16[48,64,128]{2,1,0:T(8,128)(2,1)}, bf16[48,64,128]{2,1,0:T(8,128)(2,1)S(1)}, u32[]{:S(2)}, u32[]{:S(2)}) collective-permute-start(bf16[48,64,128]{2,1,0:T(8,128)(2,1)} %slice.139), channel_id=1, source_target_pairs={{0,0},{2,8},{8,2},{10,10},{20,20},{22,28},{28,22},{30,30},{1,1},{3... | collective-permute-start | bytes 2359304 | tf_op jit(solution)/shard_map/ppermute | solution.py:349
  125.1 30.7 %collective-permute-start.11 = (bf16[48,64,128]{2,1,0:T(8,128)(2,1)}, bf16[48,64,128]{2,1,0:T(8,128)(2,1)}, u32[]{:S(2)}, u32[]{:S(2)}) collective-permute-start(bf16[48,64,128]{2,1,0:T(8,128)(2,1)} %collective-permute-done.10), channel_id=1, source_target_pairs={{20,16},{22,24},{28,18},{30,26},{0,4},{2,12},{8,6},{10,14},{21,17}... | collective-permute-start | bytes 2359304 | tf_op jit(solution)/shard_map/ppermute | solution.py:350
  155.7 0.9 copy-start.3
  155.8 1.4 copy-start.2
  157.1 49.3 %copy-start.22 = (bf16[64,128]{1,0:T(8,128)(2,1)S(1)}, bf16[64,128]{1,0:T(8,128)(2,1)}, u32[]{:S(2)}) copy-start(bf16[64,128]{1,0:T(8,128)(2,1)} %get-tuple-element.98) | copy-start | bytes 49156
  171.1 23.7 %collective-permute-start.13 = (bf16[8,64,128]{2,1,0:T(8,128)(2,1)}, bf16[8,64,128]{2,1,0:T(8,128)(2,1)S(1)}, u32[]{:S(2)}, u32[]{:S(2)}) collective-permute-start(bf16[8,64,128]{2,1,0:T(8,128)(2,1)} %get-tuple-element.57), channel_id=1, source_target_pairs={{0,8},{8,16},{16,24},{1,9},{9,17},{17,25},{2,10},{10,18},{18,26},{... | collective-permute-start | bytes 393224 | tf_op jit(solution)/shard_map/ppermute | solution.py:296
  192.5 6.5 %collective-permute-start.14 = (bf16[8,64,128]{2,1,0:T(8,128)(2,1)}, bf16[8,64,128]{2,1,0:T(8,128)(2,1)S(1)}, u32[]{:S(2)}, u32[]{:S(2)}) collective-permute-start(bf16[8,64,128]{2,1,0:T(8,128)(2,1)} %get-tuple-element.58), channel_id=1, source_target_pairs={{8,0},{16,8},{24,16},{9,1},{17,9},{25,17},{10,2},{18,10},{26,18},{... | collective-permute-start | bytes 393224 | tf_op jit(solution)/shard_map/ppermute | solution.py:296
  194.8 14.3 %copy-start.6 = (bf16[8,64,128]{2,1,0:T(8,128)(2,1)}, bf16[8,64,128]{2,1,0:T(8,128)(2,1)S(1)}, u32[]{:S(2)}) copy-start(bf16[8,64,128]{2,1,0:T(8,128)(2,1)S(1)} %collective-permute-done.13.refs_1_) | copy-start | bytes 393220
  199.0 10.1 %copy-start.8 = (bf16[8,64,128]{2,1,0:T(8,128)(2,1)}, bf16[8,64,128]{2,1,0:T(8,128)(2,1)S(1)}, u32[]{:S(2)}) copy-start(bf16[8,64,128]{2,1,0:T(8,128)(2,1)S(1)} %collective-permute-done.14.refs_2_) | copy-start | bytes 393220
  200.0 7.0 %collective-permute-start.15 = (bf16[80,8,128]{2,1,0:T(8,128)(2,1)S(1)}, bf16[80,8,128]{2,1,0:T(8,128)(2,1)S(1)}, u32[]{:S(2)}, u32[]{:S(2)}) collective-permute-start(bf16[80,8,128]{2,1,0:T(8,128)(2,1)S(1)} %pad_maximum_fusion.3), channel_id=1, source_target_pairs={{0,2},{2,4},{4,6},{1,3},{3,5},{5,7},{8,10},{10,12},{12,14},{9,11},... | collective-permute-start | bytes 491528 | tf_op jit(solution)/shard_map/ppermute | solution.py:296
  203.1 6.1 %collective-permute-start.16 = (bf16[80,8,128]{2,1,0:T(8,128)(2,1)S(1)}, bf16[80,8,128]{2,1,0:T(8,128)(2,1)S(1)}, u32[]{:S(2)}, u32[]{:S(2)}) collective-permute-start(bf16[80,8,128]{2,1,0:T(8,128)(2,1)S(1)} %pad_maximum_fusion.4), channel_id=1, source_target_pairs={{2,0},{4,2},{6,4},{3,1},{5,3},{7,5},{10,8},{12,10},{14,12},{11,9},... | collective-permute-start | bytes 491528 | tf_op jit(solution)/shard_map/ppermute | solution.py:296
  207.0 2.1 copy-start.9
  209.1 0.7 copy-start.10
  228.3 5.3 %collective-permute-start.17 = (bf16[4,64,128]{2,1,0:T(8,128)(2,1)}, bf16[4,64,128]{2,1,0:T(8,128)(2,1)S(1)}, u32[]{:S(2)}, u32[]{:S(2)}) collective-permute-start(bf16[4,64,128]{2,1,0:T(8,128)(2,1)} %get-tuple-element.64), channel_id=1, source_target_pairs={{0,8},{8,16},{16,24},{1,9},{9,17},{17,25},{2,10},{10,18},{18,26},{... | collective-permute-start | bytes 196616 | tf_op jit(solution)/shard_map/ppermute | solution.py:296
  231.6 5.8 %collective-permute-start.18 = (bf16[4,64,128]{2,1,0:T(8,128)(2,1)}, bf16[4,64,128]{2,1,0:T(8,128)(2,1)S(1)}, u32[]{:S(2)}, u32[]{:S(2)}) collective-permute-start(bf16[4,64,128]{2,1,0:T(8,128)(2,1)} %get-tuple-element.65), channel_id=1, source_target_pairs={{8,0},{16,8},{24,16},{9,1},{17,9},{25,17},{10,2},{18,10},{26,18},{... | collective-permute-start | bytes 196616 | tf_op jit(solution)/shard_map/ppermute | solution.py:296
  233.6 14.2 %copy-start.20 = (bf16[4,64,128]{2,1,0:T(8,128)(2,1)}, bf16[4,64,128]{2,1,0:T(8,128)(2,1)S(1)}, u32[]{:S(2)}) copy-start(bf16[4,64,128]{2,1,0:T(8,128)(2,1)S(1)} %collective-permute-done.17.refs_1_) | copy-start | bytes 196612
  237.4 10.4 %copy-start.21 = (bf16[4,64,128]{2,1,0:T(8,128)(2,1)}, bf16[4,64,128]{2,1,0:T(8,128)(2,1)S(1)}, u32[]{:S(2)}) copy-start(bf16[4,64,128]{2,1,0:T(8,128)(2,1)S(1)} %collective-permute-done.18.refs_2_) | copy-start | bytes 196612
  238.4 6.5 %collective-permute-start.19 = (bf16[72,8,128]{2,1,0:T(8,128)(2,1)S(1)}, bf16[72,8,128]{2,1,0:T(8,128)(2,1)S(1)}, u32[]{:S(2)}, u32[]{:S(2)}) collective-permute-start(bf16[72,8,128]{2,1,0:T(8,128)(2,1)S(1)} %pad_maximum_fusion.7), channel_id=1, source_target_pairs={{0,2},{2,4},{4,6},{1,3},{3,5},{5,7},{8,10},{10,12},{12,14},{9,11},... | collective-permute-start | bytes 442376 | tf_op jit(solution)/shard_map/ppermute | solution.py:296
  241.9 5.9 %collective-permute-start.20 = (bf16[72,8,128]{2,1,0:T(8,128)(2,1)S(1)}, bf16[72,8,128]{2,1,0:T(8,128)(2,1)S(1)}, u32[]{:S(2)}, u32[]{:S(2)}) collective-permute-start(bf16[72,8,128]{2,1,0:T(8,128)(2,1)S(1)} %pad_maximum_fusion.8), channel_id=1, source_target_pairs={{2,0},{4,2},{6,4},{3,1},{5,3},{7,5},{10,8},{12,10},{14,12},{11,9},... | collective-permute-start | bytes 442376 | tf_op jit(solution)/shard_map/ppermute | solution.py:296
  244.9 2.9 %copy-start.16 = (bf16[72,8,128]{2,1,0:T(8,128)(2,1)}, bf16[72,8,128]{2,1,0:T(8,128)(2,1)S(1)}, u32[]{:S(2)}) copy-start(bf16[72,8,128]{2,1,0:T(8,128)(2,1)S(1)} %collective-permute-done.19.refs_3_) | copy-start | bytes 442372
  247.8 0.6 copy-start.17
  248.4 17.2 %copy-start.1 = (s32[32,512]{1,0:T(8,128)S(1)}, s32[32,512]{1,0:T(8,128)}, u32[]{:S(2)}) copy-start(s32[32,512]{1,0:T(8,128)} %param.9) | copy-start | bytes 196612
  (1 other events, 0.6 us)

commit v4 on v3

--- a/solution.py
+++ b/solution.py
@@ -76,14 +76,18 @@
     low = lane_low((count, middle, values.shape[2]))
     taken = spacing // count
 
-    @pl.when(step < taken)
+    @pl.when((step < taken) & (top is not None))
     def _():
+        if top is None:
+            return
         sent = values[:count]
         rows = pl.ds(jnp.minimum(step, taken - 1) * count, count)
         top[rows] = jnp.where(low, sent[:, :middle], swapped(sent[:, middle:])).astype(BF16)
 
-    @pl.when(step >= steps - taken)
+    @pl.when((step >= steps - taken) & (bottom is not None))
     def _():
+        if bottom is None:
+            return
         sent = values[ROWS - count :]
         rows = pl.ds(jnp.maximum(step - (steps - taken), 0) * count, count)
         bottom[rows] = jnp.where(low, swapped(sent[:, :middle]), sent[:, middle:]).astype(BF16)
@@ -149,7 +153,7 @@
     return reference[...].reshape(-1, reference.shape[-1])
 
 
-def over_strips(body, kinds, *refs):
+def over_strips(body, kinds, first, *refs):
     inner = BLOCK // ROWS
 
     def one(place, carry):
@@ -157,7 +161,7 @@
         views = []
         for kind, ref in zip(kinds, refs):
             views.append(ref.at[:, rows] if kind == "halves" else ref.at[rows] if kind == "rows" else ref)
-        body(pl.program_id(0) * inner + place, *views)
+        body((pl.program_id(0) + first) * inner + place, *views)
         return carry
 
     lax.fori_loop(0, inner, one, 0)
@@ -191,7 +195,7 @@
 
 def head_kernel(near, steps, step, centre, *rest):
     halos, rest = rest[:4], rest[4:]
-    stream_in, ones, kernel, up, gain, head, bias, stream_out, activated_out, by_row, by_column, padded, taps = rest
+    stream_in, ones, kernel, up, gain, head, bias, stream_out, activated_out, by_row, *by_column, padded, taps = rest
     columns = centre.shape[1]
 
     @pl.when(step == 0)
@@ -209,23 +213,25 @@
     by_row[...] = logits.astype(BF16).reshape(by_row.shape)
     pairs = jnp.concatenate([entered[:, :, : columns // 2], entered[:, :, columns // 2 :]], axis=3)
     logits = jnp.dot(pairs.reshape(ROWS * columns, -1), head[...], preferred_element_type=F32) + bias[...]
-    by_column[...] = logits.astype(BF16).reshape(by_column.shape)
-
-
-def loss_kernel(
-    spacing, steps, inner, pieces, step, by_row, *rest
-):
-    facing, rest = rest[: sum(pieces)], rest[sum(pieces) :]
-    targets, stream, activated, ones, head, group, up, grad_out, conv_out, *rest = rest
-    edges, (turned,) = rest[:4], rest[4:]
+    logits = logits.astype(BF16).reshape(2, ROWS, columns // 2, -1)
+    place = 0
+    for piece in by_column:
+        piece[...] = logits[:, :, place : place + piece.shape[2]]
+        place += piece.shape[2]
+
+
+def loss_kernel(spacing, steps, inner, count, ends, step, by_row, *rest):
+    facing, rest = rest[:count], rest[count:]
+    targets, stream, activated, ones, head, group, up, *rest = rest
+    *outputs, turned = rest
+    grad_out, conv_out, left, right, *far = outputs[-4 - sum(ends) :]
+    top = far[0] if ends[0] else None
+    bottom = far[-1] if ends[1] else None
+    edges = top, bottom, left, right
 
     @pl.when(step % inner == 0)
     def _():
-        place = taken = 0
-        for count in pieces:
-            piece = sum(array[...].astype(F32) for array in facing[taken : taken + count])
-            turned[:, place : place + piece.shape[0]] = jnp.swapaxes(piece, 0, 1)
-            place, taken = place + piece.shape[0], taken + count
+        turned[...] = jnp.swapaxes(sum(array[...].astype(F32) for array in facing), 0, 1)
 
     start = (step % inner) * ROWS
     columns, lanes = by_row.shape[1:]
@@ -335,36 +341,28 @@
 def facing_logits(by_column):
     rows, cols = lax.axis_size("row"), lax.axis_size("col")
     if rows == cols and rows % 2 == 0:
-        cut = by_column.shape[0] * 5 // 128 * 16
-        straight, around = by_column[:cut], by_column[cut:]
+        straight, *around = by_column
         places = [(row, col) for row in range(rows) for col in range(cols)]
         part = rows // 2
         far = [(row, col) for row, col in places if row // part != col // part]
         close = [(row, col) for row, col in places if row // part == col // part]
-        both = ("row", "col")
         number = lambda row, col: row * cols + col
         other = lambda row: (row + part) % rows
-        hop = lax.ppermute(around, both, [(number(row, col), number(other(row), col)) for row, col in far])
-        straight = lax.ppermute(straight, both, [(number(row, col), number(col, row)) for row, col in places])
-        near = lax.ppermute(around, both, [(number(row, col), number(col, row)) for row, col in close])
-        hop = lax.ppermute(hop, both, [(number(other(row), col), number(col, row)) for row, col in far])
-        return [[straight], [hop, near]]
+        move = lambda array, pairs: lax.ppermute(array, ("row", "col"), pairs)
+        hops = [move(array, [(number(row, col), number(other(row), col)) for row, col in far]) for array in around]
+        straight = move(straight, [(number(row, col), number(col, row)) for row, col in places])
+        near = [move(array, [(number(row, col), number(col, row)) for row, col in close]) for array in around]
+        hops = [move(array, [(number(other(row), col), number(col, row)) for row, col in far]) for array in hops]
+        return [[straight]] + [list(pair) for pair in zip(hops, near)]
+    tile = jnp.concatenate(by_column, axis=1)
     if rows == cols:
-        return [[facing_tile(by_column)]]
-    bins = by_column.shape[2] // 2
-    tile = facing_tile(jnp.concatenate([by_column[..., :bins], by_column[..., bins:]], axis=1))
-    half = tile.shape[1] // 2
-    return [[jnp.concatenate([tile[:, :half], tile[:, half:]], axis=2)]]
-
-
-def dilated_weights(kernel):
-    both = jnp.eye(2, dtype=kernel.dtype)[None, :, None, None, :, None]
-    spread = jnp.transpose(kernel, (0, 2, 1, 3))[:, None, :, :, None, :] * both
-    return spread.reshape(6 * kernel.shape[2], 6 * kernel.shape[3])
-
-
-def mirrored(kernel):
-    return jnp.swapaxes(kernel[::-1, ::-1], 2, 3)
+        tile = facing_tile(tile)
+    else:
+        bins = tile.shape[2] // 2
+        tile = facing_tile(jnp.concatenate([tile[..., :bins], tile[..., bins:]], axis=1))
+        half = tile.shape[1] // 2
+        tile = jnp.concatenate([tile[:, :half], tile[:, half:]], axis=2)
+    return [[tile]]
 
 
 def diagonal(weight):
@@ -374,10 +372,65 @@
     )
 
 
+def dilated_weights(blocks):
+    return jnp.concatenate(
+        [jnp.concatenate([diagonal(block) for block in line], axis=1) for line in blocks], axis=0
+    )
+
+
 def two_parts(weight):
     centred = weight - jnp.mean(weight, axis=1, keepdims=True)
-    upper = lax.reduce_precision(centred, 8, 7)
-    return jnp.concatenate([diagonal(upper), diagonal(centred - upper)], axis=0).astype(BF16)
+    upper = centred.astype(BF16).astype(F32)
+    return jnp.concatenate([diagonal(upper), diagonal(centred - upper)], axis=0)
+
+
+def derived(norm_gain, w_down, w_conv, w_up, w_head, head_bias):
+    channels, bins = w_head.shape
+    gains = [norm_gain[index : index + 1] * math.sqrt(channels) for index in range(3)]
+    down = [w_down[index].astype(F32) for index in range(2)]
+    up = [w_up[index].astype(F32) for index in range(2)]
+    conv = [[[w_conv[index, row, col].astype(F32) for col in range(3)] for row in range(3)] for index in range(2)]
+    back = [[[conv[index][2 - row][2 - col].T for col in range(3)] for row in range(3)] for index in range(2)]
+    head = w_head[...].astype(F32)
+    first = lax.broadcasted_iota(jnp.int32, (channels, channels), 0)
+    second = lax.broadcasted_iota(jnp.int32, (channels, channels), 1)
+    matrices = dict(
+        downs=[diagonal(weight) for weight in down],
+        downs_back=[diagonal(weight.T) for weight in down],
+        ups=[two_parts(weight) for weight in up],
+        ups_back=[diagonal(weight.T) for weight in up],
+        convs=[dilated_weights(blocks) for blocks in conv],
+        convs_back=[dilated_weights(blocks) for blocks in back],
+        head=diagonal(head),
+        head_back=two_parts(head.T * gains[2]),
+        group=diagonal(jnp.ones((bins, bins), F32)),
+        centring=jnp.where(first == second, 1.0, 0.0) - 1.0 / channels,
+        ones=jnp.ones((channels, channels), F32),
+    )
+    matrices = jax.tree.map(lambda array: array.astype(BF16), matrices)
+    bias = head_bias[...]
+    return dict(matrices, gains=gains, bias=jnp.concatenate([bias, bias], axis=1))
+
+
+def derive(*sources):
+    shapes = jax.eval_shape(derived, *sources)
+    leaves, tree = jax.tree.flatten(shapes)
+
+    def kernel(*refs):
+        results = jax.tree.leaves(derived(*refs[: len(sources)]))
+        for ref, result in zip(refs[len(sources) :], results):
+            ref[...] = result
+
+    made = pl.pallas_call(
+        kernel,
+        grid=(1,),
+        in_specs=[pl.BlockSpec(array.shape, lambda step, rank=array.ndim: (0,) * rank) for array in sources],
+        out_specs=[pl.BlockSpec(leaf.shape, lambda step: (0, 0)) for leaf in leaves],
+        out_shape=leaves,
+        compiler_params=pltpu.CompilerParams(vmem_limit_bytes=60 * 1024 * 1024),
+        name="weights",
+    )(*sources)
+    return jax.tree.unflatten(tree, made)
 
 
 def shards(features, labels, norm_gain, w_down, w_conv, w_up, w_head, head_bias):
@@ -389,19 +442,10 @@
     lanes = 2 * narrow
     near, far = 4, 8
 
-    gains = [norm_gain[index : index + 1] * math.sqrt(channels) for index in range(3)]
-    downs = [diagonal(w_down[index]) for index in range(2)]
-    downs_back = [diagonal(w_down[index].T) for index in range(2)]
-    centring = (jnp.eye(channels) - 1.0 / channels).astype(BF16)
-    ones = jnp.ones((channels, channels), BF16)
-    ups = [two_parts(w_up[index].astype(F32)) for index in range(2)]
-    ups_back = [diagonal(w_up[index].T) for index in range(2)]
-    convs = [dilated_weights(w_conv[index]) for index in range(2)]
-    convs_back = [dilated_weights(mirrored(w_conv[index])) for index in range(2)]
-    head = diagonal(w_head)
-    head_back = two_parts(w_head.T.astype(F32) * gains[2])
-    bias = jnp.concatenate([head_bias, head_bias])[None]
-    group = diagonal(jnp.ones((bins, bins), BF16))
+    made = derive(norm_gain, w_down, w_conv, w_up, w_head, head_bias[None])
+    gains, bias, centring, ones, group = (made[name] for name in ("gains", "bias", "centring", "ones", "group"))
+    downs, downs_back, ups, ups_back = (made[name] for name in ("downs", "downs_back", "ups", "ups_back"))
+    convs, convs_back, head, head_back = (made[name] for name in ("convs", "convs_back", "head", "head_back"))
 
     def whole(array):
         zeros = (0,) * len(array.shape)
@@ -440,7 +484,7 @@
     def call(body, inputs, specs, shapes, out_specs, scratch_shapes, estimate, name):
         kinds = [kind for kind, spec in specs + out_specs] + ["whole"] * len(scratch_shapes)
         return pl.pallas_call(
-            functools.partial(over_strips, body, kinds),
+            functools.partial(over_strips, body, kinds, 0),
             grid=(half // BLOCK,),
             in_specs=[spec for kind, spec in specs],
             out_specs=[spec for kind, spec in out_specs],
@@ -451,6 +495,10 @@
             name=name,
         )(*inputs)
 
+    own_labels = lax.all_to_all(labels, "col", split_axis=1, concat_axis=0, tiled=True)
+    facing_labels = facing_tile(own_labels)
+    features, own_labels, facing_labels = lax.optimization_barrier((features, own_labels, facing_labels))
+    facing_labels = facing_labels.T
     split = features.reshape(2, half, columns, channels)
     bf_spec = strip_spec(channels)
     near_shapes, near_specs = edges(near)
@@ -466,8 +514,6 @@
         cost(0, 4),
         "entry",
     )
-    own_labels = lax.all_to_all(labels, "col", split_axis=1, concat_axis=0, tiled=True)
-    squeezed_1, own_labels = lax.optimization_barrier((squeezed_1, own_labels))
     halos = exchange(sent)
 
     centre = squeezed_1
@@ -484,12 +530,10 @@
     )
     halos = exchange(sent)
 
-    facing_labels = facing_tile(own_labels)
-    squeezed_2, facing_labels = lax.optimization_barrier((squeezed_2, facing_labels))
-    facing_labels = facing_labels.T
     centre = squeezed_2
     by_row_spec = "rows", pl.BlockSpec((BLOCK, columns, 2 * bins), lambda step: (step, 0, 0))
-    stream_2, activated_2, by_row, by_column = call(
+    parts = [columns // 4, columns // 8, columns // 8]
+    stream_2, activated_2, by_row, *by_column = call(
         functools.partial(head_kernel, far, steps),
         (centre, *halos, stream_1, ones, convs[1], ups[1], gains[2], head, bias),
         [whole(centre)] + [whole(halo) for halo in halos] + [bf_spec]
@@ -498,19 +542,19 @@
             halves(F32, channels),
             pair_shape,
             jax.ShapeDtypeStruct((half, columns, 2 * bins), BF16),
-            jax.ShapeDtypeStruct((2, half, columns // 2, 2 * bins), BF16),
+            *(jax.ShapeDtypeStruct((2, half, part, 2 * bins), BF16) for part in parts),
         ],
         [
             strip_spec(channels),
             pair_spec,
             by_row_spec,
-            ("halves", pl.BlockSpec((2, BLOCK, columns // 2, 2 * bins), lambda step: (0, step, 0, 0))),
+            *(("halves", pl.BlockSpec((2, BLOCK, part, 2 * bins), lambda step: (0, step, 0, 0))) for part in parts),
         ],
         scratch(far),
         cost(1, 14),
         "head",
     )
-    facing = facing_logits(by_column.reshape(rows, columns // 2, 2 * bins))
+    facing = facing_logits([piece.reshape(rows, piece.shape[2], 2 * bins) for piece in by_column])
 
     numbers = jnp.arange(bins, dtype=jnp.int32)
 
@@ -525,26 +569,57 @@
         axis=2,
     ).astype(BF16)
 
-    inner = BLOCK // ROWS
-    mirrored_logits = [array for piece in facing for array in piece]
-    grad_2, conv_grad_2, *sent = call(
-        functools.partial(loss_kernel, far, steps, inner, tuple(len(piece) for piece in facing)),
-        (by_row, *mirrored_logits, targets, stream_2, activated_2, ones, head_back, group, ups_back[1]),
-        [
-            by_row_spec,
-            *(("whole", pl.BlockSpec((array.shape[0], BLOCK, 2 * bins), lambda step: (0, step, 0)))
-              for array in mirrored_logits),
-            by_row_spec,
-            bf_spec,
-            pair_spec,
-        ]
-        + [whole(array) for array in (ones, head_back, group, ups_back[1])],
-        [halves(F32, channels), pair_shape] + far_shapes,
-        [strip_spec(channels), pair_spec] + far_specs,
-        [pltpu.VMEM((BLOCK, columns, 2 * bins), F32)],
-        cost(0, 18),
-        "loss",
-    )
+    taken = 0
+    outputs = []
+    sent = [None, None, None, None]
+    for index, piece in enumerate(facing):
+        blocks = piece[0].shape[1] // BLOCK
+        ends = taken == 0, index == len(facing) - 1
+
+        def moved(spec, first=taken):
+            kind, block = spec
+            return kind, pl.BlockSpec(
+                block.block_shape,
+                lambda step: tuple(
+                    place + first * (rank == (1 if kind == "halves" else 0))
+                    for rank, place in enumerate(block.index_map(step))
+                ),
+            )
+
+        weights = [ones, head_back, group, ups_back[1]]
+        side_shape, side_spec = far_shapes[2], moved(far_specs[2])
+        specs = [moved(by_row_spec)]
+        specs += [("whole", pl.BlockSpec((columns, BLOCK, 2 * bins), lambda step: (0, step, 0)))] * len(piece)
+        specs += [moved(by_row_spec), moved(bf_spec), moved(pair_spec)] + [whole(array) for array in weights]
+        inputs = [by_row, *piece, targets, stream_2, activated_2, *weights]
+        out_shapes = [halves(F32, channels), pair_shape, side_shape, side_shape]
+        out_specs = [moved(bf_spec), moved(pair_spec), side_spec, side_spec]
+        for place in range(2):
+            if ends[place]:
+                out_shapes.append(far_shapes[place])
+                out_specs.append(far_specs[place])
+        kinds = [kind for kind, spec in specs] + ["whole"] * len(outputs)
+        kinds += [kind for kind, spec in out_specs] + ["whole"]
+        body = functools.partial(loss_kernel, far, steps, BLOCK // ROWS, len(piece), ends)
+        results = pl.pallas_call(
+            functools.partial(over_strips, body, kinds, taken),
+            grid=(blocks,),
+            in_specs=[spec for kind, spec in specs] + [pl.BlockSpec(memory_space=pl.ANY)] * len(outputs),
+            out_specs=[spec for kind, spec in out_specs],
+            out_shape=out_shapes,
+            input_output_aliases={len(inputs) + place: place for place in range(len(outputs))},
+            scratch_shapes=[pltpu.VMEM((BLOCK, columns, 2 * bins), F32)],
+            compiler_params=pltpu.CompilerParams(vmem_limit_bytes=56 * 1024 * 1024),
+            cost_estimate=cost(0, 18),
+            name="loss",
+        )(*inputs, *outputs)
+        outputs = list(results[:4])
+        if ends[0]:
+            sent[0] = results[4]
+        if ends[1]:
+            sent[1] = results[-1]
+        taken += blocks
+    grad_2, conv_grad_2, *sent[2:] = outputs
     halos = exchange(sent)
 
     centre = conv_grad_2

time: 267 us -> 254 us (0.951)
  local copies, waits for them, and re-layouts: 22.2 us -> 9.63 us
  blocking collectives: 0 us -> 9.79 us
  other arithmetic: 25.4 us -> 15.8 us
  waiting for transfers between devices: 46.9 us -> 37.5 us
  Pallas kernels: 91.7 us -> 100 us
    ppermute x4 -> x7, waiting for transfers between devices: 24.7 us -> 12.6 us  [facing_logits(): move = lambda array, pairs: lax.ppermute(array, ('row', 'col'), pairs)]
    all_to_all x0 -> x1, blocking collectives: none -> 9.79 us  [shards(): lax.all_to_all(labels, 'col', split_axis=1, concat_axis=0, tiled=True)]
    pallas_call x6 -> x9, Pallas kernels: 91.7 us -> 100 us  [the longest x5 78.1 us: call(): pl.pallas_call(functools.partial(over_strips, body, kinds, 0), grid=(half...]
    ppermute x16, waiting for transfers between devices: 19.4 us -> 24.9 us  [shifted(): lax.ppermute(values, axis, [(i, i + move) for i in range(count) if 0 <= i...]
    all_to_all x1 -> x0, starting transfers between devices: 5.41 us -> none  [shards(): lax.all_to_all(labels, 'col', split_axis=1, concat_axis=0, tiled=True)]
    ppermute x4 -> x7, starting transfers between devices: 13.5 us -> 18.8 us  [facing_logits(): move = lambda array, pairs: lax.ppermute(array, ('row', 'col'), pairs)]
    concatenate x10 -> x0, other arithmetic: 5 us -> none  [the longest x7 4.16 us: diagonal(): jnp.concatenate([jnp.concatenate([weight, zeros], axis=1), jnp.concatenat...]
    slice x3 -> x0, local copies, waits for them, and re-layouts: 4.61 us -> none  [the longest x2 4.61 us: facing_logits(): straight, around = (by_column[:cut], by_column[cut:])]
  transfers between devices with their start and end apart: 22 -> 24, of which waited for: 10 -> 12; matrix products, arithmetic and copies ran while one was open for 14% -> 6% of each run, Pallas kernels for 3% -> 6%
where the time goes in v4:
time: 254 us; the launch traced here: 253 us
  Pallas kernels  100 us (39%)
  starting transfers between devices  78.9 us (31%)
  waiting for transfers between devices  37.5 us (15%)
  other arithmetic  15.8 us (6%)
  blocking collectives  9.79 us (4%)
  local copies, waits for them, and re-layouts  9.63 us (4%)
    pallas_call x5, Pallas kernels, call(): pl.pallas_call(functools.partial(over_strips, body, kinds, 0), grid=(half...  78.1 us
    ppermute x16, starting transfers between devices, shifted(): lax.ppermute(values, axis, [(i, i + move) for i in range(count) if 0 <= i...  55.5 us
    ppermute x16, waiting for transfers between devices, shifted(): lax.ppermute(values, axis, [(i, i + move) for i in range(count) if 0 <= i...  24.9 us
    pallas_call x3, Pallas kernels, shards(): pl.pallas_call(functools.partial(over_strips, body, kinds, taken), grid=(...  19.7 us
    ppermute x7, starting transfers between devices, facing_logits(): move = lambda array, pairs: lax.ppermute(array, ('row', 'col'), pairs)  18.8 us
    ppermute x7, waiting for transfers between devices, facing_logits(): move = lambda array, pairs: lax.ppermute(array, ('row', 'col'), pairs)  12.6 us
    all_to_all x1, blocking collectives, shards(): lax.all_to_all(labels, 'col', split_axis=1, concat_axis=0, tiled=True)  9.79 us
    unnamed x50, local copies, waits for them, and re-layouts  9.32 us
  transfers between devices with their start and end apart: 24, of which 12 were waited for; matrix products, arithmetic and copies ran while one was open for 6% of the time, Pallas kernels for 6%

profile of v4, /device:TPU:1, one launch (start us, length us, event | category | flops | bytes accessed | tf_op | source)
XLA Modules:
  0.0 252.7 jit_solution(15291773696318011970)
XLA Ops:
  0.8 9.8 %all_to_all.19 = s32[32,4,128]{2,0,1:T(8,128)S(1)} all-to-all(s32[32,4,128]{2,0,1:T(8,128)S(1)} %copy_bitcast_fusion), channel_id=1, replica_groups=mesh['row'=4,'col'=4,'dp'=2] {'col'}, dimensions={1} | all-to-all | bytes 131072 | tf_op jit(solution)/shard_map/all_to_all | solution.py:498
  10.6 4.5 %collective-permute-start = (s32[128,128]{1,0:T(8,128)S(1)}, s32[128,128]{1,0:T(8,128)S(1)}, u32[]{:S(2)}, u32[]{:S(2)}) collective-permute-start(s32[128,128]{1,0:T(8,128)S(1)} %bitcast.18), channel_id=1, source_target_pairs={{0,0},{2,8},{4,16},{6,24},{8,2},{10,10},{12,18},{14,26},{16,4},{18... | collective-permute-start | bytes 196616 | tf_op jit(solution)/shard_map/ppermute | solution.py:318
  15.2 1.5 copy.32.refs_1_
  16.7 1.4 copy.33.refs_4_
  18.1 2.7 %weights.1 = (f32[1,128]{1,0:T(1,128)}, bf16[128,128]{1,0:T(8,128)(2,1)}, bf16[384,384]{1,0:T(8,128)(2,1)}, bf16[384,384]{1,0:T(8,128)(2,1)}, bf16[384,384]{1,0:...) custom-call(f32[3,128]{1,0:T(4,128)} %refs_0_.1, ...), custom_call_target="tpu_custom_call" | custom-call | tf_op jit(solution)/shard_map/weights/pallas_call | solution.py:424
  20.8 8.3 %entry.1 = (bf16[64,128,128]{2,1,0:T(8,128)(2,1)}, bf16[4,64,128]{2,1,0:T(8,128)(2,1)}, bf16[4,64,128]{2,1,0:T(8,128)(2,1)}, bf16[64,8,128]{2,1,0:T(8,128)(2,1)}, bf16[64,8,128]{2,1,0:T(8,128)(2,1)}) custom-call(bf16[2,64,128,128]{3,2,1,0:T(8,128)(2,1)} %bitcast.15, bf16[128,128]{1,0:T(8,128)(2,1)} %get-tuple-element.68.refs_1_.refs_6_.refs_9_, ...), custom_call_target="tpu_custom_call" | custom-call | flops 536870912 | bytes 8388608 | tf_op jit(solution)/shard_map/entry/pallas_call | solution.py:486
  29.1 3.2 %collective-permute-start.1 = (bf16[4,64,128]{2,1,0:T(8,128)(2,1)}, bf16[4,64,128]{2,1,0:T(8,128)(2,1)S(1)}, u32[]{:S(2)}, u32[]{:S(2)}) collective-permute-start(bf16[4,64,128]{2,1,0:T(8,128)(2,1)} %get-tuple-element.73), channel_id=1, source_target_pairs={{0,8},{8,16},{16,24},{1,9},{9,17},{17,25},{2,10},{10,18},{18,26},{... | collective-permute-start | bytes 196616 | tf_op jit(solution)/shard_map/ppermute | solution.py:302
  32.3 1.9 collective-permute-start.2
  34.3 3.8 %collective-permute-done.2.refs_2_ = bf16[4,64,128]{2,1,0:T(8,128)(2,1)S(1)} collective-permute-done((bf16[4,64,128]{2,1,0:T(8,128)(2,1)}, bf16[4,64,128]{2,1,0:T(8,128)(2,1)S(1)}, u32[]{:S(2)}, u32[]{:S(2)}) %collective-permute-start.2) | collective-permute-done | bytes 65568 | tf_op jit(solution)/shard_map/ppermute | solution.py:302
  39.1 1.3 collective-permute-start.4
  41.3 4.0 %collective-permute-start.3 = (bf16[72,8,128]{2,1,0:T(8,128)(2,1)S(1)}, bf16[72,8,128]{2,1,0:T(8,128)(2,1)S(1)}, u32[]{:S(2)}, u32[]{:S(2)}) collective-permute-start(bf16[72,8,128]{2,1,0:T(8,128)(2,1)S(1)} %pad_maximum_fusion.5), channel_id=1, source_target_pairs={{0,2},{2,4},{4,6},{1,3},{3,5},{5,7},{8,10},{10,12},{12,14},{9,11},... | collective-permute-start | bytes 442376 | tf_op jit(solution)/shard_map/ppermute | solution.py:302
  45.3 2.1 collective-permute-done.3.refs_3_
  48.0 17.2 %middle.1 = (f32[2,64,128,128]{3,2,1,0:T(8,128)}, bf16[64,128,128]{2,1,0:T(8,128)(2,1)}, bf16[64,128,128]{2,1,0:T(8,128)(2,1)}, bf16[8,64,128]{2,1,0:T(8,128)(2,...) custom-call(bf16[64,128,128]{2,1,0:T(8,128)(2,1)} %get-tuple-element.72.refs_0_.refs_6_, ...), custom_call_target="tpu_custom_call" | custom-call | flops 1744830464 | bytes 25165824 | tf_op jit(solution)/shard_map/middle/pallas_call | solution.py:486
  65.2 3.1 %collective-permute-start.5 = (bf16[8,64,128]{2,1,0:T(8,128)(2,1)}, bf16[8,64,128]{2,1,0:T(8,128)(2,1)S(1)}, u32[]{:S(2)}, u32[]{:S(2)}) collective-permute-start(bf16[8,64,128]{2,1,0:T(8,128)(2,1)} %get-tuple-element.82), channel_id=1, source_target_pairs={{0,8},{8,16},{16,24},{1,9},{9,17},{17,25},{2,10},{10,18},{18,26},{... | collective-permute-start | bytes 393224 | tf_op jit(solution)/shard_map/ppermute | solution.py:302
  68.3 1.9 collective-permute-start.6
  70.6 4.2 %collective-permute-done.6.refs_2_ = bf16[8,64,128]{2,1,0:T(8,128)(2,1)S(1)} collective-permute-done((bf16[8,64,128]{2,1,0:T(8,128)(2,1)}, bf16[8,64,128]{2,1,0:T(8,128)(2,1)S(1)}, u32[]{:S(2)}, u32[]{:S(2)}) %collective-permute-start.6) | collective-permute-done | bytes 131104 | tf_op jit(solution)/shard_map/ppermute | solution.py:302
  75.8 1.3 collective-permute-start.8
  78.1 4.7 %collective-permute-start.7 = (bf16[80,8,128]{2,1,0:T(8,128)(2,1)S(1)}, bf16[80,8,128]{2,1,0:T(8,128)(2,1)S(1)}, u32[]{:S(2)}, u32[]{:S(2)}) collective-permute-start(bf16[80,8,128]{2,1,0:T(8,128)(2,1)S(1)} %pad_maximum_fusion.1), channel_id=1, source_target_pairs={{0,2},{2,4},{4,6},{1,3},{3,5},{5,7},{8,10},{10,12},{12,14},{9,11},... | collective-permute-start | bytes 491528 | tf_op jit(solution)/shard_map/ppermute | solution.py:302
  82.8 2.2 collective-permute-done.7.refs_3_
  85.7 16.7 %head.1 = (f32[2,64,128,128]{3,2,1,0:T(8,128)}, bf16[64,128,128]{2,1,0:T(8,128)(2,1)}, bf16[64,128,128]{2,1,0:T(8,128)(2,1)}, bf16[2,64,32,128]{3,2,1,0:T(8,128)...) custom-call(bf16[64,128,128]{2,1,0:T(8,128)(2,1)} %get-tuple-element.81.refs_0_.refs_6_, ...), custom_call_target="tpu_custom_call" | custom-call | flops 1744830464 | bytes 29360128 | tf_op jit(solution)/shard_map/head/pallas_call | solution.py:486
  102.4 1.9 collective-permute-start.15
  104.3 1.3 collective-permute-start.12
  105.6 1.3 collective-permute-start.9
  107.2 3.6 %collective-permute-start.14 = (bf16[128,16,128]{2,1,0:T(8,128)(2,1)}, bf16[128,16,128]{2,1,0:T(8,128)(2,1)S(1)}, u32[]{:S(2)}, u32[]{:S(2)}) collective-permute-start(bf16[128,16,128]{2,1,0:T(8,128)(2,1)} %bitcast.26), channel_id=1, source_target_pairs={{0,0},{2,8},{8,2},{10,10},{20,20},{22,28},{28,22},{30,30},{1,1},{3... | collective-permute-start | bytes 1572872 | tf_op jit(solution)/shard_map/ppermute | solution.py:351
  110.8 1.9 collective-permute-start.11
  112.8 6.9 %collective-permute-done.12 = bf16[128,16,128]{2,1,0:T(8,128)(2,1)S(1)} collective-permute-done((bf16[128,16,128]{2,1,0:T(8,128)(2,1)}, bf16[128,16,128]{2,1,0:T(8,128)(2,1)S(1)}, u32[]{:S(2)}, u32[]{:S(2)}) %collective-permute-start.12) | collective-permute-done | bytes 524320 | tf_op jit(solution)/shard_map/ppermute | solution.py:351
  119.7 5.6 %collective-permute-start.13 = (bf16[128,16,128]{2,1,0:T(8,128)(2,1)S(1)}, bf16[128,16,128]{2,1,0:T(8,128)(2,1)S(1)}, u32[]{:S(2)}, u32[]{:S(2)}) collective-permute-start(bf16[128,16,128]{2,1,0:T(8,128)(2,1)S(1)} %collective-permute-done.12), channel_id=1, source_target_pairs={{20,16},{22,24},{28,18},{30,26},{0,4},{2,12},{8,6},{10,14},{21,17}... | collective-permute-start | bytes 1572872 | tf_op jit(solution)/shard_map/ppermute | solution.py:351
  125.2 5.7 %collective-permute-done.9 = bf16[128,16,128]{2,1,0:T(8,128)(2,1)S(1)} collective-permute-done((bf16[128,16,128]{2,1,0:T(8,128)(2,1)}, bf16[128,16,128]{2,1,0:T(8,128)(2,1)S(1)}, u32[]{:S(2)}, u32[]{:S(2)}) %collective-permute-start.9) | collective-permute-done | bytes 524320 | tf_op jit(solution)/shard_map/ppermute | solution.py:351
  130.9 3.2 %collective-permute-start.10 = (bf16[128,16,128]{2,1,0:T(8,128)(2,1)S(1)}, bf16[128,16,128]{2,1,0:T(8,128)(2,1)S(1)}, u32[]{:S(2)}, u32[]{:S(2)}) collective-permute-start(bf16[128,16,128]{2,1,0:T(8,128)(2,1)S(1)} %collective-permute-done.9), channel_id=1, source_target_pairs={{20,16},{22,24},{28,18},{30,26},{0,4},{2,12},{8,6},{10,14},{21,17}... | collective-permute-start | bytes 1572872 | tf_op jit(solution)/shard_map/ppermute | solution.py:351
  134.1 5.7 %multiply_convert_fusion = (bf16[64,128,64]{2,1,0:T(8,128)(2,1)S(1)}, bf16[64,128,64]{2,1,0:T(8,128)(2,1)S(1)}) fusion(s32[64,128]{1,0:T(8,128)S(1)} %copy.35, s32[64,128]{1,0:T(8,128)S(1)} %get-tuple-element.142, s32[64,128]{1,0:T(8,128)S(1)} %copy.34, s32[64,128]{1,0:T(8,128)S(1)} %get-tuple-element.141), kind=kLoop, calls=%fused_computation | loop fusion | flops 7340032 | bytes 2228224 | tf_op jit(solution)/shard_map/convert.1
  139.8 2.6 %pad_maximum_fusion.refs_2_.refs_3_ = bf16[64,128,128]{2,1,0:T(8,128)(2,1)} fusion(bf16[64,128,64]{2,1,0:T(8,128)(2,1)S(1)} %get-tuple-element.149, bf16[64,128,64]{2,1,0:T(8,128)(2,1)S(1)} %get-tuple-element.150), kind=kLoop, calls=%fused_computation.6 | loop fusion | flops 4194304 | bytes 4194304 | tf_op jit(solution)/shard_map/concatenate | solution.py:564
  143.4 7.7 %loss.3 = (f32[2,64,128,128]{3,2,1,0:T(8,128)}, bf16[64,128,128]{2,1,0:T(8,128)(2,1)}, bf16[64,8,128]{2,1,0:T(8,128)(2,1)}, bf16[64,8,128]{2,1,0:T(8,128)(2,1)}, bf16[8,64,128]{2,1,0:T(8,128)(2,1)}) custom-call(bf16[64,128,128]{2,1,0:T(8,128)(2,1)} %get-tuple-element.92.refs_0_, bf16[128,32,128]{2,1,0:T(8,128)(2,1)} %copy-done.2, ...), custom_call_target="tpu_custom_call" | custom-call | flops 536870912 | bytes 37748736 | tf_op jit(solution)/shard_map/loss/pallas_call | solution.py:604
  152.1 5.8 %loss.4 = (f32[2,64,128,128]{3,2,1,0:T(8,128)}, bf16[64,128,128]{2,1,0:T(8,128)(2,1)}, bf16[64,8,128]{2,1,0:T(8,128)(2,1)}, bf16[64,8,128]{2,1,0:T(8,128)(2,1)}) custom-call(bf16[64,128,128]{2,1,0:T(8,128)(2,1)} %get-tuple-element.92.refs_0_, ...), custom_call_target="tpu_custom_call", output_to_operand_aliasing={{0}: (10, {}), {1}: (11, {}), {2}: (12, {}), {3}: (13, {})} | custom-call | flops 536870912 | bytes 37748736 | tf_op jit(solution)/shard_map/loss/pallas_call | solution.py:604
  158.9 6.1 %loss.5 = (f32[2,64,128,128]{3,2,1,0:T(8,128)}, bf16[64,128,128]{2,1,0:T(8,128)(2,1)}, bf16[64,8,128]{2,1,0:T(8,128)(2,1)}, bf16[64,8,128]{2,1,0:T(8,128)(2,1)}, bf16[8,64,128]{2,1,0:T(8,128)(2,1)}) custom-call(bf16[64,128,128]{2,1,0:T(8,128)(2,1)} %get-tuple-element.92.refs_0_, ...), custom_call_target="tpu_custom_call", output_to_operand_aliasing={{0}: (10, {}), {1}: (11, {}), {2}: (12, {}), {3}: (13, {})} | custom-call | flops 536870912 | bytes 37748736 | tf_op jit(solution)/shard_map/loss/pallas_call | solution.py:604
  165.0 15.8 %collective-permute-start.16 = (bf16[8,64,128]{2,1,0:T(8,128)(2,1)}, bf16[8,64,128]{2,1,0:T(8,128)(2,1)S(1)}, u32[]{:S(2)}, u32[]{:S(2)}) collective-permute-start(bf16[8,64,128]{2,1,0:T(8,128)(2,1)} %get-tuple-element.112), channel_id=1, source_target_pairs={{0,8},{8,16},{16,24},{1,9},{9,17},{17,25},{2,10},{10,18},{18,26},{... | collective-permute-start | bytes 393224 | tf_op jit(solution)/shard_map/ppermute | solution.py:302
  180.9 1.9 collective-permute-start.17
  183.1 4.0 %collective-permute-done.17.refs_2_ = bf16[8,64,128]{2,1,0:T(8,128)(2,1)S(1)} collective-permute-done((bf16[8,64,128]{2,1,0:T(8,128)(2,1)S(1)}, bf16[8,64,128]{2,1,0:T(8,128)(2,1)S(1)}, u32[]{:S(2)}, u32[]{:S(2)}) %collective-permute-start.17) | collective-permute-done | bytes 131104 | tf_op jit(solution)/shard_map/ppermute | solution.py:302
  188.1 1.3 collective-permute-start.19
  190.4 4.0 %collective-permute-start.18 = (bf16[80,8,128]{2,1,0:T(8,128)(2,1)S(1)}, bf16[80,8,128]{2,1,0:T(8,128)(2,1)S(1)}, u32[]{:S(2)}, u32[]{:S(2)}) collective-permute-start(bf16[80,8,128]{2,1,0:T(8,128)(2,1)S(1)} %pad_maximum_fusion.3), channel_id=1, source_target_pairs={{0,2},{2,4},{4,6},{1,3},{3,5},{5,7},{8,10},{10,12},{12,14},{9,11},... | collective-permute-start | bytes 491528 | tf_op jit(solution)/shard_map/ppermute | solution.py:302
  194.4 2.2 collective-permute-done.18.refs_3_
  197.3 18.7 %back.1 = (f32[2,64,128,128]{3,2,1,0:T(8,128)}, bf16[64,128,128]{2,1,0:T(8,128)(2,1)}, bf16[4,64,128]{2,1,0:T(8,128)(2,1)}, bf16[4,64,128]{2,1,0:T(8,128)(2,1)},...) custom-call(bf16[64,128,128]{2,1,0:T(8,128)(2,1)} %get-tuple-element.111.refs_0_, ...), custom_call_target="tpu_custom_call" | custom-call | flops 1744830464 | bytes 41943040 | tf_op jit(solution)/shard_map/back/pallas_call | solution.py:486
  216.0 2.9 %collective-permute-start.20 = (bf16[4,64,128]{2,1,0:T(8,128)(2,1)}, bf16[4,64,128]{2,1,0:T(8,128)(2,1)S(1)}, u32[]{:S(2)}, u32[]{:S(2)}) collective-permute-start(bf16[4,64,128]{2,1,0:T(8,128)(2,1)} %get-tuple-element.122), channel_id=1, source_target_pairs={{0,8},{8,16},{16,24},{1,9},{9,17},{17,25},{2,10},{10,18},{18,26},{... | collective-permute-start | bytes 196616 | tf_op jit(solution)/shard_map/ppermute | solution.py:302
  218.9 1.9 collective-permute-start.21
  220.8 3.8 %collective-permute-done.21.refs_2_ = bf16[4,64,128]{2,1,0:T(8,128)(2,1)S(1)} collective-permute-done((bf16[4,64,128]{2,1,0:T(8,128)(2,1)}, bf16[4,64,128]{2,1,0:T(8,128)(2,1)S(1)}, u32[]{:S(2)}, u32[]{:S(2)}) %collective-permute-start.21) | collective-permute-done | bytes 65568 | tf_op jit(solution)/shard_map/ppermute | solution.py:302
  225.6 1.3 collective-permute-start.23
  227.9 5.0 %collective-permute-start.22 = (bf16[72,8,128]{2,1,0:T(8,128)(2,1)S(1)}, bf16[72,8,128]{2,1,0:T(8,128)(2,1)S(1)}, u32[]{:S(2)}, u32[]{:S(2)}) collective-permute-start(bf16[72,8,128]{2,1,0:T(8,128)(2,1)S(1)} %pad_maximum_fusion.7), channel_id=1, source_target_pairs={{0,2},{2,4},{4,6},{1,3},{3,5},{5,7},{8,10},{10,12},{12,14},{9,11},... | collective-permute-start | bytes 442376 | tf_op jit(solution)/shard_map/ppermute | solution.py:302
  232.8 1.8 collective-permute-done.22.refs_3_
  235.3 17.2 %final.1 = f32[2,64,128,128]{3,2,1,0:T(8,128)} custom-call(bf16[64,128,128]{2,1,0:T(8,128)(2,1)} %get-tuple-element.121.refs_0_, bf16[4,64,128]{2,1,0:T(8,128)(2,1)} %copy-done.20, bf16[4,64,128]{2,1,0:T(8,128)(2,1)} %copy-done.22, bf16[72,8,128]{2,1,0:T(8,128)(2,1)} %copy-done.18, bf16[72,8,128]{2,1,0:T(8,128)(2,1)} %copy-done.17, ...), custom_call_target="tpu_custom_call" | custom-call | flops 1744830464 | bytes 33554432 | tf_op jit(solution)/shard_map/final/pallas_call | solution.py:486
  (83 shorter events, 14.9 us)
Async XLA Ops:
  0.0 0.8 copy-start
  10.6 10.2 %collective-permute-start = (s32[128,128]{1,0:T(8,128)S(1)}, s32[128,128]{1,0:T(8,128)S(1)}, u32[]{:S(2)}, u32[]{:S(2)}) collective-permute-start(s32[128,128]{1,0:T(8,128)S(1)} %bitcast.18), channel_id=1, source_target_pairs={{0,0},{2,8},{4,16},{6,24},{8,2},{10,10},{12,18},{14,26},{16,4},{18... | collective-permute-start | bytes 196616 | tf_op jit(solution)/shard_map/ppermute | solution.py:318
  29.1 5.1 %collective-permute-start.1 = (bf16[4,64,128]{2,1,0:T(8,128)(2,1)}, bf16[4,64,128]{2,1,0:T(8,128)(2,1)S(1)}, u32[]{:S(2)}, u32[]{:S(2)}) collective-permute-start(bf16[4,64,128]{2,1,0:T(8,128)(2,1)} %get-tuple-element.73), channel_id=1, source_target_pairs={{0,8},{8,16},{16,24},{1,9},{9,17},{17,25},{2,10},{10,18},{18,26},{... | collective-permute-start | bytes 196616 | tf_op jit(solution)/shard_map/ppermute | solution.py:302
  32.3 5.8 %collective-permute-start.2 = (bf16[4,64,128]{2,1,0:T(8,128)(2,1)}, bf16[4,64,128]{2,1,0:T(8,128)(2,1)S(1)}, u32[]{:S(2)}, u32[]{:S(2)}) collective-permute-start(bf16[4,64,128]{2,1,0:T(8,128)(2,1)} %get-tuple-element.74), channel_id=1, source_target_pairs={{8,0},{16,8},{24,16},{9,1},{17,9},{25,17},{10,2},{18,10},{26,18},{... | collective-permute-start | bytes 196616 | tf_op jit(solution)/shard_map/ppermute | solution.py:302
  34.3 13.1 %copy-start.19 = (bf16[4,64,128]{2,1,0:T(8,128)(2,1)}, bf16[4,64,128]{2,1,0:T(8,128)(2,1)S(1)}, u32[]{:S(2)}) copy-start(bf16[4,64,128]{2,1,0:T(8,128)(2,1)S(1)} %collective-permute-done.1.refs_1_) | copy-start | bytes 196612
  38.1 9.3 %copy-start.21 = (bf16[4,64,128]{2,1,0:T(8,128)(2,1)}, bf16[4,64,128]{2,1,0:T(8,128)(2,1)S(1)}, u32[]{:S(2)}) copy-start(bf16[4,64,128]{2,1,0:T(8,128)(2,1)S(1)} %collective-permute-done.2.refs_2_) | copy-start | bytes 196612
  39.1 6.2 %collective-permute-start.4 = (bf16[72,8,128]{2,1,0:T(8,128)(2,1)S(1)}, bf16[72,8,128]{2,1,0:T(8,128)(2,1)S(1)}, u32[]{:S(2)}, u32[]{:S(2)}) collective-permute-start(bf16[72,8,128]{2,1,0:T(8,128)(2,1)S(1)} %pad_maximum_fusion.6), channel_id=1, source_target_pairs={{2,0},{4,2},{6,4},{3,1},{5,3},{7,5},{10,8},{12,10},{14,12},{11,9},... | collective-permute-start | bytes 442376 | tf_op jit(solution)/shard_map/ppermute | solution.py:302
  41.3 6.1 %collective-permute-start.3 = (bf16[72,8,128]{2,1,0:T(8,128)(2,1)S(1)}, bf16[72,8,128]{2,1,0:T(8,128)(2,1)S(1)}, u32[]{:S(2)}, u32[]{:S(2)}) collective-permute-start(bf16[72,8,128]{2,1,0:T(8,128)(2,1)S(1)} %pad_maximum_fusion.5), channel_id=1, source_target_pairs={{0,2},{2,4},{4,6},{1,3},{3,5},{5,7},{8,10},{10,12},{12,14},{9,11},... | collective-permute-start | bytes 442376 | tf_op jit(solution)/shard_map/ppermute | solution.py:302
  45.3 2.1 copy-start.15
  47.4 0.6 copy-start.16
  65.2 5.4 %collective-permute-start.5 = (bf16[8,64,128]{2,1,0:T(8,128)(2,1)}, bf16[8,64,128]{2,1,0:T(8,128)(2,1)S(1)}, u32[]{:S(2)}, u32[]{:S(2)}) collective-permute-start(bf16[8,64,128]{2,1,0:T(8,128)(2,1)} %get-tuple-element.82), channel_id=1, source_target_pairs={{0,8},{8,16},{16,24},{1,9},{9,17},{17,25},{2,10},{10,18},{18,26},{... | collective-permute-start | bytes 393224 | tf_op jit(solution)/shard_map/ppermute | solution.py:302
  68.3 6.5 %collective-permute-start.6 = (bf16[8,64,128]{2,1,0:T(8,128)(2,1)}, bf16[8,64,128]{2,1,0:T(8,128)(2,1)S(1)}, u32[]{:S(2)}, u32[]{:S(2)}) collective-permute-start(bf16[8,64,128]{2,1,0:T(8,128)(2,1)} %get-tuple-element.83), channel_id=1, source_target_pairs={{8,0},{16,8},{24,16},{9,1},{17,9},{25,17},{10,2},{18,10},{26,18},{... | collective-permute-start | bytes 393224 | tf_op jit(solution)/shard_map/ppermute | solution.py:302
  70.6 14.4 %copy-start.9 = (bf16[8,64,128]{2,1,0:T(8,128)(2,1)}, bf16[8,64,128]{2,1,0:T(8,128)(2,1)S(1)}, u32[]{:S(2)}) copy-start(bf16[8,64,128]{2,1,0:T(8,128)(2,1)S(1)} %collective-permute-done.5.refs_1_) | copy-start | bytes 393220
  74.8 10.2 %copy-start.10 = (bf16[8,64,128]{2,1,0:T(8,128)(2,1)}, bf16[8,64,128]{2,1,0:T(8,128)(2,1)S(1)}, u32[]{:S(2)}) copy-start(bf16[8,64,128]{2,1,0:T(8,128)(2,1)S(1)} %collective-permute-done.6.refs_2_) | copy-start | bytes 393220
  75.8 7.0 %collective-permute-start.8 = (bf16[80,8,128]{2,1,0:T(8,128)(2,1)S(1)}, bf16[80,8,128]{2,1,0:T(8,128)(2,1)S(1)}, u32[]{:S(2)}, u32[]{:S(2)}) collective-permute-start(bf16[80,8,128]{2,1,0:T(8,128)(2,1)S(1)} %pad_maximum_fusion.2), channel_id=1, source_target_pairs={{2,0},{4,2},{6,4},{3,1},{5,3},{7,5},{10,8},{12,10},{14,12},{11,9},... | collective-permute-start | bytes 491528 | tf_op jit(solution)/shard_map/ppermute | solution.py:302
  78.1 7.0 %collective-permute-start.7 = (bf16[80,8,128]{2,1,0:T(8,128)(2,1)S(1)}, bf16[80,8,128]{2,1,0:T(8,128)(2,1)S(1)}, u32[]{:S(2)}, u32[]{:S(2)}) collective-permute-start(bf16[80,8,128]{2,1,0:T(8,128)(2,1)S(1)} %pad_maximum_fusion.1), channel_id=1, source_target_pairs={{0,2},{2,4},{4,6},{1,3},{3,5},{5,7},{8,10},{10,12},{12,14},{9,11},... | collective-permute-start | bytes 491528 | tf_op jit(solution)/shard_map/ppermute | solution.py:302
  82.8 2.2 copy-start.13
  85.0 0.7 copy-start.14
  102.4 40.0 %collective-permute-start.15 = (bf16[128,32,128]{2,1,0:T(8,128)(2,1)}, bf16[128,32,128]{2,1,0:T(8,128)(2,1)S(1)}, u32[]{:S(2)}, u32[]{:S(2)}) collective-permute-start(bf16[128,32,128]{2,1,0:T(8,128)(2,1)} %bitcast.22), channel_id=1, source_target_pairs={{0,0},{2,8},{4,16},{6,24},{8,2},{10,10},{12,18},{14,26},{16,4},{18... | collective-permute-start | bytes 3145736 | tf_op jit(solution)/shard_map/ppermute | solution.py:351
  104.3 15.3 %collective-permute-start.12 = (bf16[128,16,128]{2,1,0:T(8,128)(2,1)}, bf16[128,16,128]{2,1,0:T(8,128)(2,1)S(1)}, u32[]{:S(2)}, u32[]{:S(2)}) collective-permute-start(bf16[128,16,128]{2,1,0:T(8,128)(2,1)} %bitcast.25), channel_id=1, source_target_pairs={{4,20},{6,22},{12,28},{14,30},{16,0},{18,2},{24,8},{26,10},{5,21},... | collective-permute-start | bytes 1572872 | tf_op jit(solution)/shard_map/ppermute | solution.py:351
  105.6 25.3 %collective-permute-start.9 = (bf16[128,16,128]{2,1,0:T(8,128)(2,1)}, bf16[128,16,128]{2,1,0:T(8,128)(2,1)S(1)}, u32[]{:S(2)}, u32[]{:S(2)}) collective-permute-start(bf16[128,16,128]{2,1,0:T(8,128)(2,1)} %bitcast.23), channel_id=1, source_target_pairs={{4,20},{6,22},{12,28},{14,30},{16,0},{18,2},{24,8},{26,10},{5,21},... | collective-permute-start | bytes 1572872 | tf_op jit(solution)/shard_map/ppermute | solution.py:351
  107.2 43.9 %collective-permute-start.14 = (bf16[128,16,128]{2,1,0:T(8,128)(2,1)}, bf16[128,16,128]{2,1,0:T(8,128)(2,1)S(1)}, u32[]{:S(2)}, u32[]{:S(2)}) collective-permute-start(bf16[128,16,128]{2,1,0:T(8,128)(2,1)} %bitcast.26), channel_id=1, source_target_pairs={{0,0},{2,8},{8,2},{10,10},{20,20},{22,28},{28,22},{30,30},{1,1},{3... | collective-permute-start | bytes 1572872 | tf_op jit(solution)/shard_map/ppermute | solution.py:351
  110.8 47.1 %collective-permute-start.11 = (bf16[128,16,128]{2,1,0:T(8,128)(2,1)}, bf16[128,16,128]{2,1,0:T(8,128)(2,1)S(1)}, u32[]{:S(2)}, u32[]{:S(2)}) collective-permute-start(bf16[128,16,128]{2,1,0:T(8,128)(2,1)} %bitcast.24), channel_id=1, source_target_pairs={{0,0},{2,8},{8,2},{10,10},{20,20},{22,28},{28,22},{30,30},{1,1},{3... | collective-permute-start | bytes 1572872 | tf_op jit(solution)/shard_map/ppermute | solution.py:351
  119.7 31.5 %collective-permute-start.13 = (bf16[128,16,128]{2,1,0:T(8,128)(2,1)S(1)}, bf16[128,16,128]{2,1,0:T(8,128)(2,1)S(1)}, u32[]{:S(2)}, u32[]{:S(2)}) collective-permute-start(bf16[128,16,128]{2,1,0:T(8,128)(2,1)S(1)} %collective-permute-done.12), channel_id=1, source_target_pairs={{20,16},{22,24},{28,18},{30,26},{0,4},{2,12},{8,6},{10,14},{21,17}... | collective-permute-start | bytes 1572872 | tf_op jit(solution)/shard_map/ppermute | solution.py:351
  130.9 27.1 %collective-permute-start.10 = (bf16[128,16,128]{2,1,0:T(8,128)(2,1)S(1)}, bf16[128,16,128]{2,1,0:T(8,128)(2,1)S(1)}, u32[]{:S(2)}, u32[]{:S(2)}) collective-permute-start(bf16[128,16,128]{2,1,0:T(8,128)(2,1)S(1)} %collective-permute-done.9), channel_id=1, source_target_pairs={{20,16},{22,24},{28,18},{30,26},{0,4},{2,12},{8,6},{10,14},{21,17}... | collective-permute-start | bytes 1572872 | tf_op jit(solution)/shard_map/ppermute | solution.py:351
  142.4 1.0 copy-start.2
  151.1 0.8 copy-start.5
  151.2 1.0 copy-start.6
  157.9 0.8 copy-start.3
  158.0 1.0 copy-start.4
  158.9 21.9 %copy-start.23 = (bf16[8,64,128]{2,1,0:T(8,128)(2,1)S(1)}, bf16[8,64,128]{2,1,0:T(8,128)(2,1)}, u32[]{:S(2)}) copy-start(bf16[8,64,128]{2,1,0:T(8,128)(2,1)} %get-tuple-element.113) | copy-start | bytes 393220
  165.0 18.0 %collective-permute-start.16 = (bf16[8,64,128]{2,1,0:T(8,128)(2,1)}, bf16[8,64,128]{2,1,0:T(8,128)(2,1)S(1)}, u32[]{:S(2)}, u32[]{:S(2)}) collective-permute-start(bf16[8,64,128]{2,1,0:T(8,128)(2,1)} %get-tuple-element.112), channel_id=1, source_target_pairs={{0,8},{8,16},{16,24},{1,9},{9,17},{17,25},{2,10},{10,18},{18,26},{... | collective-permute-start | bytes 393224 | tf_op jit(solution)/shard_map/ppermute | solution.py:302
  180.9 6.3 %collective-permute-start.17 = (bf16[8,64,128]{2,1,0:T(8,128)(2,1)S(1)}, bf16[8,64,128]{2,1,0:T(8,128)(2,1)S(1)}, u32[]{:S(2)}, u32[]{:S(2)}) collective-permute-start(bf16[8,64,128]{2,1,0:T(8,128)(2,1)S(1)} %copy-done.23), channel_id=1, source_target_pairs={{8,0},{16,8},{24,16},{9,1},{17,9},{25,17},{10,2},{18,10},{26,18},{... | collective-permute-start | bytes 393224 | tf_op jit(solution)/shard_map/ppermute | solution.py:302
  183.1 13.5 %copy-start.7 = (bf16[8,64,128]{2,1,0:T(8,128)(2,1)}, bf16[8,64,128]{2,1,0:T(8,128)(2,1)S(1)}, u32[]{:S(2)}) copy-start(bf16[8,64,128]{2,1,0:T(8,128)(2,1)S(1)} %collective-permute-done.16.refs_1_) | copy-start | bytes 393220
  187.1 9.5 %copy-start.8 = (bf16[8,64,128]{2,1,0:T(8,128)(2,1)}, bf16[8,64,128]{2,1,0:T(8,128)(2,1)S(1)}, u32[]{:S(2)}) copy-start(bf16[8,64,128]{2,1,0:T(8,128)(2,1)S(1)} %collective-permute-done.17.refs_2_) | copy-start | bytes 393220
  188.1 6.2 %collective-permute-start.19 = (bf16[80,8,128]{2,1,0:T(8,128)(2,1)S(1)}, bf16[80,8,128]{2,1,0:T(8,128)(2,1)S(1)}, u32[]{:S(2)}, u32[]{:S(2)}) collective-permute-start(bf16[80,8,128]{2,1,0:T(8,128)(2,1)S(1)} %pad_maximum_fusion.4), channel_id=1, source_target_pairs={{2,0},{4,2},{6,4},{3,1},{5,3},{7,5},{10,8},{12,10},{14,12},{11,9},... | collective-permute-start | bytes 491528 | tf_op jit(solution)/shard_map/ppermute | solution.py:302
  190.4 6.2 %collective-permute-start.18 = (bf16[80,8,128]{2,1,0:T(8,128)(2,1)S(1)}, bf16[80,8,128]{2,1,0:T(8,128)(2,1)S(1)}, u32[]{:S(2)}, u32[]{:S(2)}) collective-permute-start(bf16[80,8,128]{2,1,0:T(8,128)(2,1)S(1)} %pad_maximum_fusion.3), channel_id=1, source_target_pairs={{0,2},{2,4},{4,6},{1,3},{3,5},{5,7},{8,10},{10,12},{12,14},{9,11},... | collective-permute-start | bytes 491528 | tf_op jit(solution)/shard_map/ppermute | solution.py:302
  194.4 2.2 copy-start.11
  196.6 0.7 copy-start.12
  216.0 4.8 %collective-permute-start.20 = (bf16[4,64,128]{2,1,0:T(8,128)(2,1)}, bf16[4,64,128]{2,1,0:T(8,128)(2,1)S(1)}, u32[]{:S(2)}, u32[]{:S(2)}) collective-permute-start(bf16[4,64,128]{2,1,0:T(8,128)(2,1)} %get-tuple-element.122), channel_id=1, source_target_pairs={{0,8},{8,16},{16,24},{1,9},{9,17},{17,25},{2,10},{10,18},{18,26},{... | collective-permute-start | bytes 196616 | tf_op jit(solution)/shard_map/ppermute | solution.py:302
  218.9 5.8 %collective-permute-start.21 = (bf16[4,64,128]{2,1,0:T(8,128)(2,1)}, bf16[4,64,128]{2,1,0:T(8,128)(2,1)S(1)}, u32[]{:S(2)}, u32[]{:S(2)}) collective-permute-start(bf16[4,64,128]{2,1,0:T(8,128)(2,1)} %get-tuple-element.123), channel_id=1, source_target_pairs={{8,0},{16,8},{24,16},{9,1},{17,9},{25,17},{10,2},{18,10},{26,18},{... | collective-permute-start | bytes 196616 | tf_op jit(solution)/shard_map/ppermute | solution.py:302
  220.8 13.9 %copy-start.20 = (bf16[4,64,128]{2,1,0:T(8,128)(2,1)}, bf16[4,64,128]{2,1,0:T(8,128)(2,1)S(1)}, u32[]{:S(2)}) copy-start(bf16[4,64,128]{2,1,0:T(8,128)(2,1)S(1)} %collective-permute-done.20.refs_1_) | copy-start | bytes 196612
  224.7 10.0 %copy-start.22 = (bf16[4,64,128]{2,1,0:T(8,128)(2,1)}, bf16[4,64,128]{2,1,0:T(8,128)(2,1)S(1)}, u32[]{:S(2)}) copy-start(bf16[4,64,128]{2,1,0:T(8,128)(2,1)S(1)} %collective-permute-done.21.refs_2_) | copy-start | bytes 196612
  225.6 7.2 %collective-permute-start.23 = (bf16[72,8,128]{2,1,0:T(8,128)(2,1)S(1)}, bf16[72,8,128]{2,1,0:T(8,128)(2,1)S(1)}, u32[]{:S(2)}, u32[]{:S(2)}) collective-permute-start(bf16[72,8,128]{2,1,0:T(8,128)(2,1)S(1)} %pad_maximum_fusion.8), channel_id=1, source_target_pairs={{2,0},{4,2},{6,4},{3,1},{5,3},{7,5},{10,8},{12,10},{14,12},{11,9},... | collective-permute-start | bytes 442376 | tf_op jit(solution)/shard_map/ppermute | solution.py:302
  227.9 6.8 %collective-permute-start.22 = (bf16[72,8,128]{2,1,0:T(8,128)(2,1)S(1)}, bf16[72,8,128]{2,1,0:T(8,128)(2,1)S(1)}, u32[]{:S(2)}, u32[]{:S(2)}) collective-permute-start(bf16[72,8,128]{2,1,0:T(8,128)(2,1)S(1)} %pad_maximum_fusion.7), channel_id=1, source_target_pairs={{0,2},{2,4},{4,6},{1,3},{3,5},{5,7},{8,10},{10,12},{12,14},{9,11},... | collective-permute-start | bytes 442376 | tf_op jit(solution)/shard_map/ppermute | solution.py:302
  232.8 1.9 copy-start.17
  234.7 0.7 copy-start.18
  235.3 17.2 %copy-start.1 = (s32[32,512]{1,0:T(8,128)S(1)}, s32[32,512]{1,0:T(8,128)}, u32[]{:S(2)}) copy-start(s32[32,512]{1,0:T(8,128)} %param.9) | copy-start | bytes 196612

commit v5 on v4

--- a/solution.py
+++ b/solution.py
@@ -385,24 +385,24 @@
 
 
 def derived(norm_gain, w_down, w_conv, w_up, w_head, head_bias):
-    channels, bins = w_head.shape
+    bins, channels = w_head.shape
     gains = [norm_gain[index : index + 1] * math.sqrt(channels) for index in range(3)]
-    down = [w_down[index].astype(F32) for index in range(2)]
+    down_back = [w_down[index].astype(F32) for index in range(2)]
     up = [w_up[index].astype(F32) for index in range(2)]
     conv = [[[w_conv[index, row, col].astype(F32) for col in range(3)] for row in range(3)] for index in range(2)]
     back = [[[conv[index][2 - row][2 - col].T for col in range(3)] for row in range(3)] for index in range(2)]
-    head = w_head[...].astype(F32)
+    head_back = w_head[...].astype(F32)
     first = lax.broadcasted_iota(jnp.int32, (channels, channels), 0)
     second = lax.broadcasted_iota(jnp.int32, (channels, channels), 1)
     matrices = dict(
-        downs=[diagonal(weight) for weight in down],
-        downs_back=[diagonal(weight.T) for weight in down],
+        downs=[diagonal(weight.T) for weight in down_back],
+        downs_back=[diagonal(weight) for weight in down_back],
         ups=[two_parts(weight) for weight in up],
         ups_back=[diagonal(weight.T) for weight in up],
         convs=[dilated_weights(blocks) for blocks in conv],
         convs_back=[dilated_weights(blocks) for blocks in back],
-        head=diagonal(head),
-        head_back=two_parts(head.T * gains[2]),
+        head=diagonal(head_back.T),
+        head_back=two_parts(head_back * gains[2]),
         group=diagonal(jnp.ones((bins, bins), F32)),
         centring=jnp.where(first == second, 1.0, 0.0) - 1.0 / channels,
         ones=jnp.ones((channels, channels), F32),
@@ -442,7 +442,7 @@
     lanes = 2 * narrow
     near, far = 4, 8
 
-    made = derive(norm_gain, w_down, w_conv, w_up, w_head, head_bias[None])
+    made = derive(norm_gain, jnp.swapaxes(w_down, 1, 2), w_conv, w_up, w_head.T, head_bias[None])
     gains, bias, centring, ones, group = (made[name] for name in ("gains", "bias", "centring", "ones", "group"))
     downs, downs_back, ups, ups_back = (made[name] for name in ("downs", "downs_back", "ups", "ups_back"))
     convs, convs_back, head, head_back = (made[name] for name in ("convs", "convs_back", "head", "head_back"))
@@ -496,9 +496,7 @@
         )(*inputs)
 
     own_labels = lax.all_to_all(labels, "col", split_axis=1, concat_axis=0, tiled=True)
-    facing_labels = facing_tile(own_labels)
-    features, own_labels, facing_labels = lax.optimization_barrier((features, own_labels, facing_labels))
-    facing_labels = facing_labels.T
+    features, own_labels = lax.optimization_barrier((features, own_labels))
     split = features.reshape(2, half, columns, channels)
     bf_spec = strip_spec(channels)
     near_shapes, near_specs = edges(near)
@@ -514,6 +512,8 @@
         cost(0, 4),
         "entry",
     )
+    own_labels, *sent = lax.optimization_barrier((own_labels, *sent))
+    facing_labels = facing_tile(own_labels)
     halos = exchange(sent)
 
     centre = squeezed_1
@@ -528,6 +528,8 @@
         cost(1, 12),
         "middle",
     )
+    facing_labels, *sent = lax.optimization_barrier((facing_labels, *sent))
+    facing_labels = facing_labels.T
     halos = exchange(sent)
 
     centre = squeezed_2

time: 254 us -> 247 us (0.972)
  blocking collectives: 9.79 us -> 0 us
  waiting for transfers between devices: 37.5 us -> 40.2 us
    all_to_all x1 -> x0, blocking collectives: 9.79 us -> none  [shards(): lax.all_to_all(labels, 'col', split_axis=1, concat_axis=0, tiled=True)]
    all_to_all x0 -> x1, starting transfers between devices: none -> 5.41 us  [shards(): lax.all_to_all(labels, 'col', split_axis=1, concat_axis=0, tiled=True)]
    unnamed x50 -> x48, local copies, waits for them, and re-layouts: 9.32 us -> 6.38 us
    ppermute x7, waiting for transfers between devices: 12.6 us -> 15.3 us  [facing_logits(): move = lambda array, pairs: lax.ppermute(array, ('row', 'col'), pairs)]
    ppermute x1, starting transfers between devices: 4.52 us -> 1.92 us  [facing_tile(): return lax.ppermute(tile, ('row', 'col'), pairs)]
  transfers between devices with their start and end apart: 24 -> 25, of which waited for: 12 -> 13; matrix products, arithmetic and copies ran while one was open for 6% -> 5% of each run, Pallas kernels for 6% -> 14%
where the time goes in v5:
time: 247 us; the launch traced here: 245 us
  Pallas kernels  100 us (40%)
  starting transfers between devices  80.9 us (33%)
  waiting for transfers between devices  40.2 us (16%)
  other arithmetic  15.8 us (6%)
  local copies, waits for them, and re-layouts  7.3 us (3%)
    pallas_call x5, Pallas kernels, call(): pl.pallas_call(functools.partial(over_strips, body, kinds, 0), grid=(half...  78 us
    ppermute x16, starting transfers between devices, shifted(): lax.ppermute(values, axis, [(i, i + move) for i in range(count) if 0 <= i...  55.3 us
    ppermute x16, waiting for transfers between devices, shifted(): lax.ppermute(values, axis, [(i, i + move) for i in range(count) if 0 <= i...  23 us
    pallas_call x3, Pallas kernels, shards(): pl.pallas_call(functools.partial(over_strips, body, kinds, taken), grid=(...  19.6 us
    ppermute x7, starting transfers between devices, facing_logits(): move = lambda array, pairs: lax.ppermute(array, ('row', 'col'), pairs)  18.2 us
    ppermute x7, waiting for transfers between devices, facing_logits(): move = lambda array, pairs: lax.ppermute(array, ('row', 'col'), pairs)  15.3 us
    unnamed x48, local copies, waits for them, and re-layouts  6.38 us
    another operation x1, other arithmetic  5.72 us
  transfers between devices with their start and end apart: 25, of which 13 were waited for; matrix products, arithmetic and copies ran while one was open for 5% of the time, Pallas kernels for 14%

profile of v5, /device:TPU:1, one launch (start us, length us, event | category | flops | bytes accessed | tf_op | source)
XLA Modules:
  0.0 245.2 jit_solution(18057310775360344578)
XLA Ops:
  1.5 5.4 %all-to-all-start = ((s32[32,4,128]{2,0,1:T(8,128)}), s32[32,4,128]{2,0,1:T(8,128)S(1)}, u32[]{:S(2)}, u32[]{:S(2)}) async-start(s32[32,4,128]{2,0,1:T(8,128)} %copy_bitcast_fusion), calls=%async_computation | async-start | bytes 131072 | tf_op jit(solution)/shard_map/all_to_all | solution.py:498
  6.9 2.7 %weights.1 = (f32[1,128]{1,0:T(1,128)}, bf16[128,128]{1,0:T(8,128)(2,1)}, bf16[384,384]{1,0:T(8,128)(2,1)}, bf16[384,384]{1,0:T(8,128)(2,1)}, bf16[384,384]{1,0:...) custom-call(f32[3,128]{1,0:T(4,128)} %refs_0_.1, ...), custom_call_target="tpu_custom_call" | custom-call | tf_op jit(solution)/shard_map/weights/pallas_call | solution.py:424
  9.6 1.9 all-to-all-done
  11.5 8.3 %entry.1 = (bf16[64,128,128]{2,1,0:T(8,128)(2,1)}, bf16[4,64,128]{2,1,0:T(8,128)(2,1)}, bf16[4,64,128]{2,1,0:T(8,128)(2,1)}, bf16[64,8,128]{2,1,0:T(8,128)(2,1)}, bf16[64,8,128]{2,1,0:T(8,128)(2,1)}) custom-call(bf16[2,64,128,128]{3,2,1,0:T(8,128)(2,1)} %bitcast.17, bf16[128,128]{1,0:T(8,128)(2,1)} %get-tuple-element.77.refs_1_.refs_6_.refs_9_, ...), custom_call_target="tpu_custom_call" | custom-call | flops 536870912 | bytes 8388608 | tf_op jit(solution)/shard_map/entry/pallas_call | solution.py:486
  19.8 5.1 %collective-permute-start = (bf16[4,64,128]{2,1,0:T(8,128)(2,1)}, bf16[4,64,128]{2,1,0:T(8,128)(2,1)S(1)}, u32[]{:S(2)}, u32[]{:S(2)}) collective-permute-start(bf16[4,64,128]{2,1,0:T(8,128)(2,1)} %get-tuple-element.87), channel_id=1, source_target_pairs={{0,8},{8,16},{16,24},{1,9},{9,17},{17,25},{2,10},{10,18},{18,26},{... | collective-permute-start | bytes 196616 | tf_op jit(solution)/shard_map/ppermute | solution.py:302
  24.9 1.9 collective-permute-start.1
  26.9 3.8 %collective-permute-done.1.refs_2_ = bf16[4,64,128]{2,1,0:T(8,128)(2,1)S(1)} collective-permute-done((bf16[4,64,128]{2,1,0:T(8,128)(2,1)}, bf16[4,64,128]{2,1,0:T(8,128)(2,1)S(1)}, u32[]{:S(2)}, u32[]{:S(2)}) %collective-permute-start.1) | collective-permute-done | bytes 65568 | tf_op jit(solution)/shard_map/ppermute | solution.py:302
  31.7 1.3 collective-permute-start.3
  33.9 4.0 %collective-permute-start.2 = (bf16[72,8,128]{2,1,0:T(8,128)(2,1)S(1)}, bf16[72,8,128]{2,1,0:T(8,128)(2,1)S(1)}, u32[]{:S(2)}, u32[]{:S(2)}) collective-permute-start(bf16[72,8,128]{2,1,0:T(8,128)(2,1)S(1)} %pad_maximum_fusion.5), channel_id=1, source_target_pairs={{0,2},{2,4},{4,6},{1,3},{3,5},{5,7},{8,10},{10,12},{12,14},{9,11},... | collective-permute-start | bytes 442376 | tf_op jit(solution)/shard_map/ppermute | solution.py:302
  37.9 1.9 collective-permute-start.4
  40.6 17.2 %middle.1 = (f32[2,64,128,128]{3,2,1,0:T(8,128)}, bf16[64,128,128]{2,1,0:T(8,128)(2,1)}, bf16[64,128,128]{2,1,0:T(8,128)(2,1)}, bf16[8,64,128]{2,1,0:T(8,128)(2,...) custom-call(bf16[64,128,128]{2,1,0:T(8,128)(2,1)} %get-tuple-element.81.refs_0_.refs_6_, ...), custom_call_target="tpu_custom_call" | custom-call | flops 1744830464 | bytes 25165824 | tf_op jit(solution)/shard_map/middle/pallas_call | solution.py:486
  57.9 3.3 %collective-permute-start.5 = (bf16[8,64,128]{2,1,0:T(8,128)(2,1)}, bf16[8,64,128]{2,1,0:T(8,128)(2,1)S(1)}, u32[]{:S(2)}, u32[]{:S(2)}) collective-permute-start(bf16[8,64,128]{2,1,0:T(8,128)(2,1)} %get-tuple-element.101), channel_id=1, source_target_pairs={{0,8},{8,16},{16,24},{1,9},{9,17},{17,25},{2,10},{10,18},{18,26},{... | collective-permute-start | bytes 393224 | tf_op jit(solution)/shard_map/ppermute | solution.py:302
  61.2 1.9 collective-permute-start.6
  63.4 4.2 %collective-permute-done.6.refs_2_ = bf16[8,64,128]{2,1,0:T(8,128)(2,1)S(1)} collective-permute-done((bf16[8,64,128]{2,1,0:T(8,128)(2,1)}, bf16[8,64,128]{2,1,0:T(8,128)(2,1)S(1)}, u32[]{:S(2)}, u32[]{:S(2)}) %collective-permute-start.6) | collective-permute-done | bytes 131104 | tf_op jit(solution)/shard_map/ppermute | solution.py:302
  68.6 1.3 collective-permute-start.8
  70.9 5.1 %collective-permute-start.7 = (bf16[80,8,128]{2,1,0:T(8,128)(2,1)S(1)}, bf16[80,8,128]{2,1,0:T(8,128)(2,1)S(1)}, u32[]{:S(2)}, u32[]{:S(2)}) collective-permute-start(bf16[80,8,128]{2,1,0:T(8,128)(2,1)S(1)} %pad_maximum_fusion.1), channel_id=1, source_target_pairs={{0,2},{2,4},{4,6},{1,3},{3,5},{5,7},{8,10},{10,12},{12,14},{9,11},... | collective-permute-start | bytes 491528 | tf_op jit(solution)/shard_map/ppermute | solution.py:302
  76.0 2.2 collective-permute-done.7.refs_3_
  78.9 16.6 %head.1 = (f32[2,64,128,128]{3,2,1,0:T(8,128)}, bf16[64,128,128]{2,1,0:T(8,128)(2,1)}, bf16[64,128,128]{2,1,0:T(8,128)(2,1)}, bf16[2,64,32,128]{3,2,1,0:T(8,128)...) custom-call(bf16[64,128,128]{2,1,0:T(8,128)(2,1)} %get-tuple-element.95.refs_0_.refs_6_, ...), custom_call_target="tpu_custom_call" | custom-call | flops 1744830464 | bytes 29360128 | tf_op jit(solution)/shard_map/head/pallas_call | solution.py:486
  95.5 1.9 collective-permute-start.15
  97.5 1.3 collective-permute-start.12
  98.8 1.3 collective-permute-start.9
  100.3 3.7 %collective-permute-start.14 = (bf16[128,16,128]{2,1,0:T(8,128)(2,1)}, bf16[128,16,128]{2,1,0:T(8,128)(2,1)S(1)}, u32[]{:S(2)}, u32[]{:S(2)}) collective-permute-start(bf16[128,16,128]{2,1,0:T(8,128)(2,1)} %bitcast.30), channel_id=1, source_target_pairs={{0,0},{2,8},{8,2},{10,10},{20,20},{22,28},{28,22},{30,30},{1,1},{3... | collective-permute-start | bytes 1572872 | tf_op jit(solution)/shard_map/ppermute | solution.py:351
  104.0 1.9 collective-permute-start.11
  105.9 9.9 %collective-permute-done.12 = bf16[128,16,128]{2,1,0:T(8,128)(2,1)S(1)} collective-permute-done((bf16[128,16,128]{2,1,0:T(8,128)(2,1)}, bf16[128,16,128]{2,1,0:T(8,128)(2,1)S(1)}, u32[]{:S(2)}, u32[]{:S(2)}) %collective-permute-start.12) | collective-permute-done | bytes 524320 | tf_op jit(solution)/shard_map/ppermute | solution.py:351
  115.8 4.7 %collective-permute-start.13 = (bf16[128,16,128]{2,1,0:T(8,128)(2,1)S(1)}, bf16[128,16,128]{2,1,0:T(8,128)(2,1)S(1)}, u32[]{:S(2)}, u32[]{:S(2)}) collective-permute-start(bf16[128,16,128]{2,1,0:T(8,128)(2,1)S(1)} %collective-permute-done.12), channel_id=1, source_target_pairs={{20,16},{22,24},{28,18},{30,26},{0,4},{2,12},{8,6},{10,14},{21,17}... | collective-permute-start | bytes 1572872 | tf_op jit(solution)/shard_map/ppermute | solution.py:351
  120.5 5.4 %collective-permute-done.9 = bf16[128,16,128]{2,1,0:T(8,128)(2,1)S(1)} collective-permute-done((bf16[128,16,128]{2,1,0:T(8,128)(2,1)}, bf16[128,16,128]{2,1,0:T(8,128)(2,1)S(1)}, u32[]{:S(2)}, u32[]{:S(2)}) %collective-permute-start.9) | collective-permute-done | bytes 524320 | tf_op jit(solution)/shard_map/ppermute | solution.py:351
  125.9 3.5 %collective-permute-start.10 = (bf16[128,16,128]{2,1,0:T(8,128)(2,1)S(1)}, bf16[128,16,128]{2,1,0:T(8,128)(2,1)S(1)}, u32[]{:S(2)}, u32[]{:S(2)}) collective-permute-start(bf16[128,16,128]{2,1,0:T(8,128)(2,1)S(1)} %collective-permute-done.9), channel_id=1, source_target_pairs={{20,16},{22,24},{28,18},{30,26},{0,4},{2,12},{8,6},{10,14},{21,17}... | collective-permute-start | bytes 1572872 | tf_op jit(solution)/shard_map/ppermute | solution.py:351
  129.4 5.7 %multiply_convert_fusion = (bf16[64,128,64]{2,1,0:T(8,128)(2,1)S(1)}, bf16[64,128,64]{2,1,0:T(8,128)(2,1)S(1)}) fusion(s32[64,128]{1,0:T(8,128)S(1)} %copy.27, s32[64,128]{1,0:T(8,128)S(1)} %get-tuple-element.160, s32[64,128]{1,0:T(8,128)S(1)} %copy.26, s32[64,128]{1,0:T(8,128)S(1)} %get-tuple-element.159), kind=kLoop, calls=%fused_computation | loop fusion | flops 7340032 | bytes 2228224 | tf_op jit(solution)/shard_map/convert.1
  135.1 2.6 %pad_maximum_fusion.refs_2_.refs_3_ = bf16[64,128,128]{2,1,0:T(8,128)(2,1)} fusion(bf16[64,128,64]{2,1,0:T(8,128)(2,1)S(1)} %get-tuple-element.167, bf16[64,128,64]{2,1,0:T(8,128)(2,1)S(1)} %get-tuple-element.168), kind=kLoop, calls=%fused_computation.6 | loop fusion | flops 4194304 | bytes 4194304 | tf_op jit(solution)/shard_map/concatenate | solution.py:566
  137.7 1.0 copy-done.2
  138.7 7.7 %loss.3 = (f32[2,64,128,128]{3,2,1,0:T(8,128)}, bf16[64,128,128]{2,1,0:T(8,128)(2,1)}, bf16[64,8,128]{2,1,0:T(8,128)(2,1)}, bf16[64,8,128]{2,1,0:T(8,128)(2,1)}, bf16[8,64,128]{2,1,0:T(8,128)(2,1)}) custom-call(bf16[64,128,128]{2,1,0:T(8,128)(2,1)} %get-tuple-element.111.refs_0_, bf16[128,32,128]{2,1,0:T(8,128)(2,1)} %copy-done.2, ...), custom_call_target="tpu_custom_call" | custom-call | flops 536870912 | bytes 37748736 | tf_op jit(solution)/shard_map/loss/pallas_call | solution.py:606
  147.4 5.8 %loss.4 = (f32[2,64,128,128]{3,2,1,0:T(8,128)}, bf16[64,128,128]{2,1,0:T(8,128)(2,1)}, bf16[64,8,128]{2,1,0:T(8,128)(2,1)}, bf16[64,8,128]{2,1,0:T(8,128)(2,1)}) custom-call(bf16[64,128,128]{2,1,0:T(8,128)(2,1)} %get-tuple-element.111.refs_0_, ...), custom_call_target="tpu_custom_call", output_to_operand_aliasing={{0}: (10, {}), {1}: (11, {}), {2}: (12, {}), {3}: (13, {})} | custom-call | flops 536870912 | bytes 37748736 | tf_op jit(solution)/shard_map/loss/pallas_call | solution.py:606
  154.2 6.0 %loss.5 = (f32[2,64,128,128]{3,2,1,0:T(8,128)}, bf16[64,128,128]{2,1,0:T(8,128)(2,1)}, bf16[64,8,128]{2,1,0:T(8,128)(2,1)}, bf16[64,8,128]{2,1,0:T(8,128)(2,1)}, bf16[8,64,128]{2,1,0:T(8,128)(2,1)}) custom-call(bf16[64,128,128]{2,1,0:T(8,128)(2,1)} %get-tuple-element.111.refs_0_, ...), custom_call_target="tpu_custom_call", output_to_operand_aliasing={{0}: (10, {}), {1}: (11, {}), {2}: (12, {}), {3}: (13, {})} | custom-call | flops 536870912 | bytes 37748736 | tf_op jit(solution)/shard_map/loss/pallas_call | solution.py:606
  160.3 12.8 %collective-permute-start.16 = (bf16[8,64,128]{2,1,0:T(8,128)(2,1)}, bf16[8,64,128]{2,1,0:T(8,128)(2,1)S(1)}, u32[]{:S(2)}, u32[]{:S(2)}) collective-permute-start(bf16[8,64,128]{2,1,0:T(8,128)(2,1)} %get-tuple-element.130), channel_id=1, source_target_pairs={{0,8},{8,16},{16,24},{1,9},{9,17},{17,25},{2,10},{10,18},{18,26},{... | collective-permute-start | bytes 393224 | tf_op jit(solution)/shard_map/ppermute | solution.py:302
  173.1 1.9 collective-permute-start.17
  175.4 4.0 %collective-permute-done.17.refs_2_ = bf16[8,64,128]{2,1,0:T(8,128)(2,1)S(1)} collective-permute-done((bf16[8,64,128]{2,1,0:T(8,128)(2,1)S(1)}, bf16[8,64,128]{2,1,0:T(8,128)(2,1)S(1)}, u32[]{:S(2)}, u32[]{:S(2)}) %collective-permute-start.17) | collective-permute-done | bytes 131104 | tf_op jit(solution)/shard_map/ppermute | solution.py:302
  179.4 1.0 pad_maximum_fusion.4
  180.4 1.3 collective-permute-start.19
  182.6 4.5 %collective-permute-start.18 = (bf16[80,8,128]{2,1,0:T(8,128)(2,1)S(1)}, bf16[80,8,128]{2,1,0:T(8,128)(2,1)S(1)}, u32[]{:S(2)}, u32[]{:S(2)}) collective-permute-start(bf16[80,8,128]{2,1,0:T(8,128)(2,1)S(1)} %pad_maximum_fusion.3), channel_id=1, source_target_pairs={{0,2},{2,4},{4,6},{1,3},{3,5},{5,7},{8,10},{10,12},{12,14},{9,11},... | collective-permute-start | bytes 491528 | tf_op jit(solution)/shard_map/ppermute | solution.py:302
  187.2 2.2 collective-permute-done.18.refs_3_
  190.1 18.6 %back.1 = (f32[2,64,128,128]{3,2,1,0:T(8,128)}, bf16[64,128,128]{2,1,0:T(8,128)(2,1)}, bf16[4,64,128]{2,1,0:T(8,128)(2,1)}, bf16[4,64,128]{2,1,0:T(8,128)(2,1)},...) custom-call(bf16[64,128,128]{2,1,0:T(8,128)(2,1)} %get-tuple-element.129.refs_0_, ...), custom_call_target="tpu_custom_call" | custom-call | flops 1744830464 | bytes 41943040 | tf_op jit(solution)/shard_map/back/pallas_call | solution.py:486
  208.7 2.6 %collective-permute-start.20 = (bf16[4,64,128]{2,1,0:T(8,128)(2,1)}, bf16[4,64,128]{2,1,0:T(8,128)(2,1)S(1)}, u32[]{:S(2)}, u32[]{:S(2)}) collective-permute-start(bf16[4,64,128]{2,1,0:T(8,128)(2,1)} %get-tuple-element.140), channel_id=1, source_target_pairs={{0,8},{8,16},{16,24},{1,9},{9,17},{17,25},{2,10},{10,18},{18,26},{... | collective-permute-start | bytes 196616 | tf_op jit(solution)/shard_map/ppermute | solution.py:302
  211.3 1.9 collective-permute-start.21
  213.3 3.8 %collective-permute-done.21.refs_2_ = bf16[4,64,128]{2,1,0:T(8,128)(2,1)S(1)} collective-permute-done((bf16[4,64,128]{2,1,0:T(8,128)(2,1)}, bf16[4,64,128]{2,1,0:T(8,128)(2,1)S(1)}, u32[]{:S(2)}, u32[]{:S(2)}) %collective-permute-start.21) | collective-permute-done | bytes 65568 | tf_op jit(solution)/shard_map/ppermute | solution.py:302
  218.1 1.3 collective-permute-start.23
  220.3 5.0 %collective-permute-start.22 = (bf16[72,8,128]{2,1,0:T(8,128)(2,1)S(1)}, bf16[72,8,128]{2,1,0:T(8,128)(2,1)S(1)}, u32[]{:S(2)}, u32[]{:S(2)}) collective-permute-start(bf16[72,8,128]{2,1,0:T(8,128)(2,1)S(1)} %pad_maximum_fusion.7), channel_id=1, source_target_pairs={{0,2},{2,4},{4,6},{1,3},{3,5},{5,7},{8,10},{10,12},{12,14},{9,11},... | collective-permute-start | bytes 442376 | tf_op jit(solution)/shard_map/ppermute | solution.py:302
  225.3 1.8 collective-permute-done.22.refs_3_
  227.8 17.2 %final.1 = f32[2,64,128,128]{3,2,1,0:T(8,128)} custom-call(bf16[64,128,128]{2,1,0:T(8,128)(2,1)} %get-tuple-element.139.refs_0_, bf16[4,64,128]{2,1,0:T(8,128)(2,1)} %copy-done.21, bf16[4,64,128]{2,1,0:T(8,128)(2,1)} %copy-done.22, bf16[72,8,128]{2,1,0:T(8,128)(2,1)} %copy-done.18, bf16[72,8,128]{2,1,0:T(8,128)(2,1)} %copy-done.17, ...), custom_call_target="tpu_custom_call" | custom-call | flops 1744830464 | bytes 33554432 | tf_op jit(solution)/shard_map/final/pallas_call | solution.py:486
  (82 shorter events, 13.7 us)
Async XLA Ops:
  0.0 0.8 copy-start
  1.5 10.0 %all-to-all-start = ((s32[32,4,128]{2,0,1:T(8,128)}), s32[32,4,128]{2,0,1:T(8,128)S(1)}, u32[]{:S(2)}, u32[]{:S(2)}) async-start(s32[32,4,128]{2,0,1:T(8,128)} %copy_bitcast_fusion), calls=%async_computation | async-start | bytes 131072 | tf_op jit(solution)/shard_map/all_to_all | solution.py:498
  19.8 7.1 %collective-permute-start = (bf16[4,64,128]{2,1,0:T(8,128)(2,1)}, bf16[4,64,128]{2,1,0:T(8,128)(2,1)S(1)}, u32[]{:S(2)}, u32[]{:S(2)}) collective-permute-start(bf16[4,64,128]{2,1,0:T(8,128)(2,1)} %get-tuple-element.87), channel_id=1, source_target_pairs={{0,8},{8,16},{16,24},{1,9},{9,17},{17,25},{2,10},{10,18},{18,26},{... | collective-permute-start | bytes 196616 | tf_op jit(solution)/shard_map/ppermute | solution.py:302
  24.9 5.8 %collective-permute-start.1 = (bf16[4,64,128]{2,1,0:T(8,128)(2,1)}, bf16[4,64,128]{2,1,0:T(8,128)(2,1)S(1)}, u32[]{:S(2)}, u32[]{:S(2)}) collective-permute-start(bf16[4,64,128]{2,1,0:T(8,128)(2,1)} %get-tuple-element.88), channel_id=1, source_target_pairs={{8,0},{16,8},{24,16},{9,1},{17,9},{25,17},{10,2},{18,10},{26,18},{... | collective-permute-start | bytes 196616 | tf_op jit(solution)/shard_map/ppermute | solution.py:302
  26.9 13.1 %copy-start.19 = (bf16[4,64,128]{2,1,0:T(8,128)(2,1)}, bf16[4,64,128]{2,1,0:T(8,128)(2,1)S(1)}, u32[]{:S(2)}) copy-start(bf16[4,64,128]{2,1,0:T(8,128)(2,1)S(1)} %collective-permute-done.refs_1_) | copy-start | bytes 196612
  30.7 9.3 %copy-start.20 = (bf16[4,64,128]{2,1,0:T(8,128)(2,1)}, bf16[4,64,128]{2,1,0:T(8,128)(2,1)S(1)}, u32[]{:S(2)}) copy-start(bf16[4,64,128]{2,1,0:T(8,128)(2,1)S(1)} %collective-permute-done.1.refs_2_) | copy-start | bytes 196612
  31.7 8.2 %collective-permute-start.3 = (bf16[72,8,128]{2,1,0:T(8,128)(2,1)S(1)}, bf16[72,8,128]{2,1,0:T(8,128)(2,1)S(1)}, u32[]{:S(2)}, u32[]{:S(2)}) collective-permute-start(bf16[72,8,128]{2,1,0:T(8,128)(2,1)S(1)} %pad_maximum_fusion.6), channel_id=1, source_target_pairs={{2,0},{4,2},{6,4},{3,1},{5,3},{7,5},{10,8},{12,10},{14,12},{11,9},... | collective-permute-start | bytes 442376 | tf_op jit(solution)/shard_map/ppermute | solution.py:302
  33.9 6.1 %collective-permute-start.2 = (bf16[72,8,128]{2,1,0:T(8,128)(2,1)S(1)}, bf16[72,8,128]{2,1,0:T(8,128)(2,1)S(1)}, u32[]{:S(2)}, u32[]{:S(2)}) collective-permute-start(bf16[72,8,128]{2,1,0:T(8,128)(2,1)S(1)} %pad_maximum_fusion.5), channel_id=1, source_target_pairs={{0,2},{2,4},{4,6},{1,3},{3,5},{5,7},{8,10},{10,12},{12,14},{9,11},... | collective-permute-start | bytes 442376 | tf_op jit(solution)/shard_map/ppermute | solution.py:302
  37.9 19.9 %collective-permute-start.4 = (s32[128,128]{1,0:T(8,128)S(1)}, s32[128,128]{1,0:T(8,128)S(1)}, u32[]{:S(2)}, u32[]{:S(2)}) collective-permute-start(s32[128,128]{1,0:T(8,128)S(1)} %bitcast.20), channel_id=1, source_target_pairs={{0,0},{2,8},{4,16},{6,24},{8,2},{10,10},{12,18},{14,26},{16,4},{18... | collective-permute-start | bytes 196616 | tf_op jit(solution)/shard_map/ppermute | solution.py:318
  39.9 0.7 copy-start.15
  57.9 5.5 %collective-permute-start.5 = (bf16[8,64,128]{2,1,0:T(8,128)(2,1)}, bf16[8,64,128]{2,1,0:T(8,128)(2,1)S(1)}, u32[]{:S(2)}, u32[]{:S(2)}) collective-permute-start(bf16[8,64,128]{2,1,0:T(8,128)(2,1)} %get-tuple-element.101), channel_id=1, source_target_pairs={{0,8},{8,16},{16,24},{1,9},{9,17},{17,25},{2,10},{10,18},{18,26},{... | collective-permute-start | bytes 393224 | tf_op jit(solution)/shard_map/ppermute | solution.py:302
  61.2 6.5 %collective-permute-start.6 = (bf16[8,64,128]{2,1,0:T(8,128)(2,1)}, bf16[8,64,128]{2,1,0:T(8,128)(2,1)S(1)}, u32[]{:S(2)}, u32[]{:S(2)}) collective-permute-start(bf16[8,64,128]{2,1,0:T(8,128)(2,1)} %get-tuple-element.102), channel_id=1, source_target_pairs={{8,0},{16,8},{24,16},{9,1},{17,9},{25,17},{10,2},{18,10},{26,18},{... | collective-permute-start | bytes 393224 | tf_op jit(solution)/shard_map/ppermute | solution.py:302
  63.4 14.8 %copy-start.9 = (bf16[8,64,128]{2,1,0:T(8,128)(2,1)}, bf16[8,64,128]{2,1,0:T(8,128)(2,1)S(1)}, u32[]{:S(2)}) copy-start(bf16[8,64,128]{2,1,0:T(8,128)(2,1)S(1)} %collective-permute-done.5.refs_1_) | copy-start | bytes 393220
  67.7 10.6 %copy-start.10 = (bf16[8,64,128]{2,1,0:T(8,128)(2,1)}, bf16[8,64,128]{2,1,0:T(8,128)(2,1)S(1)}, u32[]{:S(2)}) copy-start(bf16[8,64,128]{2,1,0:T(8,128)(2,1)S(1)} %collective-permute-done.6.refs_2_) | copy-start | bytes 393220
  68.6 7.4 %collective-permute-start.8 = (bf16[80,8,128]{2,1,0:T(8,128)(2,1)S(1)}, bf16[80,8,128]{2,1,0:T(8,128)(2,1)S(1)}, u32[]{:S(2)}, u32[]{:S(2)}) collective-permute-start(bf16[80,8,128]{2,1,0:T(8,128)(2,1)S(1)} %pad_maximum_fusion.2), channel_id=1, source_target_pairs={{2,0},{4,2},{6,4},{3,1},{5,3},{7,5},{10,8},{12,10},{14,12},{11,9},... | collective-permute-start | bytes 491528 | tf_op jit(solution)/shard_map/ppermute | solution.py:302
  70.9 7.4 %collective-permute-start.7 = (bf16[80,8,128]{2,1,0:T(8,128)(2,1)S(1)}, bf16[80,8,128]{2,1,0:T(8,128)(2,1)S(1)}, u32[]{:S(2)}, u32[]{:S(2)}) collective-permute-start(bf16[80,8,128]{2,1,0:T(8,128)(2,1)S(1)} %pad_maximum_fusion.1), channel_id=1, source_target_pairs={{0,2},{2,4},{4,6},{1,3},{3,5},{5,7},{8,10},{10,12},{12,14},{9,11},... | collective-permute-start | bytes 491528 | tf_op jit(solution)/shard_map/ppermute | solution.py:302
  76.0 2.2 copy-start.13
  78.2 0.7 copy-start.14
  95.5 42.2 %collective-permute-start.15 = (bf16[128,32,128]{2,1,0:T(8,128)(2,1)}, bf16[128,32,128]{2,1,0:T(8,128)(2,1)S(1)}, u32[]{:S(2)}, u32[]{:S(2)}) collective-permute-start(bf16[128,32,128]{2,1,0:T(8,128)(2,1)} %bitcast.26), channel_id=1, source_target_pairs={{0,0},{2,8},{4,16},{6,24},{8,2},{10,10},{12,18},{14,26},{16,4},{18... | collective-permute-start | bytes 3145736 | tf_op jit(solution)/shard_map/ppermute | solution.py:351
  97.5 18.4 %collective-permute-start.12 = (bf16[128,16,128]{2,1,0:T(8,128)(2,1)}, bf16[128,16,128]{2,1,0:T(8,128)(2,1)S(1)}, u32[]{:S(2)}, u32[]{:S(2)}) collective-permute-start(bf16[128,16,128]{2,1,0:T(8,128)(2,1)} %bitcast.29), channel_id=1, source_target_pairs={{4,20},{6,22},{12,28},{14,30},{16,0},{18,2},{24,8},{26,10},{5,21},... | collective-permute-start | bytes 1572872 | tf_op jit(solution)/shard_map/ppermute | solution.py:351
  98.8 27.1 %collective-permute-start.9 = (bf16[128,16,128]{2,1,0:T(8,128)(2,1)}, bf16[128,16,128]{2,1,0:T(8,128)(2,1)S(1)}, u32[]{:S(2)}, u32[]{:S(2)}) collective-permute-start(bf16[128,16,128]{2,1,0:T(8,128)(2,1)} %bitcast.27), channel_id=1, source_target_pairs={{4,20},{6,22},{12,28},{14,30},{16,0},{18,2},{24,8},{26,10},{5,21},... | collective-permute-start | bytes 1572872 | tf_op jit(solution)/shard_map/ppermute | solution.py:351
  100.3 46.1 %collective-permute-start.14 = (bf16[128,16,128]{2,1,0:T(8,128)(2,1)}, bf16[128,16,128]{2,1,0:T(8,128)(2,1)S(1)}, u32[]{:S(2)}, u32[]{:S(2)}) collective-permute-start(bf16[128,16,128]{2,1,0:T(8,128)(2,1)} %bitcast.30), channel_id=1, source_target_pairs={{0,0},{2,8},{8,2},{10,10},{20,20},{22,28},{28,22},{30,30},{1,1},{3... | collective-permute-start | bytes 1572872 | tf_op jit(solution)/shard_map/ppermute | solution.py:351
  104.0 49.3 %collective-permute-start.11 = (bf16[128,16,128]{2,1,0:T(8,128)(2,1)}, bf16[128,16,128]{2,1,0:T(8,128)(2,1)S(1)}, u32[]{:S(2)}, u32[]{:S(2)}) collective-permute-start(bf16[128,16,128]{2,1,0:T(8,128)(2,1)} %bitcast.28), channel_id=1, source_target_pairs={{0,0},{2,8},{8,2},{10,10},{20,20},{22,28},{28,22},{30,30},{1,1},{3... | collective-permute-start | bytes 1572872 | tf_op jit(solution)/shard_map/ppermute | solution.py:351
  115.8 30.6 %collective-permute-start.13 = (bf16[128,16,128]{2,1,0:T(8,128)(2,1)S(1)}, bf16[128,16,128]{2,1,0:T(8,128)(2,1)S(1)}, u32[]{:S(2)}, u32[]{:S(2)}) collective-permute-start(bf16[128,16,128]{2,1,0:T(8,128)(2,1)S(1)} %collective-permute-done.12), channel_id=1, source_target_pairs={{20,16},{22,24},{28,18},{30,26},{0,4},{2,12},{8,6},{10,14},{21,17}... | collective-permute-start | bytes 1572872 | tf_op jit(solution)/shard_map/ppermute | solution.py:351
  125.9 27.4 %collective-permute-start.10 = (bf16[128,16,128]{2,1,0:T(8,128)(2,1)S(1)}, bf16[128,16,128]{2,1,0:T(8,128)(2,1)S(1)}, u32[]{:S(2)}, u32[]{:S(2)}) collective-permute-start(bf16[128,16,128]{2,1,0:T(8,128)(2,1)S(1)} %collective-permute-done.9), channel_id=1, source_target_pairs={{20,16},{22,24},{28,18},{30,26},{0,4},{2,12},{8,6},{10,14},{21,17}... | collective-permute-start | bytes 1572872 | tf_op jit(solution)/shard_map/ppermute | solution.py:351
  137.7 1.0 copy-start.2
  146.4 0.8 copy-start.5
  146.5 1.0 copy-start.6
  153.3 0.8 copy-start.3
  153.3 1.0 copy-start.4
  154.2 18.9 %copy-start.23 = (bf16[8,64,128]{2,1,0:T(8,128)(2,1)S(1)}, bf16[8,64,128]{2,1,0:T(8,128)(2,1)}, u32[]{:S(2)}) copy-start(bf16[8,64,128]{2,1,0:T(8,128)(2,1)} %get-tuple-element.131) | copy-start | bytes 393220
  160.3 15.1 %collective-permute-start.16 = (bf16[8,64,128]{2,1,0:T(8,128)(2,1)}, bf16[8,64,128]{2,1,0:T(8,128)(2,1)S(1)}, u32[]{:S(2)}, u32[]{:S(2)}) collective-permute-start(bf16[8,64,128]{2,1,0:T(8,128)(2,1)} %get-tuple-element.130), channel_id=1, source_target_pairs={{0,8},{8,16},{16,24},{1,9},{9,17},{17,25},{2,10},{10,18},{18,26},{... | collective-permute-start | bytes 393224 | tf_op jit(solution)/shard_map/ppermute | solution.py:302
  173.1 6.3 %collective-permute-start.17 = (bf16[8,64,128]{2,1,0:T(8,128)(2,1)S(1)}, bf16[8,64,128]{2,1,0:T(8,128)(2,1)S(1)}, u32[]{:S(2)}, u32[]{:S(2)}) collective-permute-start(bf16[8,64,128]{2,1,0:T(8,128)(2,1)S(1)} %copy-done.23), channel_id=1, source_target_pairs={{8,0},{16,8},{24,16},{9,1},{17,9},{25,17},{10,2},{18,10},{26,18},{... | collective-permute-start | bytes 393224 | tf_op jit(solution)/shard_map/ppermute | solution.py:302
  175.3 14.0 %copy-start.7 = (bf16[8,64,128]{2,1,0:T(8,128)(2,1)}, bf16[8,64,128]{2,1,0:T(8,128)(2,1)S(1)}, u32[]{:S(2)}) copy-start(bf16[8,64,128]{2,1,0:T(8,128)(2,1)S(1)} %collective-permute-done.16.refs_1_) | copy-start | bytes 393220
  179.4 10.0 %copy-start.8 = (bf16[8,64,128]{2,1,0:T(8,128)(2,1)}, bf16[8,64,128]{2,1,0:T(8,128)(2,1)S(1)}, u32[]{:S(2)}) copy-start(bf16[8,64,128]{2,1,0:T(8,128)(2,1)S(1)} %collective-permute-done.17.refs_2_) | copy-start | bytes 393220
  180.4 6.8 %collective-permute-start.19 = (bf16[80,8,128]{2,1,0:T(8,128)(2,1)S(1)}, bf16[80,8,128]{2,1,0:T(8,128)(2,1)S(1)}, u32[]{:S(2)}, u32[]{:S(2)}) collective-permute-start(bf16[80,8,128]{2,1,0:T(8,128)(2,1)S(1)} %pad_maximum_fusion.4), channel_id=1, source_target_pairs={{2,0},{4,2},{6,4},{3,1},{5,3},{7,5},{10,8},{12,10},{14,12},{11,9},... | collective-permute-start | bytes 491528 | tf_op jit(solution)/shard_map/ppermute | solution.py:302
  182.6 6.8 %collective-permute-start.18 = (bf16[80,8,128]{2,1,0:T(8,128)(2,1)S(1)}, bf16[80,8,128]{2,1,0:T(8,128)(2,1)S(1)}, u32[]{:S(2)}, u32[]{:S(2)}) collective-permute-start(bf16[80,8,128]{2,1,0:T(8,128)(2,1)S(1)} %pad_maximum_fusion.3), channel_id=1, source_target_pairs={{0,2},{2,4},{4,6},{1,3},{3,5},{5,7},{8,10},{10,12},{12,14},{9,11},... | collective-permute-start | bytes 491528 | tf_op jit(solution)/shard_map/ppermute | solution.py:302
  187.2 2.2 copy-start.11
  189.4 0.7 copy-start.12
  208.7 4.6 %collective-permute-start.20 = (bf16[4,64,128]{2,1,0:T(8,128)(2,1)}, bf16[4,64,128]{2,1,0:T(8,128)(2,1)S(1)}, u32[]{:S(2)}, u32[]{:S(2)}) collective-permute-start(bf16[4,64,128]{2,1,0:T(8,128)(2,1)} %get-tuple-element.140), channel_id=1, source_target_pairs={{0,8},{8,16},{16,24},{1,9},{9,17},{17,25},{2,10},{10,18},{18,26},{... | collective-permute-start | bytes 196616 | tf_op jit(solution)/shard_map/ppermute | solution.py:302
  211.3 5.8 %collective-permute-start.21 = (bf16[4,64,128]{2,1,0:T(8,128)(2,1)}, bf16[4,64,128]{2,1,0:T(8,128)(2,1)S(1)}, u32[]{:S(2)}, u32[]{:S(2)}) collective-permute-start(bf16[4,64,128]{2,1,0:T(8,128)(2,1)} %get-tuple-element.141), channel_id=1, source_target_pairs={{8,0},{16,8},{24,16},{9,1},{17,9},{25,17},{10,2},{18,10},{26,18},{... | collective-permute-start | bytes 196616 | tf_op jit(solution)/shard_map/ppermute | solution.py:302
  213.3 13.9 %copy-start.21 = (bf16[4,64,128]{2,1,0:T(8,128)(2,1)}, bf16[4,64,128]{2,1,0:T(8,128)(2,1)S(1)}, u32[]{:S(2)}) copy-start(bf16[4,64,128]{2,1,0:T(8,128)(2,1)S(1)} %collective-permute-done.20.refs_1_) | copy-start | bytes 196612
  217.1 10.0 %copy-start.22 = (bf16[4,64,128]{2,1,0:T(8,128)(2,1)}, bf16[4,64,128]{2,1,0:T(8,128)(2,1)S(1)}, u32[]{:S(2)}) copy-start(bf16[4,64,128]{2,1,0:T(8,128)(2,1)S(1)} %collective-permute-done.21.refs_2_) | copy-start | bytes 196612
  218.1 7.2 %collective-permute-start.23 = (bf16[72,8,128]{2,1,0:T(8,128)(2,1)S(1)}, bf16[72,8,128]{2,1,0:T(8,128)(2,1)S(1)}, u32[]{:S(2)}, u32[]{:S(2)}) collective-permute-start(bf16[72,8,128]{2,1,0:T(8,128)(2,1)S(1)} %pad_maximum_fusion.8), channel_id=1, source_target_pairs={{2,0},{4,2},{6,4},{3,1},{5,3},{7,5},{10,8},{12,10},{14,12},{11,9},... | collective-permute-start | bytes 442376 | tf_op jit(solution)/shard_map/ppermute | solution.py:302
  220.3 6.8 %collective-permute-start.22 = (bf16[72,8,128]{2,1,0:T(8,128)(2,1)S(1)}, bf16[72,8,128]{2,1,0:T(8,128)(2,1)S(1)}, u32[]{:S(2)}, u32[]{:S(2)}) collective-permute-start(bf16[72,8,128]{2,1,0:T(8,128)(2,1)S(1)} %pad_maximum_fusion.7), channel_id=1, source_target_pairs={{0,2},{2,4},{4,6},{1,3},{3,5},{5,7},{8,10},{10,12},{12,14},{9,11},... | collective-permute-start | bytes 442376 | tf_op jit(solution)/shard_map/ppermute | solution.py:302
  225.3 1.9 copy-start.17
  227.1 0.7 copy-start.18
  227.8 17.2 %copy-start.1 = (s32[32,512]{1,0:T(8,128)S(1)}, s32[32,512]{1,0:T(8,128)}, u32[]{:S(2)}) copy-start(s32[32,512]{1,0:T(8,128)} %param.9) | copy-start | bytes 196612
  (1 other events, 0.6 us)
